TPU v7x, 256 devices: a whole 4x4x8 slice. The times are simulated.
256 devices in a mesh: sub: 64 (over z, x, y_hi), mode: 4 (over y_lo, core).
Axes of the slice: x: 4, y: 4 (y_hi: 2, y_lo: 2; y = y_hi * 2 + y_lo), z: 8, core: 2. Of those that a mesh axis runs over, the one named last changes fastest.
Arguments:
- right_side: float32 [2048, 32768], P('mode', 'sub'), may hold values from -6 to 6
- start_field: float32 [2048, 32768], P('mode', 'sub'), may hold values from -6 to 6
- coefficient: float32 [4, 32768], P(None, 'sub'), may hold values from 0.1 to 1
- gblocks: bfloat16 [4, 16, 4, 128, 128], P(None, 'mode'), may hold values from -0.125 to 0.125
- pattern: int32 [4, 16, 4], replicated, may hold values from 0 to 15, as said below
- sub_inverse: bfloat16 [32768, 512], P('sub'), may hold values from -0.125 to 0.125
- coarse_index: int32 [1024], P('sub'), may hold values from 0 to 511, as said below
- coarse_inv: float32 [1024, 16], P('sub'), may hold values from -1.5 to 1.5
- coupling: float32 [1024, 16], P('sub'), may hold values from -1 to 1
Outputs:
- field: float32 [2048, 32768], P('mode', 'sub')
- residual: float32 [2048, 32768], P('mode', 'sub')
Inputs may be any that keep to these rules, and one draw needn't show every extreme that they name: pattern[k, c, 0] = c, and the 4 entries of pattern[k, c] are distinct. `coarse_index`: the 16 entries of one subdomain are distinct.
All inputs are finite; a program needn't handle non-finite values.
Results may differ from a plain program's by a relative error of at most 0.0036.
Values may be sent and summed in bfloat16 or wider, within the bound.
No kernel may reach another device: no remote copies, remote signals or barrier semaphores. Data moves between devices by JAX's collectives and lax.ppermute only.
A program may use at most 64 MiB of HBM per device.

v0:
```python
import jax
import jax.numpy as jnp
from jax import lax
from jax.sharding import Mesh
from jax.sharding import PartitionSpec as P

ITERS = 2
SUB = ("sub_0", "sub_1", "sub_2")


def padded_2(array, sides, width):
    for axis, dim in sides:
        size, length = (lax.axis_size(axis), array.shape[dim])
        up = [(i, (i + 1) % size) for i in range(size - 1)]
        down = [(j, i) for i, j in up]
        last = lax.slice_in_dim(array, length - width, length, axis=dim)
        first = lax.slice_in_dim(array, 0, width, axis=dim)
        before = lax.ppermute(last, axis, up)
        after = lax.ppermute(first, axis, down)
        array = jnp.concatenate([before, array, after], axis=dim)
    return array


def joined_along(tiles, dim):
    tiles = jnp.moveaxis(tiles, 0, dim)
    dims = tiles.shape
    return tiles.reshape(*dims[:dim], dims[dim] * dims[dim + 1], *dims[dim + 2 :])


def copy_for_each(array, axis):
    length = lax.axis_size(axis)
    return lax.all_to_all(
        jnp.broadcast_to(array[None], (length, *array.shape)), axis, 0, 0, tiled=True
    )


def gather_directly(array, axis, dim):
    return joined_along(copy_for_each(array, axis), dim)


def filled_with(array, identity):
    return jax.tree.map(
        lambda part, zero: jnp.zeros_like(part) + jnp.asarray(zero, part.dtype), array, identity
    )


def all_in_one(array, axis):
    leaves = jax.tree.leaves(array)
    order = sorted(range(len(leaves)), key=lambda k: -leaves[k].size)
    width = (1, *leaves[order[0]].shape)[-1]
    lines = [
        jnp.pad(leaves[k].reshape(-1), (0, -leaves[k].size % width)).reshape(-1, width)
        for k in order
    ]
    both, at, found = (lax.all_gather(jnp.concatenate(lines), axis), 0, {})
    for k, line in zip(order, lines):
        piece = both[:, at : at + len(line)].reshape(len(both), -1)
        found[k] = piece[:, : leaves[k].size].reshape(-1, *leaves[k].shape)
        at += len(line)
    numbers = iter(range(len(leaves)))
    return jax.tree.map(lambda _: found[next(numbers)], array)


def prefix_by_axis(array, axes, combine, identity):
    before = start = filled_with(array, identity)
    so_far = array
    for axis in reversed(axes):
        length, mine = (lax.axis_size(axis), lax.axis_index(axis))
        pieces = all_in_one(so_far, axis)
        inside, so_far = (start, start)
        for k in range(length):
            passed = k < mine
            so_far = combine(so_far, jax.tree.map(lambda part: part[k], pieces))
            inside = jax.tree.map(lambda new, old: jnp.where(passed, new, old), so_far, inside)
        before = combine(inside, before)
    return before


def apply_terms(diff_blocks, stored_blocks, row_pattern, coef_rows):
    total = None
    for term in range(stored_blocks.shape[0]):
        rows = jnp.take(diff_blocks, row_pattern[term], axis=0)
        product = jnp.einsum(
            "jtbn,jtbc->jcn", rows, stored_blocks[term], preferred_element_type=jnp.float32
        )
        scaled = coef_rows[term][None, None, :] * product
        total = scaled if total is None else total + scaled
    return total.reshape(-1, total.shape[-1])


def compose(earlier, later):
    highest = lax.Precision.HIGHEST
    return (
        jnp.dot(earlier[0], later[0], precision=highest),
        jnp.dot(earlier[1], later[0], precision=highest) + later[1],
    )


def shards(
    right_side,
    start_field,
    coefficient,
    gblocks,
    pattern,
    sub_inverse,
    coarse_index,
    coarse_inv,
    coupling,
):
    highest = lax.Precision.HIGHEST
    modes_dev, nodes_dev = right_side.shape
    mode_index = lax.axis_index("mode")
    block = gblocks.shape[3]
    blocks_dev = gblocks.shape[1]
    coarse = coarse_index.shape[0]
    node_range = jnp.arange(nodes_dev)
    onehot = (coarse_index[:, None] == node_range[None, :]).astype(jnp.float32)
    own_pattern = lax.dynamic_slice_in_dim(pattern, mode_index * blocks_dev, blocks_dev, 1)
    field = start_field
    residual = right_side
    for turn_index in range(ITERS):
        padded = padded_2(field, ((SUB, 1),), 1)
        diffs = (2.0 * field - padded[:, :-2] - padded[:, 2:]).astype(jnp.bfloat16)
        whole = gather_directly(diffs, "mode", 0)
        operated = apply_terms(
            whole.reshape(whole.shape[0] // block, block, nodes_dev),
            gblocks,
            own_pattern,
            coefficient,
        )
        residual = right_side - operated
        local = jnp.dot(
            residual.astype(jnp.bfloat16), sub_inverse, preferred_element_type=jnp.float32
        )
        restricted = jnp.dot(residual, onehot.T, precision=highest)
        feed = jnp.dot(restricted, coarse_inv, precision=highest)
        identity_map = jnp.eye(coarse, dtype=jnp.float32)
        composed, before = prefix_by_axis(
            (coupling, feed), SUB, compose, (identity_map, jnp.zeros_like(feed))
        )
        error = jnp.dot(before, coupling, precision=highest) + feed
        field = field + local + jnp.dot(error, onehot, precision=highest)
    return (field, residual)


def solution(mesh):
    split = Mesh(
        mesh.devices.reshape(8, 4, 2, mesh.shape["mode"]), ("sub_0", "sub_1", "sub_2", "mode")
    )
    placed = (
        P("mode", SUB),
        P("mode", SUB),
        P(None, SUB),
        P(None, "mode", None, None, None),
        P(),
        P(SUB, None),
        P(SUB),
        P(SUB, None),
        P(SUB, None),
    )
    return jax.shard_map(
        shards,
        mesh=split,
        in_specs=placed,
        out_specs=(P("mode", SUB), P("mode", SUB)),
        check_vma=False,
    )
```

profile of v0, /device:TPU:50, one launch (start us, length us, event | category | flops | bytes accessed | tf_op | source)
XLA Modules:
  0.0 229.0 jit_solution(13768904031755291060)
XLA Ops:
  0.7 1.6 copy.50
  2.3 3.2 %collective-permute-start = (f32[512,1]{0,1:T(1,128)S(1)}, f32[512,1]{0,1:T(1,128)S(1)}, u32[]{:S(2)}, u32[]{:S(2)}) collective-permute-start(f32[512,1]{0,1:T(1,128)S(1)} %get-tuple-element.9), channel_id=1, source_target_pairs={{0,4},{4,8},{8,12},{12,16},{16,20},{20,24},{24,28},{28,32},{32,36}... | collective-permute-start | bytes 6152 | tf_op jit(solution)/shard_map/ppermute | solution.py:18
  5.5 4.2 %collective-permute-start.1 = (f32[512,1]{0,1:T(1,128)S(1)}, f32[512,1]{0,1:T(1,128)S(1)}, u32[]{:S(2)}, u32[]{:S(2)}) collective-permute-start(f32[512,1]{0,1:T(1,128)S(1)} %get-tuple-element.10), channel_id=1, source_target_pairs={{4,0},{8,4},{12,8},{16,12},{20,16},{24,20},{28,24},{32,28},{36,32}... | collective-permute-start | bytes 6152 | tf_op jit(solution)/shard_map/ppermute | solution.py:19
  10.2 3.2 %collective-permute-done.1 = f32[512,1]{0,1:T(1,128)S(1)} collective-permute-done((f32[512,1]{0,1:T(1,128)S(1)}, f32[512,1]{0,1:T(1,128)S(1)}, u32[]{:S(2)}, u32[]{:S(2)}) %collective-permute-start.1) | collective-permute-done | bytes 2080 | tf_op jit(solution)/shard_map/ppermute | solution.py:19
  13.9 1.5 broadcast_in_dim.13
  15.4 3.7 %all-to-all-start = ((bf16[4,512,512]{2,1,0:T(8,128)(2,1)}), bf16[4,512,512]{2,1,0:T(8,128)(2,1)S(1)}, u32[]{:S(2)}, u32[]{:S(2)}) async-start(bf16[4,512,512]{2,1,0:T(8,128)(2,1)} %broadcast_in_dim.13), calls=%async_computation | async-start | bytes 4194304 | tf_op jit(solution)/shard_map/all_to_all | solution.py:32
  19.7 25.1 %all-to-all-done = bf16[4,512,512]{2,1,0:T(8,128)(2,1)S(1)} async-done(((bf16[4,512,512]{2,1,0:T(8,128)(2,1)}), bf16[4,512,512]{2,1,0:T(8,128)(2,1)S(1)}, u32[]{:S(2)}, u32[]{:S(2)}) %all-to-all-start) | async-done | bytes 2097184 | tf_op jit(solution)/shard_map/all_to_all | solution.py:32
  44.7 2.0 gather_fusion
  46.8 2.0 gather_fusion.1
  48.8 2.0 gather_fusion.2
  50.8 2.0 gather_fusion.3
  52.8 2.6 %fusion.87 = f32[4,512,128]{1,2,0:T(8,128)S(1)} fusion(bf16[4,4,128,512]{3,2,1,0:T(8,128)(2,1)} %bitcast.463, pred[4,4]{1,0:T(4,128)(4,1)S(1)} %compare_and_fusion.3, f32[512]{0:T(512)S(1)} %bitcast.470, bf16[4,4,4,128,128]{4,3,2,1,0:T(8,128)(2,1)} %param.14), kind=kOutput, calls=%fused_computation.57 | convolution fusion | flops 269746176 | bytes 3672080 | tf_op jit(solution)/shard_map/jtbn,jtbc->jcn/dot_general | solution.py:83
  56.5 0.9 copy-done.13
  61.9 6.3 %all-gather.6 = f32[2,528,16]{1,2,0:T(8,128)S(1)} all-gather(f32[1,528,16]{1,2,0:T(8,128)S(1)} %fusion.124), channel_id=2, replica_groups=mesh['sub_0'=8,'sub_1'=4,'sub_2'=2,'mode'=4] {'sub_2'}, dimensions={0}, use_global_device_ids=true | all-gather | bytes 101376 | tf_op jit(solution)/shard_map/all_gather | solution.py:55
  68.9 14.6 %all-gather.7 = f32[4,528,16]{1,2,0:T(8,128)S(1)} all-gather(f32[1,528,16]{1,2,0:T(8,128)S(1)} %maximum_bitcast_fusion), channel_id=3, replica_groups=mesh['sub_0'=8,'sub_1'=4,'sub_2'=2,'mode'=4] {'sub_1'}, dimensions={0}, use_global_device_ids=true | all-gather | bytes 168960 | tf_op jit(solution)/shard_map/all_gather | solution.py:55
  85.7 28.1 %all-gather.8 = f32[8,528,16]{1,2,0:T(8,128)S(1)} all-gather(f32[1,528,16]{1,2,0:T(8,128)S(1)} %maximum_bitcast_fusion.1), channel_id=4, replica_groups=mesh['sub_0'=8,'sub_1'=4,'sub_2'=2,'mode'=4] {'sub_0'}, dimensions={0}, use_global_device_ids=true | all-gather | bytes 304128 | tf_op jit(solution)/shard_map/all_gather | solution.py:55
  117.9 1.9 collective-permute-start.2
  119.8 5.4 %collective-permute-start.3 = (f32[512,1]{0,1:T(1,128)S(1)}, f32[512,1]{0,1:T(1,128)S(1)}, u32[]{:S(2)}, u32[]{:S(2)}) collective-permute-start(f32[512,1]{0,1:T(1,128)S(1)} %get-tuple-element.8), channel_id=1, source_target_pairs={{4,0},{8,4},{12,8},{16,12},{20,16},{24,20},{28,24},{32,28},{36,32}... | collective-permute-start | bytes 6152 | tf_op jit(solution)/shard_map/ppermute | solution.py:19
  125.3 2.4 %collective-permute-done.3 = f32[512,1]{0,1:T(1,128)S(1)} collective-permute-done((f32[512,1]{0,1:T(1,128)S(1)}, f32[512,1]{0,1:T(1,128)S(1)}, u32[]{:S(2)}, u32[]{:S(2)}) %collective-permute-start.3) | collective-permute-done | bytes 2080 | tf_op jit(solution)/shard_map/ppermute | solution.py:19
  128.4 28.1 %all_to_all.10 = bf16[4,512,512]{2,1,0:T(8,128)(2,1)S(1)} all-to-all(bf16[4,512,512]{2,1,0:T(8,128)(2,1)S(1)} %broadcast_in_dim.14), channel_id=1, replica_groups=mesh['sub_0'=8,'sub_1'=4,'sub_2'=2,'mode'=4] {'mode'}, dimensions={0} | all-to-all | bytes 4194304 | tf_op jit(solution)/shard_map/all_to_all | solution.py:32
  156.5 2.0 gather_fusion.4
  158.5 2.0 gather_fusion.5
  160.5 2.0 gather_fusion.6
  162.5 2.0 gather_fusion.7
  164.6 2.6 %fusion.66 = f32[4,512,128]{1,2,0:T(8,128)S(1)} fusion(bf16[4,4,128,512]{3,2,1,0:T(8,128)(2,1)} %bitcast.460, pred[4,4]{1,0:T(4,128)(4,1)S(1)} %compare_and_fusion.3, f32[512]{0:T(512)S(1)} %bitcast.471, bf16[4,4,4,128,128]{4,3,2,1,0:T(8,128)(2,1)} %param.14), kind=kOutput, calls=%fused_computation.50 | convolution fusion | flops 269746176 | bytes 3672080 | tf_op jit(solution)/shard_map/jtbn,jtbc->jcn/dot_general | solution.py:83
  168.3 0.9 copy-done.10
  169.9 0.9 copy-done.9
  173.2 6.2 %all-gather.9 = f32[2,528,16]{1,2,0:T(8,128)S(1)} all-gather(f32[1,528,16]{1,2,0:T(8,128)S(1)} %fusion.125), channel_id=5, replica_groups=mesh['sub_0'=8,'sub_1'=4,'sub_2'=2,'mode'=4] {'sub_2'}, dimensions={0}, use_global_device_ids=true | all-gather | bytes 101376 | tf_op jit(solution)/shard_map/all_gather | solution.py:55
  180.1 14.2 %all-gather.10 = f32[4,528,16]{1,2,0:T(8,128)S(1)} all-gather(f32[1,528,16]{1,2,0:T(8,128)S(1)} %maximum_bitcast_fusion.2), channel_id=6, replica_groups=mesh['sub_0'=8,'sub_1'=4,'sub_2'=2,'mode'=4] {'sub_1'}, dimensions={0}, use_global_device_ids=true | all-gather | bytes 168960 | tf_op jit(solution)/shard_map/all_gather | solution.py:55
  194.5 1.5 convolution_add_fusion.1
  198.0 26.2 %all-gather.11 = f32[8,528,16]{1,2,0:T(8,128)S(1)} all-gather(f32[1,528,16]{1,2,0:T(8,128)S(1)} %maximum_bitcast_fusion.3), channel_id=7, replica_groups=mesh['sub_0'=8,'sub_1'=4,'sub_2'=2,'mode'=4] {'sub_0'}, dimensions={0}, use_global_device_ids=true | all-gather | bytes 304128 | tf_op jit(solution)/shard_map/all_gather | solution.py:55
  227.7 1.3 copy.60
  (150 shorter events, 25.2 us)
Async XLA Ops:
  0.6 116.0 %copy-start = (bf16[512,512]{1,0:T(8,128)(2,1)S(1)}, bf16[512,512]{1,0:T(8,128)(2,1)}, u32[]{:S(2)}) copy-start(bf16[512,512]{1,0:T(8,128)(2,1)} %param.16) | copy-start | bytes 1572868
  0.6 9.0 %copy-start.18 = (s32[4,16,4]{1,2,0:T(4,128)S(1)}, s32[4,16,4]{1,2,0:T(4,128)}, u32[]{:S(2)}) copy-start(s32[4,16,4]{1,2,0:T(4,128)} %param.15) | copy-start | bytes 3076
  2.3 13.1 %copy-start.3 = (f32[512,512]{0,1:T(8,128)}, f32[512,512]{0,1:T(8,128)S(1)}, u32[]{:S(2)}) copy-start(f32[512,512]{0,1:T(8,128)S(1)} %copy.50) | copy-start | bytes 3145732
  2.3 7.9 %collective-permute-start = (f32[512,1]{0,1:T(1,128)S(1)}, f32[512,1]{0,1:T(1,128)S(1)}, u32[]{:S(2)}, u32[]{:S(2)}) collective-permute-start(f32[512,1]{0,1:T(1,128)S(1)} %get-tuple-element.9), channel_id=1, source_target_pairs={{0,4},{4,8},{8,12},{12,16},{16,20},{20,24},{24,28},{28,32},{32,36}... | collective-permute-start | bytes 6152 | tf_op jit(solution)/shard_map/ppermute | solution.py:18
  5.5 7.9 %collective-permute-start.1 = (f32[512,1]{0,1:T(1,128)S(1)}, f32[512,1]{0,1:T(1,128)S(1)}, u32[]{:S(2)}, u32[]{:S(2)}) collective-permute-start(f32[512,1]{0,1:T(1,128)S(1)} %get-tuple-element.10), channel_id=1, source_target_pairs={{4,0},{8,4},{12,8},{16,12},{20,16},{24,20},{28,24},{32,28},{36,32}... | collective-permute-start | bytes 6152 | tf_op jit(solution)/shard_map/ppermute | solution.py:19
  15.4 4.1 %copy-start.15 = (f32[16,16]{1,0:T(8,128)S(1)}, f32[16,16]{1,0:T(8,128)}, u32[]{:S(2)}) copy-start(f32[16,16]{1,0:T(8,128)} %param.19) | copy-start | bytes 3076
  15.4 4.3 %copy-start.19 = (f32[4,512]{1,0:T(4,128)S(1)}, f32[4,512]{1,0:T(4,128)}, u32[]{:S(2)}) copy-start(f32[4,512]{1,0:T(4,128)} %param.13) | copy-start | bytes 24580
  15.4 29.4 %all-to-all-start = ((bf16[4,512,512]{2,1,0:T(8,128)(2,1)}), bf16[4,512,512]{2,1,0:T(8,128)(2,1)S(1)}, u32[]{:S(2)}, u32[]{:S(2)}) async-start(bf16[4,512,512]{2,1,0:T(8,128)(2,1)} %broadcast_in_dim.13), calls=%async_computation | async-start | bytes 4194304 | tf_op jit(solution)/shard_map/all_to_all | solution.py:32
  52.8 2.6 %copy-start.14 = (bf16[16,128,512]{2,1,0:T(8,128)(2,1)S(1)}, bf16[16,128,512]{2,1,0:T(8,128)(2,1)}, u32[]{:S(2)}) copy-start(bf16[16,128,512]{2,1,0:T(8,128)(2,1)} %gather_fusion.1) | copy-start | bytes 6291460
  52.8 3.0 %copy-start.20 = (bf16[4,4,4,128,128]{4,3,2,1,0:T(8,128)(2,1)S(1)}, bf16[4,4,4,128,128]{4,3,2,1,0:T(8,128)(2,1)}, u32[]{:S(2)}) copy-start(bf16[4,4,4,128,128]{4,3,2,1,0:T(8,128)(2,1)} %param.14) | copy-start | bytes 6291460
  55.8 1.6 copy-start.13
  57.4 1.6 copy-start.12
  59.0 1.2 copy-start.6
  60.2 0.7 copy-start.17
  60.2 1.3 copy-start.16
  61.9 54.8 %copy-start.4 = (f32[512,512]{0,1:T(8,128)S(1)}, f32[512,512]{0,1:T(8,128)}, u32[]{:S(2)}) copy-start(f32[512,512]{0,1:T(8,128)} %copy-done.3) | copy-start | bytes 3145732
  117.9 9.8 %copy-start.1 = (f32[512,512]{0,1:T(8,128)}, f32[512,512]{0,1:T(8,128)S(1)}, u32[]{:S(2)}) copy-start(f32[512,512]{0,1:T(8,128)S(1)} %convolution_add_fusion.2) | copy-start | bytes 3145732
  117.9 7.4 %collective-permute-start.2 = (f32[512,1]{0,1:T(1,128)S(1)}, f32[512,1]{0,1:T(1,128)S(1)}, u32[]{:S(2)}, u32[]{:S(2)}) collective-permute-start(f32[512,1]{0,1:T(1,128)S(1)} %get-tuple-element.7), channel_id=1, source_target_pairs={{0,4},{4,8},{8,12},{12,16},{16,20},{20,24},{24,28},{28,32},{32,36}... | collective-permute-start | bytes 6152 | tf_op jit(solution)/shard_map/ppermute | solution.py:18
  119.8 7.9 %collective-permute-start.3 = (f32[512,1]{0,1:T(1,128)S(1)}, f32[512,1]{0,1:T(1,128)S(1)}, u32[]{:S(2)}, u32[]{:S(2)}) collective-permute-start(f32[512,1]{0,1:T(1,128)S(1)} %get-tuple-element.8), channel_id=1, source_target_pairs={{4,0},{8,4},{12,8},{16,12},{20,16},{24,20},{28,24},{32,28},{36,32}... | collective-permute-start | bytes 6152 | tf_op jit(solution)/shard_map/ppermute | solution.py:19
  164.6 2.6 %copy-start.11 = (bf16[16,128,512]{2,1,0:T(8,128)(2,1)S(1)}, bf16[16,128,512]{2,1,0:T(8,128)(2,1)}, u32[]{:S(2)}) copy-start(bf16[16,128,512]{2,1,0:T(8,128)(2,1)} %gather_fusion.5) | copy-start | bytes 6291460
  164.6 3.0 %copy-start.21 = (bf16[4,4,4,128,128]{4,3,2,1,0:T(8,128)(2,1)S(1)}, bf16[4,4,4,128,128]{4,3,2,1,0:T(8,128)(2,1)}, u32[]{:S(2)}) copy-start(bf16[4,4,4,128,128]{4,3,2,1,0:T(8,128)(2,1)} %param.14) | copy-start | bytes 6291460
  167.6 1.6 copy-start.10
  169.2 1.6 copy-start.9
  170.8 1.2 copy-start.7
  172.0 22.5 %copy-start.2 = (f32[512,512]{0,1:T(8,128)S(1)}, f32[512,512]{0,1:T(8,128)}, u32[]{:S(2)}) copy-start(f32[512,512]{0,1:T(8,128)} %copy-done.1) | copy-start | bytes 3145732
  172.2 23.8 %copy-start.5 = (f32[512,512]{1,0:T(8,128)}, f32[512,512]{1,0:T(8,128)S(1)}, u32[]{:S(2)}) copy-start(f32[512,512]{1,0:T(8,128)S(1)} %bitcast_subtract_fusion) | copy-start | bytes 3145732
  196.0 31.0 %copy-start.8 = (f32[512,512]{0,1:T(8,128)S(1)}, f32[512,512]{0,1:T(8,128)}, u32[]{:S(2)}) copy-start(f32[512,512]{0,1:T(8,128)} %convolution_add_fusion.1) | copy-start | bytes 3145732
where the time goes:
time: 230 us; the launch traced here: 229 us
  blocking collectives  124 us (54%)
  waiting for transfers between devices  30.7 us (13%)
  local copies, waits for them, and re-layouts  28.1 us (12%)
  matrix products  25 us (11%)
  starting transfers between devices  18.4 us (8%)
    all_gather x6, blocking collectives, all_in_one(): both, at, found = (lax.all_gather(jnp.concatenate(lines), axis), 0, {})  95.5 us
    all_to_all x1, blocking collectives, copy_for_each(): lax.all_to_all(jnp.broadcast_to(array[None], (length, *array.shape)), axi...  28.1 us
    all_to_all x1, waiting for transfers between devices, copy_for_each(): lax.all_to_all(jnp.broadcast_to(array[None], (length, *array.shape)), axi...  25.1 us
    gather x8, local copies, waits for them, and re-layouts, apply_terms(): rows = jnp.take(diff_blocks, row_pattern[term], axis=0)  16.1 us
    ppermute x2, starting transfers between devices, padded_2(): after = lax.ppermute(first, axis, down)  9.6 us
    dot_general x8, matrix products, apply_terms(): jnp.einsum('jtbn,jtbc->jcn', rows, stored_blocks[term], preferred_element...  9.43 us
    unnamed x47, local copies, waits for them, and re-layouts  8.82 us
    dot_general x28, matrix products, compose(): jnp.dot(earlier[1], later[0], precision=highest) + later[1]  7.56 us
  transfers between devices with their start and end apart: 5, of which 3 were waited for; matrix products, arithmetic and copies ran while one was open for 0% of the time, Pallas kernels for 0%

commit v1 on v0

v1 whole, which is shorter than its diff:
```python
import functools

import jax
import jax.numpy as jnp
from jax import lax
from jax.experimental import pallas as pl
from jax.experimental.pallas import tpu as pltpu
from jax.sharding import Mesh
from jax.sharding import PartitionSpec as P

SUB = ("z", "x", "yh")
PLANE = ("x", "yh")
MODE = ("yl", "core")
EDGE = 32
LANES = 128
F32 = jnp.float32
BF16 = jnp.bfloat16
VMEM = pl.BlockSpec(memory_space=pltpu.VMEM)
SMEM = pl.BlockSpec(memory_space=pltpu.SMEM)


def params(mib):
    return pltpu.CompilerParams(vmem_limit_bytes=mib * 2**20)


def shape(dims, dtype=F32):
    return jax.ShapeDtypeStruct(dims, dtype)


def start_kernel(field_ref, middle_ref, top_ref, low_ref, last_ref, first_ref):
    field = jnp.transpose(field_ref[...])
    nodes = field.shape[0]
    diffs = 2.0 * field - pltpu.roll(field, 1, 0) - pltpu.roll(field, nodes - 1, 0)
    middle_ref[...] = diffs[EDGE : nodes - EDGE].astype(BF16)
    top_ref[...] = field[: EDGE + 8]
    low_ref[...] = field[nodes - EDGE - 8 :]
    last_ref[...] = jnp.broadcast_to(field[nodes - 1 :], last_ref.shape)
    first_ref[...] = jnp.broadcast_to(field[:1], first_ref.shape)


def start(field):
    modes, nodes = field.shape
    column = lambda rows: pl.BlockSpec((rows, LANES), lambda j: (0, j))
    return pl.pallas_call(
        start_kernel,
        grid=(modes // LANES,),
        in_specs=[pl.BlockSpec((LANES, nodes), lambda j: (j, 0))],
        out_specs=[column(nodes - 2 * EDGE), column(EDGE + 8), column(EDGE + 8), column(8), column(8)],
        out_shape=[
            shape((nodes - 2 * EDGE, modes), BF16),
            shape((EDGE + 8, modes)),
            shape((EDGE + 8, modes)),
            shape((8, modes)),
            shape((8, modes)),
        ],
        name="start",
    )(field)


def affected(index_ref, nodes):
    found = []
    for c in range(index_ref.shape[0]):
        for off in (-1, 0, 1):
            found.append(jnp.clip(index_ref[c] + off, 0, nodes - 1))
    return found + [0, nodes - 1]


def around(index_ref, nodes):
    found = []
    for c in range(index_ref.shape[0]):
        for off in (-2, -1, 0, 1, 2):
            found.append(jnp.clip(index_ref[c] + off, 0, nodes - 1))
    return found + [0, 1, nodes - 2, nodes - 1]


def padded(count):
    return -(-count // 16) * 16


def at(row):
    return slice(row, row + 1) if isinstance(row, int) else pl.ds(row, 1)


def prepare_kernel(index_ref, right_ref, inverse_ref, field_ref, coef_ref, right_t_ref, inverse_t_ref, field_t_ref, coef_t_ref, right_rows_ref, coef_rows_ref):
    right_t_ref[...] = jnp.transpose(right_ref[...])
    inverse_t_ref[...] = jnp.transpose(inverse_ref[...].astype(F32)).astype(BF16)
    field_t_ref[...] = jnp.transpose(field_ref[...])
    terms, nodes = coef_ref.shape
    found = affected(index_ref, nodes)
    right_rows_ref[...] = jnp.zeros_like(right_rows_ref)
    for j, n in enumerate(found):
        right_rows_ref[j : j + 1] = right_t_ref[at(n), :]

    @pl.when(pl.program_id(0) == 0)
    def _():
        wide = jnp.concatenate([coef_ref[...], jnp.zeros((LANES - terms, nodes), F32)], axis=0)
        coef_t_ref[...] = jnp.transpose(wide)
        coef_rows_ref[...] = jnp.zeros_like(coef_rows_ref)
        for j, n in enumerate(found):
            coef_rows_ref[j : j + 1] = coef_t_ref[at(n), :]


def prepare(index, right_side, sub_inverse, field, coefficient):
    modes, nodes = right_side.shape
    count = padded(3 * index.shape[0] + 2)
    rows = lambda width: pl.BlockSpec((LANES, width), lambda j: (j, 0))
    column = lambda height: pl.BlockSpec((height, LANES), lambda j: (0, j))
    fixed = lambda height: pl.BlockSpec((height, LANES), lambda j: (0, 0))
    return pl.pallas_call(
        prepare_kernel,
        grid=(modes // LANES,),
        in_specs=[
            SMEM,
            rows(nodes),
            rows(nodes),
            rows(nodes),
            pl.BlockSpec(coefficient.shape, lambda j: (0, 0)),
        ],
        out_specs=[column(nodes)] * 3 + [fixed(nodes), column(count), fixed(count)],
        out_shape=[
            shape((nodes, modes)),
            shape((nodes, nodes), BF16),
            shape((nodes, modes)),
            shape((nodes, LANES)),
            shape((count, modes)),
            shape((count, LANES)),
        ],
        name="prepare",
    )(index, right_side, sub_inverse, field, coefficient)


def edge_kernel(top_ref, low_ref, left_ref, right_ref, edge_ref):
    top = top_ref[...]
    before = jnp.concatenate([left_ref[:1], top[: EDGE - 1]], axis=0)
    edge_ref[:EDGE] = (2.0 * top[:EDGE] - before - top[1 : EDGE + 1]).astype(BF16)
    low = low_ref[...]
    after = jnp.concatenate([low[9:], right_ref[:1]], axis=0)
    edge_ref[EDGE:] = (2.0 * low[8:] - low[7:-1] - after).astype(BF16)


def edges(top, low, left, right):
    return pl.pallas_call(
        edge_kernel,
        in_specs=[VMEM] * 4,
        out_specs=VMEM,
        out_shape=shape((2 * EDGE, top.shape[1]), BF16),
        compiler_params=params(16),
        name="edges",
    )(top, low, left, right)


HBM = pl.BlockSpec(memory_space=pltpu.HBM)
ANY = pl.BlockSpec(memory_space=pl.ANY)


def copies(pairs, sems):
    made = [pltpu.make_async_copy(a, b, sems.at[n]) for n, (a, b) in enumerate(pairs)]
    for copy in made:
        copy.start()
    return made


def finished(made):
    for copy in made:
        copy.wait()


def into_blocks(part_refs, blocks_ref):
    each = part_refs[0].shape[-1] // LANES
    return [
        (part.at[:, pl.ds(b * LANES, LANES)], blocks_ref.at[n * each + b])
        for n, part in enumerate(part_refs)
        for b in range(each)
    ]


def operated(blocks_ref, g_ref, pattern_ref, me, coefs, c, relative):
    total = None
    own = g_ref.shape[1]
    for k in range(g_ref.shape[0]):
        rows = []
        for t in range(g_ref.shape[2]):
            row = pattern_ref[k, t, me * own + c]
            if relative:
                owner = lax.div(row, own)
                row = (owner ^ me) * own + lax.rem(row, own)
            rows.append(blocks_ref[row])
        weights = g_ref[k, c].reshape(-1, LANES)
        product = jnp.dot(jnp.concatenate(rows, axis=1), weights, preferred_element_type=F32)
        scaled = coefs[k] * product
        total = scaled if total is None else total + scaled
    return total


def columns_of(coef, count):
    return [coef[:, k : k + 1] for k in range(count)]


def lanes_of(c):
    return pl.ds(pl.multiple_of(c * LANES, LANES), LANES)


def bulk_kernel(skip, me_ref, pattern_ref, a_ref, b_ref, c_ref, d_ref, g_ref, coef_ref, out_ref, blocks_ref, sems):
    made = copies(into_blocks([a_ref, b_ref, c_ref, d_ref], blocks_ref), sems)
    coefs = columns_of(coef_ref[skip : skip + out_ref.shape[0]], g_ref.shape[0])
    finished(made)

    @pl.loop(0, g_ref.shape[1])
    def _(c):
        out_ref[:, lanes_of(c)] = operated(blocks_ref, g_ref, pattern_ref, me_ref[0], coefs, c, True)


def bulk(me, pattern, parts, gblocks, coef, skip):
    rows, modes = parts[0].shape
    return pl.pallas_call(
        functools.partial(bulk_kernel, skip),
        in_specs=[SMEM, SMEM] + [ANY] * 4 + [VMEM] * 2,
        out_specs=VMEM,
        out_shape=shape((rows, modes)),
        scratch_shapes=[
            pltpu.VMEM((4 * modes // LANES, rows, LANES), BF16),
            pltpu.SemaphoreType.DMA((16,)),
        ],
        compiler_params=params(16),
    )(me, pattern, *parts, gblocks, coef)


def two_terms(value):
    high = value.astype(BF16).astype(F32)
    return high, value - high


def feed_of(rows, inverse):
    coarse = inverse.shape[0]
    inverse_t = jnp.transpose(inverse)
    feed = inverse_t[:, :1] * rows[:1]
    for c in range(1, coarse):
        feed = feed + inverse_t[:, c : c + 1] * rows[c : c + 1]
    return feed


def flags(index_ref, node):
    coarse = index_ref.shape[0]
    row = lax.broadcasted_iota(jnp.int32, (coarse, LANES), 0)
    found = jnp.zeros((coarse, LANES), F32)
    for c in range(coarse):
        found = jnp.where((row == c) & (index_ref[c] == node), 1.0, found)
    return found


def folded(row):
    count = row.shape[1] // LANES
    return jnp.concatenate([row[:, b * LANES : (b + 1) * LANES] for b in range(count)], axis=0)


def unfolded(rows):
    return jnp.concatenate([rows[b : b + 1] for b in range(rows.shape[0])], axis=1)


LAST, FIRST, NEXT = 32, 33, 48


def first_kernel(me_ref, pattern_ref, index_ref, a_ref, b_ref, c_ref, d_ref, g_ref, coef_ref, right_ref, mid_ref, sub_ref, field_ref, inverse_ref, coupling_ref, message_ref, base_ref, diffs_ref, around_ref, blocks_ref, res_ref, sub_vmem, base_vmem, diffs_vmem, rows_ref, sems):
    nodes, _ = field_ref.shape
    coarse = inverse_ref.shape[0]
    made = copies(
        into_blocks([a_ref, b_ref, c_ref, d_ref], blocks_ref)
        + [(right_ref, res_ref), (sub_ref, sub_vmem), (field_ref, base_vmem)],
        sems,
    )
    coef = jnp.concatenate([coef_ref[:EDGE], coef_ref[nodes - EDGE :]], axis=0)
    coefs = columns_of(coef, g_ref.shape[0])
    finished(made[:17])
    inner = slice(EDGE, nodes - EDGE)
    res_ref[inner] = res_ref[inner] - mid_ref[...]

    @pl.loop(0, g_ref.shape[1])
    def _(c):
        total = operated(blocks_ref, g_ref, pattern_ref, me_ref[0], coefs, c, True)
        res_ref[:EDGE, lanes_of(c)] = res_ref[:EDGE, lanes_of(c)] - total[:EDGE]
        res_ref[nodes - EDGE :, lanes_of(c)] = res_ref[nodes - EDGE :, lanes_of(c)] - total[EDGE:]

    finished(made[17:])
    for c in range(coarse):
        rows_ref[c : c + 1] = res_ref[pl.ds(index_ref[c], 1), :]
    feed = feed_of(rows_ref[...], inverse_ref[...])
    local = jnp.dot(sub_vmem[...], res_ref[...].astype(BF16), preferred_element_type=F32)
    base = base_vmem[...] + local
    base_vmem[...] = base
    out = [pltpu.make_async_copy(base_vmem, base_ref, sems.at[0])]
    out[0].start()
    diffs = 2.0 * base - pltpu.roll(base, 1, 0) - pltpu.roll(base, nodes - 1, 0)
    diffs_vmem[...] = diffs.astype(BF16)
    out.append(pltpu.make_async_copy(diffs_vmem, diffs_ref, sems.at[1]))
    out[1].start()

    lane = lax.broadcasted_iota(jnp.int32, (coarse, LANES), 1)
    high, low = two_terms(
        jnp.concatenate([jnp.transpose(coupling_ref[...]), jnp.zeros((coarse, LANES - coarse), F32)], axis=1)
    )
    at_last, at_first = flags(index_ref, nodes - 1), flags(index_ref, 0)
    block = high + pltpu.roll(low, coarse, 1)
    block = block + jnp.where(lane == LAST, at_last, 0.0) + jnp.where(lane == FIRST, at_first, 0.0)
    first = base[:1] + jnp.sum(at_first[:, :1] * feed.astype(BF16).astype(F32), axis=0, keepdims=True)
    edge = jnp.concatenate(
        two_terms(folded(base[nodes - 1 :])) + two_terms(folded(first)), axis=0
    )
    sent = jnp.concatenate([feed, block, edge], axis=1).astype(BF16)
    for p in range(message_ref.shape[0]):
        message_ref[p] = sent
    for j, n in enumerate(around(index_ref, nodes)):
        around_ref[j : j + 1] = base_vmem[at(n), :]
    finished(out)


def first_update(me, pattern, index, parts, gblocks, coef, right, mid, sub_t, field, inverse, coupling, plane):
    nodes, modes = right.shape
    coarse = inverse.shape[0]
    return pl.pallas_call(
        first_kernel,
        in_specs=[SMEM] * 3 + [ANY] * 4 + [VMEM] * 2 + [ANY, VMEM] + [ANY] * 2 + [VMEM] * 2,
        out_specs=[VMEM, ANY, ANY, VMEM],
        out_shape=[
            shape((plane, coarse, modes + 2 * LANES), BF16),
            shape((nodes, modes)),
            shape((nodes, modes), BF16),
            shape((padded(5 * coarse + 4), modes)),
        ],
        scratch_shapes=[
            pltpu.VMEM((4 * modes // LANES, 2 * EDGE, LANES), BF16),
            pltpu.VMEM((nodes, modes), F32),
            pltpu.VMEM((nodes, nodes), BF16),
            pltpu.VMEM((nodes, modes), F32),
            pltpu.VMEM((nodes, modes), BF16),
            pltpu.VMEM((coarse, modes), F32),
            pltpu.SemaphoreType.DMA((19,)),
        ],
        compiler_params=params(24),
        name="first_update",
    )(me, pattern, index, *parts, gblocks, coef, right, mid, sub_t, field, inverse, coupling)


def advance(coupling_t, state, push):
    moved = push
    for c in range(state.shape[0]):
        moved = moved + coupling_t[:, c : c + 1] * state[c : c + 1]
    return moved


def step_of(block, coarse, at=0):
    block = block.astype(F32)
    if at:
        block = pltpu.roll(block, LANES - at, 1)
    return block + pltpu.roll(block, LANES - coarse, 1)


def plane_kernel(feeds_ref, out_ref):
    plane, coarse, width = feeds_ref.shape
    modes = width - 2 * LANES
    row = lax.broadcasted_iota(jnp.int32, (coarse, LANES), 0)
    lane = lax.broadcasted_iota(jnp.int32, (coarse, LANES), 1)
    matrix = (row == lane).astype(F32)
    state = jnp.zeros((coarse, modes), F32)
    for p in range(plane):
        step = step_of(feeds_ref[p, :, modes : modes + LANES], coarse)
        state = advance(step, state, feeds_ref[p, :, :modes].astype(F32))
        matrix = advance(step, matrix, jnp.zeros_like(matrix))
    matrix = jnp.where(lane < coarse, matrix, 0.0)
    high, low = two_terms(matrix)
    first = feeds_ref[0, :, modes : modes + LANES].astype(F32)
    final = feeds_ref[plane - 1, :, modes : modes + LANES].astype(F32)
    block = high + pltpu.roll(low, coarse, 1)
    block = block + jnp.where(lane == LAST, final, 0.0) + jnp.where(lane == FIRST, first, 0.0)
    block = block + jnp.where((lane >= NEXT) & (lane < NEXT + 2 * coarse), pltpu.roll(first, NEXT, 1), 0.0)
    edge = jnp.where(
        row < coarse // 2,
        feeds_ref[plane - 1, :, modes + LANES :].astype(F32),
        feeds_ref[0, :, modes + LANES :].astype(F32),
    )
    sent = jnp.concatenate([state, block, edge], axis=1).astype(BF16)
    for z in range(out_ref.shape[0]):
        out_ref[z] = sent


def plane_totals(feeds, planes):
    _, coarse, width = feeds.shape
    return pl.pallas_call(
        plane_kernel,
        in_specs=[VMEM],
        out_specs=VMEM,
        out_shape=shape((planes, coarse, width), BF16),
        compiler_params=params(8),
        name="plane_totals",
    )(feeds)


def second_plane_kernel(feeds_ref, first_ref, out_ref):
    plane, coarse, modes = feeds_ref.shape
    state = feeds_ref[0].astype(F32)
    for p in range(1, plane):
        step = step_of(first_ref[p, :, modes : modes + LANES], coarse)
        state = advance(step, state, feeds_ref[p].astype(F32))
    for z in range(out_ref.shape[0]):
        out_ref[z] = state.astype(BF16)


def second_plane_totals(feeds, first, planes):
    _, coarse, modes = feeds.shape
    return pl.pallas_call(
        second_plane_kernel,
        in_specs=[VMEM] * 2,
        out_specs=VMEM,
        out_shape=shape((planes, coarse, modes), BF16),
        compiler_params=params(8),
        name="second_plane_totals",
    )(feeds, first)


def errors(z_ref, p_ref, feeds_ref, totals_ref, steps_ref, plane_steps_ref):
    coarse = steps_ref.shape[1]
    modes = steps_ref.shape[2] - 2 * LANES

    def across(z, state):
        step = step_of(plane_steps_ref[z, :, modes : modes + LANES], coarse)
        return advance(step, state, totals_ref[z, :, :modes].astype(F32))

    def within(p, state):
        step = step_of(steps_ref[p, :, modes : modes + LANES], coarse)
        return advance(step, state, feeds_ref[p, :, :modes].astype(F32))

    before = lax.fori_loop(0, z_ref[0], across, jnp.zeros((coarse, modes), F32))
    before = lax.fori_loop(0, p_ref[0], within, before)
    return before, within(p_ref[0], before)


def correct_kernel(z_ref, p_ref, index_ref, feeds_ref, totals_ref, around_ref, sent_ref, error_ref, wide_ref, rows_ref):
    nodes, modes = wide_ref.shape[0] - 16, wide_ref.shape[1]
    plane, planes = feeds_ref.shape[0], totals_ref.shape[0]
    z, p = z_ref[0], p_ref[0]
    before, error = errors(z_ref, p_ref, feeds_ref, totals_ref, feeds_ref, totals_ref)
    coarse = error.shape[0]

    block, edge = slice(modes, modes + LANES), slice(modes + LANES, modes + 2 * LANES)
    p_left, z_left = jnp.maximum(p - 1, 0), jnp.maximum(z - 1, 0)
    p_right, z_right = jnp.minimum(p + 1, plane - 1), jnp.minimum(z + 1, planes - 1)
    here = p > 0
    left_block = jnp.where(here, feeds_ref[p_left, :, block].astype(F32), totals_ref[z_left, :, block].astype(F32))
    left_edge = jnp.where(here, feeds_ref[p_left, :, edge].astype(F32), totals_ref[z_left, :, edge].astype(F32))
    left = unfolded(left_edge[:4] + left_edge[4:8])
    left = left + jnp.sum(left_block[:, LAST : LAST + 1] * before, axis=0, keepdims=True)
    left = jnp.where((z > 0) | here, left, 0.0)
    here = p < plane - 1
    near, far = feeds_ref[p_right, :, block], totals_ref[z_right, :, block]
    step = jnp.where(here, step_of(near, coarse), step_of(far, coarse, NEXT))
    flag = jnp.where(here, near.astype(F32), far.astype(F32))
    right_edge = jnp.where(here, feeds_ref[p_right, :, edge].astype(F32), totals_ref[z_right, :, edge].astype(F32))
    moved = advance(step, error, jnp.zeros_like(error))
    right = unfolded(right_edge[8:12] + right_edge[12:])
    right = right + jnp.sum(flag[:, FIRST : FIRST + 1] * moved, axis=0, keepdims=True)
    right = jnp.where((z < planes - 1) | here, right, 0.0)

    error_ref[...] = error
    for j, n in enumerate(around(index_ref, nodes)):
        wide_ref[at(8 + n), :] = around_ref[j : j + 1]
    wide_ref[7:8] = left
    wide_ref[8 + nodes : 9 + nodes] = right
    for c in range(coarse):
        row = pl.ds(8 + index_ref[c], 1)
        wide_ref[row, :] = wide_ref[row, :] + error[c : c + 1]
    found = affected(index_ref, nodes)
    rows_ref[...] = jnp.zeros_like(rows_ref)
    for j, n in enumerate(found):
        rows_ref[j : j + 1] = (
            2.0 * wide_ref[at(8 + n), :] - wide_ref[at(7 + n), :] - wide_ref[at(9 + n), :]
        )
    sent = rows_ref[...].astype(BF16)
    for m in range(sent_ref.shape[0]):
        sent_ref[m] = sent


def correct(z, p, index, feeds, totals, near, nodes, modes_by):
    modes = near.shape[1]
    coarse = index.shape[0]
    rows = padded(3 * coarse + 2)
    return pl.pallas_call(
        correct_kernel,
        in_specs=[SMEM] * 3 + [VMEM] * 3,
        out_specs=[VMEM] * 2,
        out_shape=[shape((modes_by, rows, modes), BF16), shape((coarse, modes))],
        scratch_shapes=[pltpu.VMEM((nodes + 16, modes), F32), pltpu.VMEM((rows, modes), F32)],
        compiler_params=params(16),
        name="correct",
    )(z, p, index, feeds, totals, near)


def redo_kernel(me_ref, pattern_ref, diffs_ref, g_ref, coef_ref, right_ref, inverse_ref, message_ref, res_ref, blocks_ref, rows_ref, sems):
    made = copies(into_blocks([diffs_ref.at[m] for m in range(diffs_ref.shape[0])], blocks_ref), sems)
    coefs = columns_of(coef_ref[...], g_ref.shape[0])
    finished(made)

    @pl.loop(0, g_ref.shape[1])
    def _(c):
        total = operated(blocks_ref, g_ref, pattern_ref, me_ref[0], coefs, c, False)
        res_ref[:, lanes_of(c)] = right_ref[:, lanes_of(c)] - total

    for c in range(inverse_ref.shape[0]):
        rows_ref[c : c + 1] = res_ref[3 * c + 1 : 3 * c + 2]
    feed = feed_of(rows_ref[...], inverse_ref[...]).astype(BF16)
    for p in range(message_ref.shape[0]):
        message_ref[p] = feed


def redo(me, pattern, diffs, gblocks, coef_rows, right_rows, inverse, plane):
    rows, modes = right_rows.shape
    coarse = inverse.shape[0]
    return pl.pallas_call(
        redo_kernel,
        in_specs=[SMEM] * 2 + [ANY] + [VMEM] * 4,
        out_specs=[VMEM] * 2,
        out_shape=[shape((plane, coarse, modes), BF16), shape((rows, modes))],
        scratch_shapes=[
            pltpu.VMEM((4 * modes // LANES, rows, LANES), BF16),
            pltpu.VMEM((coarse, modes), F32),
            pltpu.SemaphoreType.DMA((16,)),
        ],
        compiler_params=params(16),
        name="redo",
    )(me, pattern, diffs, gblocks, coef_rows, right_rows, inverse)


def last_local_kernel(index_ref, op_ref, right_ref, rows_ref, sub_ref, base_ref, error_ref, base_out_ref, res_out_ref, res_ref, field_ref):
    nodes = op_ref.shape[0]
    res_ref[...] = right_ref[...] - op_ref[...]
    for j, n in enumerate(affected(index_ref, nodes)):
        res_ref[at(n), :] = rows_ref[j : j + 1]
    res = res_ref[...]
    field_ref[...] = base_ref[...] + jnp.dot(sub_ref[...], res.astype(BF16), preferred_element_type=F32)
    for c in range(error_ref.shape[0]):
        field_ref[at(index_ref[c]), :] = field_ref[at(index_ref[c]), :] + error_ref[c : c + 1]
    base_out_ref[...] = jnp.transpose(field_ref[...])
    res_out_ref[...] = jnp.transpose(res)


def last_local(index, op, right, rows, sub_t, base, error):
    nodes, modes = op.shape
    column = lambda height: pl.BlockSpec((height, LANES), lambda j: (0, j))
    row = pl.BlockSpec((LANES, nodes), lambda j: (j, 0))
    return pl.pallas_call(
        last_local_kernel,
        grid=(modes // LANES,),
        in_specs=[
            SMEM,
            column(nodes),
            column(nodes),
            column(rows.shape[0]),
            pl.BlockSpec((nodes, nodes), lambda j: (0, 0)),
            column(nodes),
            column(error.shape[0]),
        ],
        out_specs=[row, row],
        out_shape=[shape((modes, nodes)), shape((modes, nodes))],
        scratch_shapes=[pltpu.VMEM((nodes, LANES), F32), pltpu.VMEM((nodes, LANES), F32)],
        name="last_local",
    )(index, op, right, rows, sub_t, base, error)


def last_kernel(z_ref, p_ref, index_ref, feeds_ref, totals_ref, steps_ref, plane_steps_ref, base_ref, out_ref, base_vmem, out_vmem, sems):
    modes, nodes = base_ref.shape
    load = pltpu.make_async_copy(base_ref, base_vmem, sems.at[0])
    load.start()
    _, error = errors(z_ref, p_ref, feeds_ref, totals_ref, steps_ref, plane_steps_ref)
    coarse = error.shape[0]
    high = error.astype(BF16).astype(F32)
    rest = error - high
    mid = rest.astype(BF16).astype(F32)
    terms = jnp.transpose(jnp.concatenate([high, mid, rest - mid], axis=0)).astype(BF16)
    node = lax.broadcasted_iota(jnp.int32, (coarse, nodes), 1)
    row = lax.broadcasted_iota(jnp.int32, (coarse, nodes), 0)
    wanted = jnp.zeros((coarse, nodes), jnp.int32)
    for c in range(coarse):
        wanted = jnp.where(row == c, index_ref[c], wanted)
    onehot = (node == wanted).astype(F32)
    onehot = jnp.concatenate([onehot] * 3, axis=0).astype(BF16)
    load.wait()
    made = []
    for n in range(modes // LANES):
        rows = slice(n * LANES, (n + 1) * LANES)
        out_vmem[rows] = base_vmem[rows] + jnp.dot(terms[rows], onehot, preferred_element_type=F32)
        made.append(pltpu.make_async_copy(out_vmem.at[rows], out_ref.at[rows], sems.at[1 + n]))
        made[-1].start()
    finished(made)


def last(z, p, index, feeds, totals, steps, plane_steps, base):
    modes, _ = base.shape
    return pl.pallas_call(
        last_kernel,
        in_specs=[SMEM] * 3 + [VMEM] * 4 + [ANY],
        out_specs=ANY,
        out_shape=shape(base.shape),
        scratch_shapes=[
            pltpu.VMEM(base.shape, F32),
            pltpu.VMEM(base.shape, F32),
            pltpu.SemaphoreType.DMA((1 + modes // LANES,)),
        ],
        compiler_params=params(16),
        name="last",
    )(z, p, index, feeds, totals, steps, plane_steps, base)


def from_neighbours(last_rows, first_rows):
    size = lax.axis_size(SUB)
    up = [(i, i + 1) for i in range(size - 1)]
    left = lax.ppermute(last_rows, SUB, up)
    right = lax.ppermute(first_rows, SUB, [(j, i) for i, j in up])
    return left, right


def over_modes(own):
    swap = [(0, 1), (1, 0)]
    across = lax.ppermute(own, "yl", swap)
    beside = lax.ppermute(own, "core", swap)
    onward = lax.ppermute(across, "core", swap)
    return own, beside, across, onward


def shards(right_side, start_field, coefficient, gblocks, pattern, sub_inverse, coarse_index, coarse_inv, coupling):
    me = lax.axis_index(MODE).reshape(1)
    z, p = lax.axis_index("z").reshape(1), lax.axis_index(PLANE).reshape(1)
    planes, plane = lax.axis_size("z"), lax.axis_size(PLANE)
    nodes = start_field.shape[1]
    pattern = jnp.swapaxes(pattern, 1, 2)
    diffs, top, low, last_rows, first_rows = start(start_field)
    parts = over_modes(diffs)
    left, right = from_neighbours(last_rows, first_rows)
    edge_rows = edges(top, low, left, right)
    edge_parts = over_modes(edge_rows)
    rhs, sub_t, field, coef, right_rows, coef_rows = prepare(
        coarse_index, right_side, sub_inverse, start_field, coefficient
    )
    mid = bulk(me, pattern, parts, gblocks, coef, EDGE)
    message, base, diffs, near = first_update(
        me, pattern, coarse_index, edge_parts, gblocks, coef, rhs, mid, sub_t, field, coarse_inv, coupling, plane
    )
    feeds = lax.all_to_all(message, PLANE, 0, 0, tiled=True)
    diffs, feeds = lax.optimization_barrier((diffs, feeds))
    parts = over_modes(diffs)
    totals = plane_totals(feeds, planes)
    totals = lax.all_to_all(totals, "z", 0, 0, tiled=True)
    rows, error = correct(z, p, coarse_index, feeds, totals, near, nodes, lax.axis_size(MODE))
    rows = lax.all_to_all(rows, MODE, 0, 0, tiled=True)
    op = bulk(me, pattern, parts, gblocks, coef, 0)
    message, res_rows = redo(me, pattern, rows, gblocks, coef_rows, right_rows, coarse_inv, plane)
    later = lax.all_to_all(message, PLANE, 0, 0, tiled=True)
    base, residual = last_local(coarse_index, op, rhs, res_rows, sub_t, base, error)
    later_totals = second_plane_totals(later, feeds, planes)
    later_totals = lax.all_to_all(later_totals, "z", 0, 0, tiled=True)
    field = last(z, p, coarse_index, later, later_totals, feeds, totals, base)
    return field, residual


def solution(mesh):
    split = Mesh(mesh.devices.reshape(8, 4, 2, 2, 2), SUB + MODE)
    placed = (
        P(MODE, SUB),
        P(MODE, SUB),
        P(None, SUB),
        P(None, MODE, None, None, None),
        P(),
        P(SUB, None),
        P(SUB),
        P(SUB, None),
        P(SUB, None),
    )
    return jax.shard_map(shards, mesh=split, in_specs=placed, out_specs=(P(MODE, SUB), P(MODE, SUB)), check_vma=False)
```

time: 230 us -> 145 us (0.63)
  the two profiles are of different devices: /device:TPU:50 before, /device:TPU:32 now
where the time goes in v1:
time: 145 us; the launch traced here: 144 us
  Pallas kernels  37 us (26%)
  starting transfers between devices  31.7 us (22%)
  waiting for transfers between devices  29.9 us (21%)
  blocking collectives  29.2 us (20%)
  local copies, waits for them, and re-layouts  15.1 us (10%)
    all_to_all x1, blocking collectives, shards(): feeds = lax.all_to_all(message, PLANE, 0, 0, tiled=True)  16.5 us
    unnamed x58, local copies, waits for them, and re-layouts  15.1 us
    ppermute x3, waiting for transfers between devices, over_modes(): across = lax.ppermute(own, 'yl', swap)  14.1 us
    all_to_all x1, blocking collectives, shards(): later = lax.all_to_all(message, PLANE, 0, 0, tiled=True)  12.6 us
    pallas_call x2, Pallas kernels, bulk(): pl.pallas_call(functools.partial(bulk_kernel, skip), in_specs=[SMEM, SMEM...  8.99 us
    all_to_all x1, starting transfers between devices, shards(): totals = lax.all_to_all(totals, 'z', 0, 0, tiled=True)  8.43 us
    all_to_all x1, waiting for transfers between devices, shards(): totals = lax.all_to_all(totals, 'z', 0, 0, tiled=True)  8.32 us
    pallas_call x1, Pallas kernels, last_local(): pl.pallas_call(last_local_kernel, grid=(modes // LANES,), in_specs=[SMEM,...  5.62 us
  transfers between devices with their start and end apart: 14, of which 5 were waited for; matrix products, arithmetic and copies ran while one was open for 0% of the time, Pallas kernels for 18%

profile of v1, /device:TPU:32, one launch (start us, length us, event | category | flops | bytes accessed | tf_op | source)
XLA Modules:
  0.0 143.9 jit_solution(17688951344900844158)
XLA Ops:
  0.6 3.7 %start.1 = (bf16[448,512]{1,0:T(8,128)(2,1)}, f32[40,512]{1,0:T(8,128)}, f32[40,512]{1,0:T(8,128)}, f32[8,512]{1,0:T(8,128)}, f32[8,512]{1,0:T(8,128)}) custom-call(f32[512,512]{1,0:T(8,128)} %field_ref.3), custom_call_target="tpu_custom_call" | custom-call | tf_op jit(solution)/shard_map/start/pallas_call | solution.py:44
  4.4 1.7 %collective-permute-start.6 = (bf16[448,512]{1,0:T(8,128)(2,1)}, bf16[448,512]{1,0:T(8,128)(2,1)S(1)}, u32[]{:S(2)}, u32[]{:S(2)}) collective-permute-start(bf16[448,512]{1,0:T(8,128)(2,1)} %get-tuple-element.31.a_ref), channel_id=1, source_target_pairs={{0,2},{2,0},{1,3},{3,1},{4,6},{6,4},{5,7},{7,5},{8,10},{10,8},{9,1... | collective-permute-start | bytes 1376264 | tf_op jit(solution)/shard_map/ppermute | solution.py:621
  6.0 10.9 %collective-permute-done.6.c_ref = bf16[448,512]{1,0:T(8,128)(2,1)S(1)} collective-permute-done((bf16[448,512]{1,0:T(8,128)(2,1)}, bf16[448,512]{1,0:T(8,128)(2,1)S(1)}, u32[]{:S(2)}, u32[]{:S(2)}) %collective-permute-start.6) | collective-permute-done | bytes 458784 | tf_op jit(solution)/shard_map/ppermute | solution.py:621
  16.9 5.1 %collective-permute-start = (f32[8,512]{1,0:T(8,128)}, f32[8,512]{1,0:T(8,128)S(1)}, u32[]{:S(2)}, u32[]{:S(2)}) collective-permute-start(f32[8,512]{1,0:T(8,128)} %get-tuple-element.27), channel_id=1, source_target_pairs={{0,4},{4,8},{8,12},{12,16},{16,20},{20,24},{24,28},{28,32},{32,36}... | collective-permute-start | bytes 49160 | tf_op jit(solution)/shard_map/ppermute | solution.py:614
  22.0 5.3 %collective-permute-start.1 = (f32[8,512]{1,0:T(8,128)}, f32[8,512]{1,0:T(8,128)S(1)}, u32[]{:S(2)}, u32[]{:S(2)}) collective-permute-start(f32[8,512]{1,0:T(8,128)} %get-tuple-element.28), channel_id=1, source_target_pairs={{4,0},{8,4},{12,8},{16,12},{20,16},{24,20},{28,24},{32,28},{36,32}... | collective-permute-start | bytes 49160 | tf_op jit(solution)/shard_map/ppermute | solution.py:615
  27.3 2.1 %collective-permute-done.1.right_ref = f32[8,512]{1,0:T(8,128)S(1)} collective-permute-done((f32[8,512]{1,0:T(8,128)}, f32[8,512]{1,0:T(8,128)S(1)}, u32[]{:S(2)}, u32[]{:S(2)}) %collective-permute-start.1) | collective-permute-done | bytes 16416 | tf_op jit(solution)/shard_map/ppermute | solution.py:615
  31.2 1.2 collective-permute-start.3
  32.4 3.2 %collective-permute-done.3.c_ref = bf16[64,512]{1,0:T(8,128)(2,1)} collective-permute-done((bf16[64,512]{1,0:T(8,128)(2,1)S(1)}, bf16[64,512]{1,0:T(8,128)(2,1)}, u32[]{:S(2)}, u32[]{:S(2)}) %collective-permute-start.3) | collective-permute-done | bytes 65568 | tf_op jit(solution)/shard_map/ppermute | solution.py:621
  35.6 4.6 %prepare.1 = (f32[512,512]{1,0:T(8,128)}, bf16[512,512]{1,0:T(8,128)(2,1)}, f32[512,512]{1,0:T(8,128)}, f32[512,128]{1,0:T(8,128)}, f32[64,512]{1,0:T(8,128)}, /*index=5*/f32[64,128]{1,0:T(8,128)}) custom-call(s32[16]{0:T(128)} %index_ref.9, f32[512,512]{1,0:T(8,128)} %right_ref.1, bf16[512,512]{1,0:T(8,128)(2,1)} %inverse_ref.3, f32[512,512]{1,0:T(8,128)} %field_ref.3, ...), custom_call_target="tpu_custom_call" | custom-call | tf_op jit(solution)/shard_map/prepare/pallas_call | solution.py:109
  42.8 1.0 copy-done.10
  43.8 1.0 copy-done.12
  44.8 1.0 copy-done.14
  45.9 1.0 copy-done.16
  46.9 3.8 %shard_map.104.mid_ref = f32[448,512]{1,0:T(8,128)S(1)} custom-call(s32[1]{0:T(128)} %bitcast.2.me_ref, s32[4,4,16]{2,1,0:T(4,128)S(1)} %bitcast.4, bf16[448,512]{1,0:T(8,128)(2,1)S(1)} %copy-done.10, bf16[448,512]{1,0:T(8,128)(2,1)S(1)} %copy-done.14, bf16[448,512]{1,0:T(8,128)(2,1)S(1)} %copy-done.12, bf16[448,512]{1,0:T(8,128)(2,1)S(1)} %copy-done.16, ...), custom_call_target="tpu_custom_call" | custom-call | tf_op jit(solution)/shard_map/pallas_call | solution.py:215
  50.8 4.6 %first_update.1 = (bf16[8,16,768]{2,1,0:T(8,128)(2,1)S(1)}, f32[512,512]{1,0:T(8,128)S(1)}, bf16[512,512]{1,0:T(8,128)(2,1)}, f32[96,512]{1,0:T(8,128)S(1)}) custom-call(s32[1]{0:T(128)} %bitcast.2.me_ref, s32[4,4,16]{2,1,0:T(4,128)S(1)} %bitcast.5, s32[16]{0:T(128)S(1)} %copy-done.26, bf16[64,512]{1,0:T(8,128)(2,1)S(1)} %edges.1.a_ref, ...), custom_call_target="tpu_custom_call" | custom-call | tf_op jit(solution)/shard_map/first_update/pallas_call | solution.py:319
  55.4 1.0 copy-done.9
  56.4 16.5 %all_to_all.25.feeds_ref.first_ref.steps_ref = bf16[8,16,768]{2,1,0:T(8,128)(2,1)S(1)} all-to-all(bf16[8,16,768]{2,1,0:T(8,128)(2,1)S(1)} %get-tuple-element.35), channel_id=1, replica_groups=mesh['z'=8,'x'=4,'yh'=2,'yl'=2,'core'=2] {'x','yh'}, dimensions={0} | all-to-all | bytes 393216 | tf_op jit(solution)/shard_map/all_to_all | solution.py:645
  72.9 1.4 collective-permute-start.9
  74.3 1.9 %plane_totals.1 = bf16[8,16,768]{2,1,0:T(8,128)(2,1)} custom-call(bf16[8,16,768]{2,1,0:T(8,128)(2,1)S(1)} %all_to_all.25.feeds_ref.first_ref.steps_ref), custom_call_target="tpu_custom_call" | custom-call | tf_op jit(solution)/shard_map/plane_totals/pallas_call | solution.py:387
  76.2 8.4 %all-to-all-start.1 = ((bf16[8,16,768]{2,1,0:T(8,128)(2,1)}), bf16[8,16,768]{2,1,0:T(8,128)(2,1)S(1)}, u32[]{:S(2)}, u32[]{:S(2)}) async-start(bf16[8,16,768]{2,1,0:T(8,128)(2,1)} %plane_totals.1), calls=%async_computation.1 | async-start | bytes 393216 | tf_op jit(solution)/shard_map/all_to_all | solution.py:649
  84.7 8.3 %all-to-all-done.1.totals_ref.plane_steps_ref = bf16[8,16,768]{2,1,0:T(8,128)(2,1)S(1)} async-done(((bf16[8,16,768]{2,1,0:T(8,128)(2,1)}), bf16[8,16,768]{2,1,0:T(8,128)(2,1)S(1)}, u32[]{:S(2)}, u32[]{:S(2)}) %all-to-all-start.1) | async-done | bytes 196640 | tf_op jit(solution)/shard_map/all_to_all | solution.py:649
  93.0 1.6 %correct.1 = (bf16[4,64,512]{2,1,0:T(8,128)(2,1)S(1)}, f32[16,512]{1,0:T(8,128)S(1)}) custom-call(s32[1]{0:T(128)} %bitcast.z_ref, s32[1]{0:T(128)} %bitcast.1.p_ref, s32[16]{0:T(128)S(1)} %copy-done.26, bf16[8,16,768]{2,1,0:T(8,128)(2,1)S(1)} %all_to_all.25.feeds_ref.first_ref.steps_ref, bf16[8,16,768]{2,1,0:T(8,128)(2,1)S(1)} %all-to-all-done.1.totals_ref.plane_steps_ref, ...), custom_call_target="tpu_custom_call" | custom-call | tf_op jit(solution)/shard_map/correct/pallas_call | solution.py:485
  95.9 3.5 %all-to-all-start.2 = ((bf16[4,64,512]{2,1,0:T(8,128)(2,1)}), bf16[4,64,512]{2,1,0:T(8,128)(2,1)S(1)}, u32[]{:S(2)}, u32[]{:S(2)}) async-start(bf16[4,64,512]{2,1,0:T(8,128)(2,1)} %copy-done.17), calls=%async_computation.2 | async-start | bytes 524288 | tf_op jit(solution)/shard_map/all_to_all | solution.py:651
  100.0 5.4 %all-to-all-done.2.diffs_ref = bf16[4,64,512]{2,1,0:T(8,128)(2,1)S(1)} async-done(((bf16[4,64,512]{2,1,0:T(8,128)(2,1)}), bf16[4,64,512]{2,1,0:T(8,128)(2,1)S(1)}, u32[]{:S(2)}, u32[]{:S(2)}) %all-to-all-start.2) | async-done | bytes 262176 | tf_op jit(solution)/shard_map/all_to_all | solution.py:651
  107.1 2.0 %redo.1 = (bf16[8,16,512]{2,1,0:T(8,128)(2,1)S(1)}, f32[64,512]{1,0:T(8,128)S(1)}) custom-call(s32[1]{0:T(128)} %bitcast.2.me_ref, s32[4,4,16]{2,1,0:T(4,128)S(1)} %bitcast.6, bf16[4,64,512]{2,1,0:T(8,128)(2,1)S(1)} %all-to-all-done.2.diffs_ref, bf16[4,4,4,128,128]{4,3,2,1,0:T(8,128)(2,1)S(1)} %copy-done, f32[64,128]{1,0:T(8,128)S(1)} %copy-done.23, ...), custom_call_target="tpu_custom_call" | custom-call | tf_op jit(solution)/shard_map/redo/pallas_call | solution.py:516
  109.7 12.6 %all_to_all.26.feeds_ref = bf16[8,16,512]{2,1,0:T(8,128)(2,1)S(1)} all-to-all(bf16[8,16,512]{2,1,0:T(8,128)(2,1)S(1)} %get-tuple-element.41), channel_id=1, replica_groups=mesh['z'=8,'x'=4,'yh'=2,'yl'=2,'core'=2] {'x','yh'}, dimensions={0} | all-to-all | bytes 262144 | tf_op jit(solution)/shard_map/all_to_all | solution.py:654
  122.4 1.6 %second_plane_totals.1 = bf16[8,16,512]{2,1,0:T(8,128)(2,1)} custom-call(bf16[8,16,512]{2,1,0:T(8,128)(2,1)S(1)} %all_to_all.26.feeds_ref, bf16[8,16,768]{2,1,0:T(8,128)(2,1)S(1)} %all_to_all.25.feeds_ref.first_ref.steps_ref), custom_call_target="tpu_custom_call" | custom-call | tf_op jit(solution)/shard_map/second_plane_totals/pallas_call | solution.py:409
  124.0 4.5 %all-to-all-start.4 = ((bf16[8,16,512]{2,1,0:T(8,128)(2,1)}), bf16[8,16,512]{2,1,0:T(8,128)(2,1)S(1)}, u32[]{:S(2)}, u32[]{:S(2)}) async-start(bf16[8,16,512]{2,1,0:T(8,128)(2,1)} %second_plane_totals.1), calls=%async_computation.4 | async-start | bytes 262144 | tf_op jit(solution)/shard_map/all_to_all | solution.py:657
  128.6 5.2 %shard_map.105.op_ref = f32[512,512]{1,0:T(8,128)S(1)} custom-call(s32[1]{0:T(128)} %bitcast.2.me_ref, s32[4,4,16]{2,1,0:T(4,128)S(1)} %bitcast.7, bf16[512,512]{1,0:T(8,128)(2,1)} %get-tuple-element.42.a_ref, bf16[512,512]{1,0:T(8,128)(2,1)} %collective-permute-done.8.b_ref, bf16[512,512]{1,0:T(8,128)(2,1)S(1)} %collective-permute-done.9.c_ref, ...), custom_call_target="tpu_custom_call" | custom-call | tf_op jit(solution)/shard_map/pallas_call | solution.py:215
  134.7 5.6 %last_local.1 = (f32[512,512]{1,0:T(8,128)}, f32[512,512]{1,0:T(8,128)}) custom-call(s32[16]{0:T(128)} %index_ref.9, f32[512,512]{1,0:T(8,128)} %copy-done.2, f32[512,512]{1,0:T(8,128)} %get-tuple-element.30.right_ref, f32[64,512]{1,0:T(8,128)} %copy-done.20, bf16[512,512]{1,0:T(8,128)(2,1)} %get-tuple-element.32.sub_ref, f32[512,512]{1,0:T(8,128)} %copy-done.9, ...), custom_call_target="tpu_custom_call" | custom-call | tf_op jit(solution)/shard_map/last_local/pallas_call | solution.py:548
  140.4 1.2 copy-done.8
  141.6 2.3 %last.1 = f32[512,512]{1,0:T(8,128)} custom-call(s32[1]{0:T(128)} %bitcast.z_ref, s32[1]{0:T(128)} %bitcast.1.p_ref, s32[16]{0:T(128)S(1)} %copy-done.27, bf16[8,16,512]{2,1,0:T(8,128)(2,1)S(1)} %all_to_all.26.feeds_ref, bf16[8,16,512]{2,1,0:T(8,128)(2,1)S(1)} %all-to-all-done.4.totals_ref, bf16[8,16,768]{2,1,0:T(8,128)(2,1)S(1)} %all_to_all.25.feeds_ref.first_ref.steps_ref, ...), custom_call_target="tpu_custom_call" | custom-call | tf_op jit(solution)/shard_map/last/pallas_call | solution.py:596
  (68 shorter events, 9.5 us)
Async XLA Ops:
  0.6 41.2 %copy-start.18 = (s32[4,16,4]{1,2,0:T(4,128)S(1)}, s32[4,16,4]{1,2,0:T(4,128)}, u32[]{:S(2)}) copy-start(s32[4,16,4]{1,2,0:T(4,128)} %param.13) | copy-start | bytes 3076
  0.6 41.2 %copy-start = (bf16[4,4,4,128,128]{4,3,2,1,0:T(8,128)(2,1)S(1)}, bf16[4,4,4,128,128]{4,3,2,1,0:T(8,128)(2,1)}, u32[]{:S(2)}) copy-start(bf16[4,4,4,128,128]{4,3,2,1,0:T(8,128)(2,1)} %g_ref.7) | copy-start | bytes 6291460
  4.4 12.6 %collective-permute-start.6 = (bf16[448,512]{1,0:T(8,128)(2,1)}, bf16[448,512]{1,0:T(8,128)(2,1)S(1)}, u32[]{:S(2)}, u32[]{:S(2)}) collective-permute-start(bf16[448,512]{1,0:T(8,128)(2,1)} %get-tuple-element.31.a_ref), channel_id=1, source_target_pairs={{0,2},{2,0},{1,3},{3,1},{4,6},{6,4},{5,7},{7,5},{8,10},{10,8},{9,1... | collective-permute-start | bytes 1376264 | tf_op jit(solution)/shard_map/ppermute | solution.py:621
  6.0 34.3 %collective-permute-start.5 = (bf16[448,512]{1,0:T(8,128)(2,1)}, bf16[448,512]{1,0:T(8,128)(2,1)S(1)}, u32[]{:S(2)}, u32[]{:S(2)}) collective-permute-start(bf16[448,512]{1,0:T(8,128)(2,1)} %get-tuple-element.31.a_ref), channel_id=1, source_target_pairs={{0,1},{1,0},{2,3},{3,2},{4,5},{5,4},{6,7},{7,6},{8,9},{9,8},{10,11... | collective-permute-start | bytes 1376264 | tf_op jit(solution)/shard_map/ppermute | solution.py:622
  16.9 24.9 %copy-start.11 = (bf16[448,512]{1,0:T(8,128)(2,1)}, bf16[448,512]{1,0:T(8,128)(2,1)S(1)}, u32[]{:S(2)}) copy-start(bf16[448,512]{1,0:T(8,128)(2,1)S(1)} %collective-permute-done.6.c_ref) | copy-start | bytes 1376260
  16.9 24.1 %collective-permute-start.7 = (bf16[448,512]{1,0:T(8,128)(2,1)S(1)}, bf16[448,512]{1,0:T(8,128)(2,1)S(1)}, u32[]{:S(2)}, u32[]{:S(2)}) collective-permute-start(bf16[448,512]{1,0:T(8,128)(2,1)S(1)} %collective-permute-done.6.c_ref), channel_id=1, source_target_pairs={{0,1},{1,0},{2,3},{3,2},{4,5},{5,4},{6,7},{7,6},{8,9},{9,8},{10,11... | collective-permute-start | bytes 1376264 | tf_op jit(solution)/shard_map/ppermute | solution.py:623
  16.9 10.4 %collective-permute-start = (f32[8,512]{1,0:T(8,128)}, f32[8,512]{1,0:T(8,128)S(1)}, u32[]{:S(2)}, u32[]{:S(2)}) collective-permute-start(f32[8,512]{1,0:T(8,128)} %get-tuple-element.27), channel_id=1, source_target_pairs={{0,4},{4,8},{8,12},{12,16},{16,20},{20,24},{24,28},{28,32},{32,36}... | collective-permute-start | bytes 49160 | tf_op jit(solution)/shard_map/ppermute | solution.py:614
  22.0 7.3 %collective-permute-start.1 = (f32[8,512]{1,0:T(8,128)}, f32[8,512]{1,0:T(8,128)S(1)}, u32[]{:S(2)}, u32[]{:S(2)}) collective-permute-start(f32[8,512]{1,0:T(8,128)} %get-tuple-element.28), channel_id=1, source_target_pairs={{4,0},{8,4},{12,8},{16,12},{20,16},{24,20},{28,24},{32,28},{36,32}... | collective-permute-start | bytes 49160 | tf_op jit(solution)/shard_map/ppermute | solution.py:615
  31.2 4.5 %collective-permute-start.3 = (bf16[64,512]{1,0:T(8,128)(2,1)S(1)}, bf16[64,512]{1,0:T(8,128)(2,1)}, u32[]{:S(2)}, u32[]{:S(2)}) collective-permute-start(bf16[64,512]{1,0:T(8,128)(2,1)S(1)} %edges.1.a_ref), channel_id=1, source_target_pairs={{0,2},{2,0},{1,3},{3,1},{4,6},{6,4},{5,7},{7,5},{8,10},{10,8},{9,1... | collective-permute-start | bytes 196616 | tf_op jit(solution)/shard_map/ppermute | solution.py:621
  32.4 18.3 %collective-permute-start.2 = (bf16[64,512]{1,0:T(8,128)(2,1)S(1)}, bf16[64,512]{1,0:T(8,128)(2,1)}, u32[]{:S(2)}, u32[]{:S(2)}) collective-permute-start(bf16[64,512]{1,0:T(8,128)(2,1)S(1)} %edges.1.a_ref), channel_id=1, source_target_pairs={{0,1},{1,0},{2,3},{3,2},{4,5},{5,4},{6,7},{7,6},{8,9},{9,8},{10,11... | collective-permute-start | bytes 196616 | tf_op jit(solution)/shard_map/ppermute | solution.py:622
  35.6 15.1 %collective-permute-start.4 = (bf16[64,512]{1,0:T(8,128)(2,1)}, bf16[64,512]{1,0:T(8,128)(2,1)}, u32[]{:S(2)}, u32[]{:S(2)}) collective-permute-start(bf16[64,512]{1,0:T(8,128)(2,1)} %collective-permute-done.3.c_ref), channel_id=1, source_target_pairs={{0,1},{1,0},{2,3},{3,2},{4,5},{5,4},{6,7},{7,6},{8,9},{9,8},{10,11... | collective-permute-start | bytes 196616 | tf_op jit(solution)/shard_map/ppermute | solution.py:623
  42.8 1.0 copy-start.10
  43.8 1.0 copy-start.12
  44.8 1.0 copy-start.14
  45.9 1.0 copy-start.16
  46.9 3.9 %copy-start.1 = (f32[512,512]{1,0:T(8,128)S(1)}, f32[512,512]{1,0:T(8,128)}, u32[]{:S(2)}) copy-start(f32[512,512]{1,0:T(8,128)} %get-tuple-element.30.right_ref) | copy-start | bytes 3145732
  46.9 3.9 %copy-start.4 = (f32[512,128]{1,0:T(8,128)S(1)}, f32[512,128]{1,0:T(8,128)}, u32[]{:S(2)}) copy-start(f32[512,128]{1,0:T(8,128)} %get-tuple-element.29.coef_ref) | copy-start | bytes 786436
  46.9 3.9 %copy-start.6 = (bf16[512,512]{1,0:T(8,128)(2,1)S(1)}, bf16[512,512]{1,0:T(8,128)(2,1)}, u32[]{:S(2)}) copy-start(bf16[512,512]{1,0:T(8,128)(2,1)} %get-tuple-element.32.sub_ref) | copy-start | bytes 1572868
  46.9 3.9 %copy-start.7 = (f32[512,512]{1,0:T(8,128)S(1)}, f32[512,512]{1,0:T(8,128)}, u32[]{:S(2)}) copy-start(f32[512,512]{1,0:T(8,128)} %get-tuple-element.33.field_ref) | copy-start | bytes 3145732
  46.9 3.9 %copy-start.25 = (f32[16,16]{1,0:T(8,128)S(1)}, f32[16,16]{1,0:T(8,128)}, u32[]{:S(2)}) copy-start(f32[16,16]{1,0:T(8,128)} %inverse_ref.5) | copy-start | bytes 3076
  46.9 3.9 %copy-start.26 = (s32[16]{0:T(128)S(1)}, s32[16]{0:T(128)}, u32[]{:S(2)}) copy-start(s32[16]{0:T(128)} %index_ref.9) | copy-start | bytes 196
  46.9 3.9 %copy-start.28 = (f32[16,16]{1,0:T(8,128)S(1)}, f32[16,16]{1,0:T(8,128)}, u32[]{:S(2)}) copy-start(f32[16,16]{1,0:T(8,128)} %coupling_ref.1) | copy-start | bytes 3076
  55.4 1.0 copy-start.9
  72.9 27.0 %collective-permute-start.9 = (bf16[512,512]{1,0:T(8,128)(2,1)}, bf16[512,512]{1,0:T(8,128)(2,1)S(1)}, u32[]{:S(2)}, u32[]{:S(2)}) collective-permute-start(bf16[512,512]{1,0:T(8,128)(2,1)} %get-tuple-element.42.a_ref), channel_id=1, source_target_pairs={{0,2},{2,0},{1,3},{3,1},{4,6},{6,4},{5,7},{7,5},{8,10},{10,8},{9,1... | collective-permute-start | bytes 1572872 | tf_op jit(solution)/shard_map/ppermute | solution.py:621
  76.2 16.8 %all-to-all-start.1 = ((bf16[8,16,768]{2,1,0:T(8,128)(2,1)}), bf16[8,16,768]{2,1,0:T(8,128)(2,1)S(1)}, u32[]{:S(2)}, u32[]{:S(2)}) async-start(bf16[8,16,768]{2,1,0:T(8,128)(2,1)} %plane_totals.1), calls=%async_computation.1 | async-start | bytes 393216 | tf_op jit(solution)/shard_map/all_to_all | solution.py:649
  95.9 32.7 %copy-start.5 = (f32[512,128]{1,0:T(8,128)S(1)}, f32[512,128]{1,0:T(8,128)}, u32[]{:S(2)}) copy-start(f32[512,128]{1,0:T(8,128)} %get-tuple-element.29.coef_ref) | copy-start | bytes 786436
  95.9 9.5 %all-to-all-start.2 = ((bf16[4,64,512]{2,1,0:T(8,128)(2,1)}), bf16[4,64,512]{2,1,0:T(8,128)(2,1)S(1)}, u32[]{:S(2)}, u32[]{:S(2)}) async-start(bf16[4,64,512]{2,1,0:T(8,128)(2,1)} %copy-done.17), calls=%async_computation.2 | async-start | bytes 524288 | tf_op jit(solution)/shard_map/all_to_all | solution.py:651
  99.4 29.1 %collective-permute-start.8 = (bf16[512,512]{1,0:T(8,128)(2,1)}, bf16[512,512]{1,0:T(8,128)(2,1)}, u32[]{:S(2)}, u32[]{:S(2)}) collective-permute-start(bf16[512,512]{1,0:T(8,128)(2,1)} %get-tuple-element.42.a_ref), channel_id=1, source_target_pairs={{0,1},{1,0},{2,3},{3,2},{4,5},{5,4},{6,7},{7,6},{8,9},{9,8},{10,11... | collective-permute-start | bytes 1572872 | tf_op jit(solution)/shard_map/ppermute | solution.py:622
  99.9 28.6 %collective-permute-start.10 = (bf16[512,512]{1,0:T(8,128)(2,1)S(1)}, bf16[512,512]{1,0:T(8,128)(2,1)}, u32[]{:S(2)}, u32[]{:S(2)}) collective-permute-start(bf16[512,512]{1,0:T(8,128)(2,1)S(1)} %collective-permute-done.9.c_ref), channel_id=1, source_target_pairs={{0,1},{1,0},{2,3},{3,2},{4,5},{5,4},{6,7},{7,6},{8,9},{9,8},{10,11... | collective-permute-start | bytes 1572872 | tf_op jit(solution)/shard_map/ppermute | solution.py:623
  124.0 16.4 %all-to-all-start.4 = ((bf16[8,16,512]{2,1,0:T(8,128)(2,1)}), bf16[8,16,512]{2,1,0:T(8,128)(2,1)S(1)}, u32[]{:S(2)}, u32[]{:S(2)}) async-start(bf16[8,16,512]{2,1,0:T(8,128)(2,1)} %second_plane_totals.1), calls=%async_computation.4 | async-start | bytes 262144 | tf_op jit(solution)/shard_map/all_to_all | solution.py:657
  134.7 5.6 %copy-start.27 = (s32[16]{0:T(128)S(1)}, s32[16]{0:T(128)}, u32[]{:S(2)}) copy-start(s32[16]{0:T(128)} %index_ref.9) | copy-start | bytes 196
  140.4 1.2 copy-start.8
  (11 other events, 8.8 us)

commit v2 on v1

--- a/solution.py
+++ b/solution.py
@@ -1,5 +1,3 @@
-import functools
-
 import jax
 import jax.numpy as jnp
 from jax import lax
@@ -11,7 +9,7 @@
 SUB = ("z", "x", "yh")
 PLANE = ("x", "yh")
 MODE = ("yl", "core")
-EDGE = 32
+EDGE = 16
 LANES = 128
 F32 = jnp.float32
 BF16 = jnp.bfloat16
@@ -19,8 +17,8 @@
 SMEM = pl.BlockSpec(memory_space=pltpu.SMEM)
 
 
-def params(mib):
-    return pltpu.CompilerParams(vmem_limit_bytes=mib * 2**20)
+def params(kib=63600):
+    return pltpu.CompilerParams(vmem_limit_bytes=kib * 1024)
 
 
 def shape(dims, dtype=F32):
@@ -144,7 +142,7 @@
         in_specs=[VMEM] * 4,
         out_specs=VMEM,
         out_shape=shape((2 * EDGE, top.shape[1]), BF16),
-        compiler_params=params(16),
+        compiler_params=params(16384),
         name="edges",
     )(top, low, left, right)
 
@@ -165,25 +163,24 @@
         copy.wait()
 
 
-def into_blocks(part_refs, blocks_ref):
+def into_blocks(part_refs, blocks_ref, rows=slice(None)):
     each = part_refs[0].shape[-1] // LANES
     return [
-        (part.at[:, pl.ds(b * LANES, LANES)], blocks_ref.at[n * each + b])
+        (part.at[:, pl.ds(b * LANES, LANES)], blocks_ref.at[n * each + b, rows])
         for n, part in enumerate(part_refs)
         for b in range(each)
     ]
 
 
-def operated(blocks_ref, g_ref, pattern_ref, me, coefs, c, relative):
+def operated(blocks_ref, g_ref, pattern_ref, me, first, coefs, c):
     total = None
-    own = g_ref.shape[1]
+    own = pattern_ref.shape[2] // 4
     for k in range(g_ref.shape[0]):
         rows = []
         for t in range(g_ref.shape[2]):
-            row = pattern_ref[k, t, me * own + c]
-            if relative:
-                owner = lax.div(row, own)
-                row = (owner ^ me) * own + lax.rem(row, own)
+            row = pattern_ref[k, t, me * own + first + c]
+            owner = lax.div(row, own)
+            row = (owner ^ me) * own + lax.rem(row, own)
             rows.append(blocks_ref[row])
         weights = g_ref[k, c].reshape(-1, LANES)
         product = jnp.dot(jnp.concatenate(rows, axis=1), weights, preferred_element_type=F32)
@@ -192,6 +189,17 @@
     return total
 
 
+def weights_into(g_ref, g_vmem, sems, first):
+    return [
+        pltpu.make_async_copy(g_ref.at[:, c], g_vmem.at[:, c], sems.at[first + c])
+        for c in range(g_ref.shape[1])
+    ]
+
+
+def wait_weights(g_ref, g_vmem, sems, first, c):
+    pltpu.make_async_copy(g_ref.at[:, c], g_vmem.at[:, c], sems.at[first + c]).wait()
+
+
 def columns_of(coef, count):
     return [coef[:, k : k + 1] for k in range(count)]
 
@@ -200,29 +208,59 @@
     return pl.ds(pl.multiple_of(c * LANES, LANES), LANES)
 
 
-def bulk_kernel(skip, me_ref, pattern_ref, a_ref, b_ref, c_ref, d_ref, g_ref, coef_ref, out_ref, blocks_ref, sems):
+def bulk_kernel(me_ref, pattern_ref, a_ref, b_ref, c_ref, d_ref, g_hbm, coef_ref, out_ref, blocks_ref, g_ref, sems):
+    weights = weights_into(g_hbm, g_ref, sems, 16)
+    weights[0].start()
     made = copies(into_blocks([a_ref, b_ref, c_ref, d_ref], blocks_ref), sems)
-    coefs = columns_of(coef_ref[skip : skip + out_ref.shape[0]], g_ref.shape[0])
+    for copy in weights[1:]:
+        copy.start()
+    coefs = columns_of(coef_ref[...], g_ref.shape[0])
     finished(made)
 
     @pl.loop(0, g_ref.shape[1])
     def _(c):
-        out_ref[:, lanes_of(c)] = operated(blocks_ref, g_ref, pattern_ref, me_ref[0], coefs, c, True)
-
-
-def bulk(me, pattern, parts, gblocks, coef, skip):
+        wait_weights(g_hbm, g_ref, sems, 16, c)
+        out_ref[:, lanes_of(c)] = operated(blocks_ref, g_ref, pattern_ref, me_ref[0], 0, coefs, c)
+
+
+def bulk(me, pattern, parts, gblocks, coef):
     rows, modes = parts[0].shape
     return pl.pallas_call(
-        functools.partial(bulk_kernel, skip),
-        in_specs=[SMEM, SMEM] + [ANY] * 4 + [VMEM] * 2,
+        bulk_kernel,
+        in_specs=[SMEM, SMEM] + [ANY] * 5 + [VMEM],
         out_specs=VMEM,
         out_shape=shape((rows, modes)),
         scratch_shapes=[
             pltpu.VMEM((4 * modes // LANES, rows, LANES), BF16),
-            pltpu.SemaphoreType.DMA((16,)),
-        ],
-        compiler_params=params(16),
+            pltpu.VMEM(gblocks.shape, BF16),
+            pltpu.SemaphoreType.DMA((16 + gblocks.shape[1],)),
+        ],
+        compiler_params=params(52000),
+        name="whole",
     )(me, pattern, *parts, gblocks, coef)
+
+
+def hold_kernel(g_ref, after_ref, out_ref, sems):
+    del after_ref
+    made = [
+        pltpu.make_async_copy(g_ref.at[:, c], out_ref.at[:, c], sems.at[c])
+        for c in range(out_ref.shape[1])
+    ]
+    for copy in made:
+        copy.start()
+    finished(made)
+
+
+def hold(gblocks, after, count):
+    terms, _, *rest = gblocks.shape
+    return pl.pallas_call(
+        hold_kernel,
+        in_specs=[HBM, ANY],
+        out_specs=VMEM,
+        out_shape=shape((terms, count, *rest), BF16),
+        scratch_shapes=[pltpu.SemaphoreType.DMA((count,))],
+        compiler_params=params(16384),
+    )(gblocks, after)
 
 
 def two_terms(value):
@@ -260,27 +298,37 @@
 LAST, FIRST, NEXT = 32, 33, 48
 
 
-def first_kernel(me_ref, pattern_ref, index_ref, a_ref, b_ref, c_ref, d_ref, g_ref, coef_ref, right_ref, mid_ref, sub_ref, field_ref, inverse_ref, coupling_ref, message_ref, base_ref, diffs_ref, around_ref, blocks_ref, res_ref, sub_vmem, base_vmem, diffs_vmem, rows_ref, sems):
+def first_kernel(me_ref, pattern_ref, index_ref, a_ref, b_ref, c_ref, d_ref, ea_ref, eb_ref, ec_ref, ed_ref, g_hbm, coef_ref, right_ref, sub_ref, field_ref, inverse_ref, coupling_ref, message_ref, base_ref, diffs_ref, around_ref, blocks_ref, res_ref, sub_vmem, base_vmem, diffs_vmem, rows_ref, g_ref, sems):
     nodes, _ = field_ref.shape
     coarse = inverse_ref.shape[0]
+    inner = pl.ds(EDGE, nodes - 2 * EDGE)
+    weights = weights_into(g_hbm, g_ref, sems, 51)
+    weights[0].start()
     made = copies(
-        into_blocks([a_ref, b_ref, c_ref, d_ref], blocks_ref)
-        + [(right_ref, res_ref), (sub_ref, sub_vmem), (field_ref, base_vmem)],
+        into_blocks([a_ref, b_ref, c_ref, d_ref], blocks_ref, inner)
+        + into_blocks([r.at[pl.ds(0, EDGE)] for r in (ea_ref, eb_ref, ec_ref, ed_ref)], blocks_ref, pl.ds(0, EDGE))
+        + into_blocks([r.at[pl.ds(EDGE, EDGE)] for r in (ea_ref, eb_ref, ec_ref, ed_ref)], blocks_ref, pl.ds(nodes - EDGE, EDGE))
+        + [(right_ref, res_ref)],
         sems,
     )
-    coef = jnp.concatenate([coef_ref[:EDGE], coef_ref[nodes - EDGE :]], axis=0)
-    coefs = columns_of(coef, g_ref.shape[0])
-    finished(made[:17])
-    inner = slice(EDGE, nodes - EDGE)
-    res_ref[inner] = res_ref[inner] - mid_ref[...]
+    for copy in weights[1:]:
+        copy.start()
+    later = [
+        pltpu.make_async_copy(sub_ref, sub_vmem, sems.at[49]),
+        pltpu.make_async_copy(field_ref, base_vmem, sems.at[50]),
+    ]
+    for copy in later:
+        copy.start()
+    coefs = columns_of(coef_ref[...], g_ref.shape[0])
+    finished(made)
 
     @pl.loop(0, g_ref.shape[1])
     def _(c):
-        total = operated(blocks_ref, g_ref, pattern_ref, me_ref[0], coefs, c, True)
-        res_ref[:EDGE, lanes_of(c)] = res_ref[:EDGE, lanes_of(c)] - total[:EDGE]
-        res_ref[nodes - EDGE :, lanes_of(c)] = res_ref[nodes - EDGE :, lanes_of(c)] - total[EDGE:]
-
-    finished(made[17:])
+        wait_weights(g_hbm, g_ref, sems, 51, c)
+        total = operated(blocks_ref, g_ref, pattern_ref, me_ref[0], 0, coefs, c)
+        res_ref[:, lanes_of(c)] = res_ref[:, lanes_of(c)] - total
+
+    finished(later)
     for c in range(coarse):
         rows_ref[c : c + 1] = res_ref[pl.ds(index_ref[c], 1), :]
     feed = feed_of(rows_ref[...], inverse_ref[...])
@@ -313,12 +361,12 @@
     finished(out)
 
 
-def first_update(me, pattern, index, parts, gblocks, coef, right, mid, sub_t, field, inverse, coupling, plane):
+def first_update(me, pattern, index, parts, edge_parts, gblocks, coef, right, sub_t, field, inverse, coupling, plane):
     nodes, modes = right.shape
     coarse = inverse.shape[0]
     return pl.pallas_call(
         first_kernel,
-        in_specs=[SMEM] * 3 + [ANY] * 4 + [VMEM] * 2 + [ANY, VMEM] + [ANY] * 2 + [VMEM] * 2,
+        in_specs=[SMEM] * 3 + [ANY] * 9 + [VMEM] + [ANY] * 3 + [VMEM] * 2,
         out_specs=[VMEM, ANY, ANY, VMEM],
         out_shape=[
             shape((plane, coarse, modes + 2 * LANES), BF16),
@@ -327,17 +375,18 @@
             shape((padded(5 * coarse + 4), modes)),
         ],
         scratch_shapes=[
-            pltpu.VMEM((4 * modes // LANES, 2 * EDGE, LANES), BF16),
+            pltpu.VMEM((4 * modes // LANES, nodes, LANES), BF16),
             pltpu.VMEM((nodes, modes), F32),
             pltpu.VMEM((nodes, nodes), BF16),
             pltpu.VMEM((nodes, modes), F32),
             pltpu.VMEM((nodes, modes), BF16),
             pltpu.VMEM((coarse, modes), F32),
-            pltpu.SemaphoreType.DMA((19,)),
-        ],
-        compiler_params=params(24),
+            pltpu.VMEM(gblocks.shape, BF16),
+            pltpu.SemaphoreType.DMA((51 + gblocks.shape[1],)),
+        ],
+        compiler_params=params(52000),
         name="first_update",
-    )(me, pattern, index, *parts, gblocks, coef, right, mid, sub_t, field, inverse, coupling)
+    )(me, pattern, index, *parts, *edge_parts, gblocks, coef, right, sub_t, field, inverse, coupling)
 
 
 def advance(coupling_t, state, push):
@@ -354,18 +403,54 @@
     return block + pltpu.roll(block, LANES - coarse, 1)
 
 
-def plane_kernel(feeds_ref, out_ref):
+def lanes_and_rows(coarse):
+    row = lax.broadcasted_iota(jnp.int32, (coarse, LANES), 0)
+    lane = lax.broadcasted_iota(jnp.int32, (coarse, LANES), 1)
+    return row, lane
+
+
+def side_by_side(squares):
+    coarse = squares[0].shape[0]
+    _, lane = lanes_and_rows(coarse)
+    total = None
+    for n, square in enumerate(squares):
+        square = jnp.where(lane < coarse, square, 0.0)
+        square = pltpu.roll(square, n * coarse, 1) if n else square
+        total = square if total is None else total + square
+    return total
+
+
+def terms_of(weights):
+    return jnp.concatenate(two_terms(weights), axis=0).astype(BF16)
+
+
+def plane_kernel(p_ref, feeds_ref, out_ref, inside_ref, weights_ref, carry_ref):
     plane, coarse, width = feeds_ref.shape
     modes = width - 2 * LANES
-    row = lax.broadcasted_iota(jnp.int32, (coarse, LANES), 0)
-    lane = lax.broadcasted_iota(jnp.int32, (coarse, LANES), 1)
-    matrix = (row == lane).astype(F32)
-    state = jnp.zeros((coarse, modes), F32)
-    for p in range(plane):
-        step = step_of(feeds_ref[p, :, modes : modes + LANES], coarse)
-        state = advance(step, state, feeds_ref[p, :, :modes].astype(F32))
-        matrix = advance(step, matrix, jnp.zeros_like(matrix))
-    matrix = jnp.where(lane < coarse, matrix, 0.0)
+    p = p_ref[0]
+    row, lane = lanes_and_rows(coarse)
+    one = (row == lane).astype(F32)
+    none = jnp.zeros_like(one)
+    whole, before = one, none
+    wholes, befores = [], []
+    for q in range(plane - 1, -1, -1):
+        step = step_of(feeds_ref[q, :, modes : modes + LANES], coarse)
+        before = jnp.where(q == p - 1, one, before)
+        wholes.append(whole)
+        befores.append(before)
+        whole = advance(whole, step, none)
+        before = advance(before, step, none)
+    carry_ref[...] = jnp.where(p == 0, one, before)
+    totals, excluding = side_by_side(wholes[::-1]), side_by_side(befores[::-1])
+    own = step_of(feeds_ref[p, :, modes : modes + LANES], coarse)
+    including = advance(own, excluding, (lane == p * coarse + row).astype(F32))
+    totals = terms_of(totals)
+    weights_ref[...] = jnp.concatenate([totals, terms_of(including)], axis=0)
+    feeds = feeds_ref[:, :, :modes].reshape(plane * coarse, modes)
+    sums = jnp.dot(jnp.concatenate([totals, terms_of(excluding)], axis=0), feeds, preferred_element_type=F32)
+    state = sums[:coarse] + sums[coarse : 2 * coarse]
+    inside_ref[...] = sums[2 * coarse : 3 * coarse] + sums[3 * coarse :]
+    matrix = jnp.where(lane < coarse, whole, 0.0)
     high, low = two_terms(matrix)
     first = feeds_ref[0, :, modes : modes + LANES].astype(F32)
     final = feeds_ref[plane - 1, :, modes : modes + LANES].astype(F32)
@@ -382,63 +467,64 @@
         out_ref[z] = sent
 
 
-def plane_totals(feeds, planes):
-    _, coarse, width = feeds.shape
+def plane_totals(p, feeds, planes):
+    plane, coarse, width = feeds.shape
     return pl.pallas_call(
         plane_kernel,
-        in_specs=[VMEM],
-        out_specs=VMEM,
-        out_shape=shape((planes, coarse, width), BF16),
-        compiler_params=params(8),
+        in_specs=[SMEM, VMEM],
+        out_specs=[VMEM] * 4,
+        out_shape=[
+            shape((planes, coarse, width), BF16),
+            shape((coarse, width - 2 * LANES)),
+            shape((4 * coarse, plane * coarse), BF16),
+            shape((coarse, LANES)),
+        ],
+        compiler_params=params(52000),
         name="plane_totals",
-    )(feeds)
-
-
-def second_plane_kernel(feeds_ref, first_ref, out_ref):
+    )(p, feeds)
+
+
+def second_plane_kernel(feeds_ref, weights_ref, out_ref, inside_ref):
     plane, coarse, modes = feeds_ref.shape
-    state = feeds_ref[0].astype(F32)
-    for p in range(1, plane):
-        step = step_of(first_ref[p, :, modes : modes + LANES], coarse)
-        state = advance(step, state, feeds_ref[p].astype(F32))
+    feeds = feeds_ref[...].reshape(plane * coarse, modes)
+    sums = jnp.dot(weights_ref[...], feeds, preferred_element_type=F32)
+    state = (sums[:coarse] + sums[coarse : 2 * coarse]).astype(BF16)
+    inside_ref[...] = sums[2 * coarse : 3 * coarse] + sums[3 * coarse :]
     for z in range(out_ref.shape[0]):
-        out_ref[z] = state.astype(BF16)
-
-
-def second_plane_totals(feeds, first, planes):
+        out_ref[z] = state
+
+
+def second_plane_totals(feeds, weights, planes):
     _, coarse, modes = feeds.shape
     return pl.pallas_call(
         second_plane_kernel,
         in_specs=[VMEM] * 2,
-        out_specs=VMEM,
-        out_shape=shape((planes, coarse, modes), BF16),
-        compiler_params=params(8),
+        out_specs=[VMEM] * 2,
+        out_shape=[shape((planes, coarse, modes), BF16), shape((coarse, modes))],
+        compiler_params=params(52000),
         name="second_plane_totals",
-    )(feeds, first)
-
-
-def errors(z_ref, p_ref, feeds_ref, totals_ref, steps_ref, plane_steps_ref):
-    coarse = steps_ref.shape[1]
-    modes = steps_ref.shape[2] - 2 * LANES
-
-    def across(z, state):
-        step = step_of(plane_steps_ref[z, :, modes : modes + LANES], coarse)
-        return advance(step, state, totals_ref[z, :, :modes].astype(F32))
-
-    def within(p, state):
-        step = step_of(steps_ref[p, :, modes : modes + LANES], coarse)
-        return advance(step, state, feeds_ref[p, :, :modes].astype(F32))
-
-    before = lax.fori_loop(0, z_ref[0], across, jnp.zeros((coarse, modes), F32))
-    before = lax.fori_loop(0, p_ref[0], within, before)
-    return before, within(p_ref[0], before)
-
-
-def correct_kernel(z_ref, p_ref, index_ref, feeds_ref, totals_ref, around_ref, sent_ref, error_ref, wide_ref, rows_ref):
+    )(feeds, weights)
+
+
+def correct_kernel(z_ref, p_ref, index_ref, feeds_ref, totals_ref, inside_ref, carry_ref, around_ref, sent_ref, error_ref, weights_ref, wide_ref, rows_ref):
     nodes, modes = wide_ref.shape[0] - 16, wide_ref.shape[1]
     plane, planes = feeds_ref.shape[0], totals_ref.shape[0]
     z, p = z_ref[0], p_ref[0]
-    before, error = errors(z_ref, p_ref, feeds_ref, totals_ref, feeds_ref, totals_ref)
-    coarse = error.shape[0]
+    coarse = index_ref.shape[0]
+    none = jnp.zeros((coarse, LANES), F32)
+    factor = none
+    factors = []
+    for q in range(planes - 1, -1, -1):
+        factor = jnp.where(q == z - 1, carry_ref[...], factor)
+        factors.append(factor)
+        factor = advance(factor, step_of(totals_ref[q, :, modes : modes + LANES], coarse), none)
+    weights = side_by_side(factors[::-1])
+    totals = totals_ref[:, :, :modes].reshape(planes * coarse, modes)
+    sums = jnp.dot(terms_of(weights), totals, preferred_element_type=F32)
+    before = inside_ref[...] + sums[:coarse] + sums[coarse:]
+    own = step_of(feeds_ref[p, :, modes : modes + LANES], coarse)
+    error = advance(own, before, feeds_ref[p, :, :modes].astype(F32))
+    weights_ref[...] = terms_of(advance(own, weights, none))
 
     block, edge = slice(modes, modes + LANES), slice(modes + LANES, modes + 2 * LANES)
     p_left, z_left = jnp.maximum(p - 1, 0), jnp.maximum(z - 1, 0)
@@ -473,34 +559,36 @@
         rows_ref[j : j + 1] = (
             2.0 * wide_ref[at(8 + n), :] - wide_ref[at(7 + n), :] - wide_ref[at(9 + n), :]
         )
-    sent = rows_ref[...].astype(BF16)
-    for m in range(sent_ref.shape[0]):
-        sent_ref[m] = sent
-
-
-def correct(z, p, index, feeds, totals, near, nodes, modes_by):
+    sent_ref[...] = rows_ref[...].astype(BF16)
+
+
+def correct(z, p, index, feeds, totals, inside, carry, near, nodes):
     modes = near.shape[1]
     coarse = index.shape[0]
     rows = padded(3 * coarse + 2)
     return pl.pallas_call(
         correct_kernel,
-        in_specs=[SMEM] * 3 + [VMEM] * 3,
-        out_specs=[VMEM] * 2,
-        out_shape=[shape((modes_by, rows, modes), BF16), shape((coarse, modes))],
+        in_specs=[SMEM] * 3 + [VMEM] * 5,
+        out_specs=[VMEM] * 3,
+        out_shape=[
+            shape((rows, modes), BF16),
+            shape((coarse, modes)),
+            shape((2 * coarse, totals.shape[0] * coarse), BF16),
+        ],
         scratch_shapes=[pltpu.VMEM((nodes + 16, modes), F32), pltpu.VMEM((rows, modes), F32)],
-        compiler_params=params(16),
+        compiler_params=params(52000),
         name="correct",
-    )(z, p, index, feeds, totals, near)
-
-
-def redo_kernel(me_ref, pattern_ref, diffs_ref, g_ref, coef_ref, right_ref, inverse_ref, message_ref, res_ref, blocks_ref, rows_ref, sems):
-    made = copies(into_blocks([diffs_ref.at[m] for m in range(diffs_ref.shape[0])], blocks_ref), sems)
+    )(z, p, index, feeds, totals, inside, carry, near)
+
+
+def redo_kernel(me_ref, pattern_ref, a_ref, b_ref, c_ref, d_ref, g_ref, coef_ref, right_ref, inverse_ref, message_ref, res_ref, blocks_ref, rows_ref, sems):
+    made = copies(into_blocks([a_ref, b_ref, c_ref, d_ref], blocks_ref), sems)
     coefs = columns_of(coef_ref[...], g_ref.shape[0])
     finished(made)
 
     @pl.loop(0, g_ref.shape[1])
     def _(c):
-        total = operated(blocks_ref, g_ref, pattern_ref, me_ref[0], coefs, c, False)
+        total = operated(blocks_ref, g_ref, pattern_ref, me_ref[0], 0, coefs, c)
         res_ref[:, lanes_of(c)] = right_ref[:, lanes_of(c)] - total
 
     for c in range(inverse_ref.shape[0]):
@@ -510,12 +598,12 @@
         message_ref[p] = feed
 
 
-def redo(me, pattern, diffs, gblocks, coef_rows, right_rows, inverse, plane):
+def redo(me, pattern, parts, gblocks, coef_rows, right_rows, inverse, plane):
     rows, modes = right_rows.shape
     coarse = inverse.shape[0]
     return pl.pallas_call(
         redo_kernel,
-        in_specs=[SMEM] * 2 + [ANY] + [VMEM] * 4,
+        in_specs=[SMEM] * 2 + [ANY] * 4 + [VMEM] * 4,
         out_specs=[VMEM] * 2,
         out_shape=[shape((plane, coarse, modes), BF16), shape((rows, modes))],
         scratch_shapes=[
@@ -523,9 +611,9 @@
             pltpu.VMEM((coarse, modes), F32),
             pltpu.SemaphoreType.DMA((16,)),
         ],
-        compiler_params=params(16),
+        compiler_params=params(52000),
         name="redo",
-    )(me, pattern, diffs, gblocks, coef_rows, right_rows, inverse)
+    )(me, pattern, *parts, gblocks, coef_rows, right_rows, inverse)
 
 
 def last_local_kernel(index_ref, op_ref, right_ref, rows_ref, sub_ref, base_ref, error_ref, base_out_ref, res_out_ref, res_ref, field_ref):
@@ -564,12 +652,14 @@
     )(index, op, right, rows, sub_t, base, error)
 
 
-def last_kernel(z_ref, p_ref, index_ref, feeds_ref, totals_ref, steps_ref, plane_steps_ref, base_ref, out_ref, base_vmem, out_vmem, sems):
+def last_kernel(index_ref, totals_ref, inside_ref, weights_ref, base_ref, out_ref, base_vmem, out_vmem, sems):
     modes, nodes = base_ref.shape
     load = pltpu.make_async_copy(base_ref, base_vmem, sems.at[0])
     load.start()
-    _, error = errors(z_ref, p_ref, feeds_ref, totals_ref, steps_ref, plane_steps_ref)
-    coarse = error.shape[0]
+    planes, coarse, _ = totals_ref.shape
+    totals = totals_ref[...].reshape(planes * coarse, modes)
+    sums = jnp.dot(weights_ref[...], totals, preferred_element_type=F32)
+    error = inside_ref[...] + sums[:coarse] + sums[coarse:]
     high = error.astype(BF16).astype(F32)
     rest = error - high
     mid = rest.astype(BF16).astype(F32)
@@ -591,11 +681,11 @@
     finished(made)
 
 
-def last(z, p, index, feeds, totals, steps, plane_steps, base):
+def last(index, totals, inside, weights, base):
     modes, _ = base.shape
     return pl.pallas_call(
         last_kernel,
-        in_specs=[SMEM] * 3 + [VMEM] * 4 + [ANY],
+        in_specs=[SMEM] + [VMEM] * 3 + [ANY],
         out_specs=ANY,
         out_shape=shape(base.shape),
         scratch_shapes=[
@@ -603,9 +693,9 @@
             pltpu.VMEM(base.shape, F32),
             pltpu.SemaphoreType.DMA((1 + modes // LANES,)),
         ],
-        compiler_params=params(16),
+        compiler_params=params(52000),
         name="last",
-    )(z, p, index, feeds, totals, steps, plane_steps, base)
+    )(index, totals, inside, weights, base)
 
 
 def from_neighbours(last_rows, first_rows):
@@ -622,6 +712,13 @@
     beside = lax.ppermute(own, "core", swap)
     onward = lax.ppermute(across, "core", swap)
     return own, beside, across, onward
+
+
+def over_modes_directly(own):
+    across = lax.ppermute(own, "yl", [(0, 1), (1, 0)])
+    diagonal = lax.ppermute(own, MODE, [(0, 3), (1, 2), (2, 1), (3, 0)])
+    beside = lax.ppermute(own, "core", [(0, 1), (1, 0)])
+    return own, beside, across, diagonal
 
 
 def shards(right_side, start_field, coefficient, gblocks, pattern, sub_inverse, coarse_index, coarse_inv, coupling):
@@ -634,28 +731,27 @@
     parts = over_modes(diffs)
     left, right = from_neighbours(last_rows, first_rows)
     edge_rows = edges(top, low, left, right)
-    edge_parts = over_modes(edge_rows)
+    edge_parts = over_modes_directly(edge_rows)
     rhs, sub_t, field, coef, right_rows, coef_rows = prepare(
         coarse_index, right_side, sub_inverse, start_field, coefficient
     )
-    mid = bulk(me, pattern, parts, gblocks, coef, EDGE)
     message, base, diffs, near = first_update(
-        me, pattern, coarse_index, edge_parts, gblocks, coef, rhs, mid, sub_t, field, coarse_inv, coupling, plane
+        me, pattern, coarse_index, parts, edge_parts, gblocks, coef, rhs, sub_t, field, coarse_inv, coupling, plane
     )
+    parts = over_modes(diffs)
     feeds = lax.all_to_all(message, PLANE, 0, 0, tiled=True)
-    diffs, feeds = lax.optimization_barrier((diffs, feeds))
-    parts = over_modes(diffs)
-    totals = plane_totals(feeds, planes)
+    totals, inside, weights, carry = plane_totals(p, feeds, planes)
     totals = lax.all_to_all(totals, "z", 0, 0, tiled=True)
-    rows, error = correct(z, p, coarse_index, feeds, totals, near, nodes, lax.axis_size(MODE))
-    rows = lax.all_to_all(rows, MODE, 0, 0, tiled=True)
-    op = bulk(me, pattern, parts, gblocks, coef, 0)
-    message, res_rows = redo(me, pattern, rows, gblocks, coef_rows, right_rows, coarse_inv, plane)
+    rows, error, plane_weights = correct(z, p, coarse_index, feeds, totals, inside, carry, near, nodes)
+    rows = over_modes_directly(rows)
+    op = bulk(me, pattern, parts, gblocks, coef)
+    held = hold(gblocks, error, gblocks.shape[1])
+    message, res_rows = redo(me, pattern, rows, held, coef_rows, right_rows, coarse_inv, plane)
     later = lax.all_to_all(message, PLANE, 0, 0, tiled=True)
     base, residual = last_local(coarse_index, op, rhs, res_rows, sub_t, base, error)
-    later_totals = second_plane_totals(later, feeds, planes)
+    later_totals, inside = second_plane_totals(later, weights, planes)
     later_totals = lax.all_to_all(later_totals, "z", 0, 0, tiled=True)
-    field = last(z, p, coarse_index, later, later_totals, feeds, totals, base)
+    field = last(coarse_index, later_totals, inside, plane_weights, base)
     return field, residual
 
 

time: 145 us -> 141 us (0.972)
  blocking collectives: 29.2 us -> 14.1 us
  starting transfers between devices: 31.7 us -> 40.2 us
  waiting for transfers between devices: 29.9 us -> 32.7 us
    all_to_all x1 -> x0, blocking collectives: 16.5 us -> none  [shards(): feeds = lax.all_to_all(message, PLANE, 0, 0, tiled=True)]
    all_to_all x1, starting transfers between devices: 3.54 us -> 9.14 us  [shards(): feeds = lax.all_to_all(message, PLANE, 0, 0, tiled=True)]
    ppermute x0 -> x6, starting transfers between devices: none -> 4.08 us  [the longest x2 3.34 us: over_modes_directly(): across = lax.ppermute(own, 'yl', [(0, 1), (1, 0)])]
    all_to_all x1, waiting for transfers between devices: 5.37 us -> 8.37 us  [shards(): feeds = lax.all_to_all(message, PLANE, 0, 0, tiled=True)]
    ppermute x0 -> x6, waiting for transfers between devices: none -> 2.73 us  [the longest x2 1.4 us: over_modes_directly(): across = lax.ppermute(own, 'yl', [(0, 1), (1, 0)])]
    ppermute x3 -> x2, waiting for transfers between devices: 14.1 us -> 11.6 us  [over_modes(): across = lax.ppermute(own, 'yl', swap)]
    all_to_all x1, blocking collectives: 12.6 us -> 14.1 us  [shards(): later = lax.all_to_all(message, PLANE, 0, 0, tiled=True)]
    ppermute x3 -> x2, starting transfers between devices: 4.28 us -> 2.78 us  [over_modes(): across = lax.ppermute(own, 'yl', swap)]
  transfers between devices with their start and end apart: 14 -> 17, of which waited for: 5 -> 6; matrix products, arithmetic and copies ran while one was open for 0% -> 0% of each run, Pallas kernels for 18% -> 16%
where the time goes in v2:
time: 141 us; the launch traced here: 140 us
  starting transfers between devices  40.2 us (29%)
  Pallas kernels  36.8 us (26%)
  waiting for transfers between devices  32.7 us (23%)
  local copies, waits for them, and re-layouts  15.2 us (11%)
  blocking collectives  14.1 us (10%)
    unnamed x68, local copies, waits for them, and re-layouts  15.2 us
    all_to_all x1, blocking collectives, shards(): later = lax.all_to_all(message, PLANE, 0, 0, tiled=True)  14.1 us
    ppermute x2, waiting for transfers between devices, over_modes(): across = lax.ppermute(own, 'yl', swap)  11.6 us
    all_to_all x1, starting transfers between devices, shards(): feeds = lax.all_to_all(message, PLANE, 0, 0, tiled=True)  9.14 us
    all_to_all x1, starting transfers between devices, shards(): totals = lax.all_to_all(totals, 'z', 0, 0, tiled=True)  8.57 us
    all_to_all x1, waiting for transfers between devices, shards(): feeds = lax.all_to_all(message, PLANE, 0, 0, tiled=True)  8.37 us
    pallas_call x1, Pallas kernels, first_update(): pl.pallas_call(first_kernel, in_specs=[SMEM] * 3 + [ANY] * 9 + [VMEM] + [...  8.08 us
    all_to_all x1, waiting for transfers between devices, shards(): totals = lax.all_to_all(totals, 'z', 0, 0, tiled=True)  7.9 us
  transfers between devices with their start and end apart: 17, of which 6 were waited for; matrix products, arithmetic and copies ran while one was open for 0% of the time, Pallas kernels for 16%

profile of v2, /device:TPU:32, one launch (start us, length us, event | category | flops | bytes accessed | tf_op | source)
XLA Modules:
  0.0 140.2 jit_solution(16595744443071332121)
XLA Ops:
  0.7 3.6 %start.1 = (bf16[480,512]{1,0:T(8,128)(2,1)}, f32[24,512]{1,0:T(8,128)}, f32[24,512]{1,0:T(8,128)}, f32[8,512]{1,0:T(8,128)}, f32[8,512]{1,0:T(8,128)}) custom-call(f32[512,512]{1,0:T(8,128)} %field_ref.3), custom_call_target="tpu_custom_call" | custom-call | tf_op jit(solution)/shard_map/start/pallas_call | solution.py:42
  4.3 1.7 %collective-permute-start.1 = (bf16[480,512]{1,0:T(8,128)(2,1)}, bf16[480,512]{1,0:T(8,128)(2,1)S(1)}, u32[]{:S(2)}, u32[]{:S(2)}) collective-permute-start(bf16[480,512]{1,0:T(8,128)(2,1)} %get-tuple-element.30.a_ref), channel_id=1, source_target_pairs={{0,2},{2,0},{1,3},{3,1},{4,6},{6,4},{5,7},{7,5},{8,10},{10,8},{9,1... | collective-permute-start | bytes 1474568 | tf_op jit(solution)/shard_map/ppermute | solution.py:711
  6.0 11.6 %collective-permute-done.1.c_ref = bf16[480,512]{1,0:T(8,128)(2,1)S(1)} collective-permute-done((bf16[480,512]{1,0:T(8,128)(2,1)}, bf16[480,512]{1,0:T(8,128)(2,1)S(1)}, u32[]{:S(2)}, u32[]{:S(2)}) %collective-permute-start.1) | collective-permute-done | bytes 491552 | tf_op jit(solution)/shard_map/ppermute | solution.py:711
  17.6 5.1 %collective-permute-start.3 = (f32[8,512]{1,0:T(8,128)}, f32[8,512]{1,0:T(8,128)S(1)}, u32[]{:S(2)}, u32[]{:S(2)}) collective-permute-start(f32[8,512]{1,0:T(8,128)} %get-tuple-element.33), channel_id=1, source_target_pairs={{0,4},{4,8},{8,12},{12,16},{16,20},{20,24},{24,28},{28,32},{32,36}... | collective-permute-start | bytes 49160 | tf_op jit(solution)/shard_map/ppermute | solution.py:704
  22.7 5.3 %collective-permute-start.4 = (f32[8,512]{1,0:T(8,128)}, f32[8,512]{1,0:T(8,128)S(1)}, u32[]{:S(2)}, u32[]{:S(2)}) collective-permute-start(f32[8,512]{1,0:T(8,128)} %get-tuple-element.34), channel_id=1, source_target_pairs={{4,0},{8,4},{12,8},{16,12},{20,16},{24,20},{28,24},{32,28},{36,32}... | collective-permute-start | bytes 49160 | tf_op jit(solution)/shard_map/ppermute | solution.py:705
  27.9 2.1 %collective-permute-done.4.right_ref = f32[8,512]{1,0:T(8,128)S(1)} collective-permute-done((f32[8,512]{1,0:T(8,128)}, f32[8,512]{1,0:T(8,128)S(1)}, u32[]{:S(2)}, u32[]{:S(2)}) %collective-permute-start.4) | collective-permute-done | bytes 16416 | tf_op jit(solution)/shard_map/ppermute | solution.py:705
  31.7 1.2 collective-permute-start.6
  33.6 4.6 %prepare.1 = (f32[512,512]{1,0:T(8,128)}, bf16[512,512]{1,0:T(8,128)(2,1)}, f32[512,512]{1,0:T(8,128)}, f32[512,128]{1,0:T(8,128)}, f32[64,512]{1,0:T(8,128)}, /*index=5*/f32[64,128]{1,0:T(8,128)}) custom-call(s32[16]{0:T(128)} %index_ref.9, f32[512,512]{1,0:T(8,128)} %right_ref.1, bf16[512,512]{1,0:T(8,128)(2,1)} %inverse_ref.3, f32[512,512]{1,0:T(8,128)} %field_ref.3, ...), custom_call_target="tpu_custom_call" | custom-call | tf_op jit(solution)/shard_map/prepare/pallas_call | solution.py:107
  39.8 0.9 copy-done.1
  40.8 1.0 copy-done.6
  41.8 1.0 copy-done.8
  42.8 1.0 copy-done.10
  43.9 8.1 %first_update.1 = (bf16[8,16,768]{2,1,0:T(8,128)(2,1)}, f32[512,512]{1,0:T(8,128)}, bf16[512,512]{1,0:T(8,128)(2,1)S(1)}, f32[96,512]{1,0:T(8,128)S(1)}) custom-call(s32[1]{0:T(128)} %bitcast.me_ref, s32[4,4,16]{2,1,0:T(4,128)S(1)} %bitcast.4, s32[16]{0:T(128)S(1)} %copy-done.26, bf16[480,512]{1,0:T(8,128)(2,1)S(1)} %copy-done.4, ...), custom_call_target="tpu_custom_call" | custom-call | tf_op jit(solution)/shard_map/first_update/pallas_call | solution.py:367
  52.6 1.1 collective-permute-start.12
  53.8 9.1 %all-to-all-start = ((bf16[8,16,768]{2,1,0:T(8,128)(2,1)}), bf16[8,16,768]{2,1,0:T(8,128)(2,1)S(1)}, u32[]{:S(2)}, u32[]{:S(2)}) async-start(bf16[8,16,768]{2,1,0:T(8,128)(2,1)} %get-tuple-element.39), calls=%async_computation | async-start | bytes 393216 | tf_op jit(solution)/shard_map/all_to_all | solution.py:742
  62.9 8.4 %all-to-all-done.feeds_ref = bf16[8,16,768]{2,1,0:T(8,128)(2,1)S(1)} async-done(((bf16[8,16,768]{2,1,0:T(8,128)(2,1)}), bf16[8,16,768]{2,1,0:T(8,128)(2,1)S(1)}, u32[]{:S(2)}, u32[]{:S(2)}) %all-to-all-start) | async-done | bytes 196640 | tf_op jit(solution)/shard_map/all_to_all | solution.py:742
  71.3 1.5 %plane_totals.1 = (bf16[8,16,768]{2,1,0:T(8,128)(2,1)S(1)}, f32[16,512]{1,0:T(8,128)S(1)}, bf16[64,128]{1,0:T(8,128)(2,1)S(1)}, f32[16,128]{1,0:T(8,128)S(1)}) custom-call(s32[1]{0:T(128)} %bitcast.3.p_ref, bf16[8,16,768]{2,1,0:T(8,128)(2,1)S(1)} %all-to-all-done.feeds_ref), custom_call_target="tpu_custom_call" | custom-call | tf_op jit(solution)/shard_map/plane_totals/pallas_call | solution.py:472
  75.3 8.6 %all-to-all-start.1 = ((bf16[8,16,768]{2,1,0:T(8,128)(2,1)}), bf16[8,16,768]{2,1,0:T(8,128)(2,1)S(1)}, u32[]{:S(2)}, u32[]{:S(2)}) async-start(bf16[8,16,768]{2,1,0:T(8,128)(2,1)} %copy-done.11), calls=%async_computation.1 | async-start | bytes 393216 | tf_op jit(solution)/shard_map/all_to_all | solution.py:744
  84.4 7.9 %all-to-all-done.1.totals_ref = bf16[8,16,768]{2,1,0:T(8,128)(2,1)S(1)} async-done(((bf16[8,16,768]{2,1,0:T(8,128)(2,1)}), bf16[8,16,768]{2,1,0:T(8,128)(2,1)S(1)}, u32[]{:S(2)}, u32[]{:S(2)}) %all-to-all-start.1) | async-done | bytes 196640 | tf_op jit(solution)/shard_map/all_to_all | solution.py:744
  92.3 0.9 copy-done.13
  95.3 2.1 %correct.1 = (bf16[64,512]{1,0:T(8,128)(2,1)S(1)}, f32[16,512]{1,0:T(8,128)S(1)}, bf16[32,128]{1,0:T(8,128)(2,1)S(1)}) custom-call(s32[1]{0:T(128)} %bitcast.2.z_ref, s32[1]{0:T(128)} %bitcast.3.p_ref, s32[16]{0:T(128)S(1)} %copy-done.27, bf16[8,16,768]{2,1,0:T(8,128)(2,1)S(1)} %all-to-all-done.feeds_ref, bf16[8,16,768]{2,1,0:T(8,128)(2,1)S(1)} %all-to-all-done.1.totals_ref, ...), custom_call_target="tpu_custom_call" | custom-call | tf_op jit(solution)/shard_map/correct/pallas_call | solution.py:569
  98.1 2.1 %collective-permute-start.9 = (bf16[64,512]{1,0:T(8,128)(2,1)S(1)}, bf16[64,512]{1,0:T(8,128)(2,1)S(1)}, u32[]{:S(2)}, u32[]{:S(2)}) collective-permute-start(bf16[64,512]{1,0:T(8,128)(2,1)S(1)} %get-tuple-element.44.a_ref), channel_id=1, source_target_pairs={{0,2},{2,0},{1,3},{3,1},{4,6},{6,4},{5,7},{7,5},{8,10},{10,8},{9,1... | collective-permute-start | bytes 196616 | tf_op jit(solution)/shard_map/ppermute | solution.py:718
  100.4 1.3 collective-permute-done.10.d_ref
  101.7 1.4 collective-permute-done.9.c_ref
  103.1 2.0 %redo.1 = (bf16[8,16,512]{2,1,0:T(8,128)(2,1)S(1)}, f32[64,512]{1,0:T(8,128)S(1)}) custom-call(s32[1]{0:T(128)} %bitcast.me_ref, s32[4,4,16]{2,1,0:T(4,128)S(1)} %bitcast.5, bf16[64,512]{1,0:T(8,128)(2,1)S(1)} %get-tuple-element.44.a_ref, bf16[64,512]{1,0:T(8,128)(2,1)S(1)} %collective-permute-done.8.b_ref, ...), custom_call_target="tpu_custom_call" | custom-call | tf_op jit(solution)/shard_map/redo/pallas_call | solution.py:604
  105.2 14.1 %all_to_all.20.feeds_ref = bf16[8,16,512]{2,1,0:T(8,128)(2,1)S(1)} all-to-all(bf16[8,16,512]{2,1,0:T(8,128)(2,1)S(1)} %get-tuple-element.48), channel_id=1, replica_groups=mesh['z'=8,'x'=4,'yh'=2,'yl'=2,'core'=2] {'x','yh'}, dimensions={0} | all-to-all | bytes 262144 | tf_op jit(solution)/shard_map/all_to_all | solution.py:750
  119.3 0.8 second_plane_totals.1
  120.1 4.7 %all-to-all-start.3 = ((bf16[8,16,512]{2,1,0:T(8,128)(2,1)}), bf16[8,16,512]{2,1,0:T(8,128)(2,1)S(1)}, u32[]{:S(2)}, u32[]{:S(2)}) async-start(bf16[8,16,512]{2,1,0:T(8,128)(2,1)} %get-tuple-element.50), calls=%async_computation.3 | async-start | bytes 262144 | tf_op jit(solution)/shard_map/all_to_all | solution.py:753
  124.9 6.2 %whole.1.op_ref = f32[512,512]{1,0:T(8,128)} custom-call(s32[1]{0:T(128)} %bitcast.me_ref, s32[4,4,16]{2,1,0:T(4,128)S(1)} %bitcast.6, bf16[512,512]{1,0:T(8,128)(2,1)S(1)} %get-tuple-element.53.a_ref, bf16[512,512]{1,0:T(8,128)(2,1)} %collective-permute-done.11.b_ref, bf16[512,512]{1,0:T(8,128)(2,1)S(1)} %collective-permute-done.12.c_ref, ...), custom_call_target="tpu_custom_call" | custom-call | tf_op jit(solution)/shard_map/whole/pallas_call | solution.py:228
  131.1 5.6 %last_local.1 = (f32[512,512]{1,0:T(8,128)}, f32[512,512]{1,0:T(8,128)}) custom-call(s32[16]{0:T(128)} %index_ref.9, f32[512,512]{1,0:T(8,128)} %whole.1.op_ref, f32[512,512]{1,0:T(8,128)} %get-tuple-element.36.right_ref, f32[64,512]{1,0:T(8,128)} %copy-done.16, bf16[512,512]{1,0:T(8,128)(2,1)} %get-tuple-element.37.sub_ref, ...), custom_call_target="tpu_custom_call" | custom-call | tf_op jit(solution)/shard_map/last_local/pallas_call | solution.py:636
  136.8 1.2 copy-done.3
  138.0 2.0 %last.1 = f32[512,512]{1,0:T(8,128)} custom-call(s32[16]{0:T(128)S(1)} %copy-done.28, bf16[8,16,512]{2,1,0:T(8,128)(2,1)S(1)} %all-to-all-done.3.totals_ref, f32[16,512]{1,0:T(8,128)S(1)} %get-tuple-element.51.inside_ref, bf16[32,128]{1,0:T(8,128)(2,1)S(1)} %copy-done.31, f32[512,512]{1,0:T(8,128)S(1)} %copy-done.3), custom_call_target="tpu_custom_call" | custom-call | tf_op jit(solution)/shard_map/last/pallas_call | solution.py:686
  (83 shorter events, 10.6 us)
Async XLA Ops:
  0.6 39.2 %copy-start.26 = (s32[16]{0:T(128)S(1)}, s32[16]{0:T(128)}, u32[]{:S(2)}) copy-start(s32[16]{0:T(128)} %index_ref.9) | copy-start | bytes 196
  0.6 39.2 %copy-start.17 = (s32[4,16,4]{1,2,0:T(4,128)S(1)}, s32[4,16,4]{1,2,0:T(4,128)}, u32[]{:S(2)}) copy-start(s32[4,16,4]{1,2,0:T(4,128)} %param.13) | copy-start | bytes 3076
  0.7 39.2 %copy-start.21 = (f32[16,16]{1,0:T(8,128)S(1)}, f32[16,16]{1,0:T(8,128)}, u32[]{:S(2)}) copy-start(f32[16,16]{1,0:T(8,128)} %inverse_ref.5) | copy-start | bytes 3076
  0.7 39.2 %copy-start.29 = (f32[16,16]{1,0:T(8,128)S(1)}, f32[16,16]{1,0:T(8,128)}, u32[]{:S(2)}) copy-start(f32[16,16]{1,0:T(8,128)} %coupling_ref.1) | copy-start | bytes 3076
  4.3 35.5 %copy-start.4 = (bf16[480,512]{1,0:T(8,128)(2,1)S(1)}, bf16[480,512]{1,0:T(8,128)(2,1)}, u32[]{:S(2)}) copy-start(bf16[480,512]{1,0:T(8,128)(2,1)} %get-tuple-element.30.a_ref) | copy-start | bytes 1474564
  4.3 13.3 %collective-permute-start.1 = (bf16[480,512]{1,0:T(8,128)(2,1)}, bf16[480,512]{1,0:T(8,128)(2,1)S(1)}, u32[]{:S(2)}, u32[]{:S(2)}) collective-permute-start(bf16[480,512]{1,0:T(8,128)(2,1)} %get-tuple-element.30.a_ref), channel_id=1, source_target_pairs={{0,2},{2,0},{1,3},{3,1},{4,6},{6,4},{5,7},{7,5},{8,10},{10,8},{9,1... | collective-permute-start | bytes 1474568 | tf_op jit(solution)/shard_map/ppermute | solution.py:711
  6.0 32.3 %collective-permute-start = (bf16[480,512]{1,0:T(8,128)(2,1)}, bf16[480,512]{1,0:T(8,128)(2,1)S(1)}, u32[]{:S(2)}, u32[]{:S(2)}) collective-permute-start(bf16[480,512]{1,0:T(8,128)(2,1)} %get-tuple-element.30.a_ref), channel_id=1, source_target_pairs={{0,1},{1,0},{2,3},{3,2},{4,5},{5,4},{6,7},{7,6},{8,9},{9,8},{10,11... | collective-permute-start | bytes 1474568 | tf_op jit(solution)/shard_map/ppermute | solution.py:712
  17.5 22.3 %copy-start.5 = (bf16[480,512]{1,0:T(8,128)(2,1)}, bf16[480,512]{1,0:T(8,128)(2,1)S(1)}, u32[]{:S(2)}) copy-start(bf16[480,512]{1,0:T(8,128)(2,1)S(1)} %collective-permute-done.1.c_ref) | copy-start | bytes 1474564
  17.5 21.5 %collective-permute-start.2 = (bf16[480,512]{1,0:T(8,128)(2,1)S(1)}, bf16[480,512]{1,0:T(8,128)(2,1)S(1)}, u32[]{:S(2)}, u32[]{:S(2)}) collective-permute-start(bf16[480,512]{1,0:T(8,128)(2,1)S(1)} %collective-permute-done.1.c_ref), channel_id=1, source_target_pairs={{0,1},{1,0},{2,3},{3,2},{4,5},{5,4},{6,7},{7,6},{8,9},{9,8},{10,11... | collective-permute-start | bytes 1474568 | tf_op jit(solution)/shard_map/ppermute | solution.py:713
  17.6 10.4 %collective-permute-start.3 = (f32[8,512]{1,0:T(8,128)}, f32[8,512]{1,0:T(8,128)S(1)}, u32[]{:S(2)}, u32[]{:S(2)}) collective-permute-start(f32[8,512]{1,0:T(8,128)} %get-tuple-element.33), channel_id=1, source_target_pairs={{0,4},{4,8},{8,12},{12,16},{16,20},{20,24},{24,28},{28,32},{32,36}... | collective-permute-start | bytes 49160 | tf_op jit(solution)/shard_map/ppermute | solution.py:704
  22.7 7.3 %collective-permute-start.4 = (f32[8,512]{1,0:T(8,128)}, f32[8,512]{1,0:T(8,128)S(1)}, u32[]{:S(2)}, u32[]{:S(2)}) collective-permute-start(f32[8,512]{1,0:T(8,128)} %get-tuple-element.34), channel_id=1, source_target_pairs={{4,0},{8,4},{12,8},{16,12},{20,16},{24,20},{28,24},{32,28},{36,32}... | collective-permute-start | bytes 49160 | tf_op jit(solution)/shard_map/ppermute | solution.py:705
  31.6 6.6 %collective-permute-start.5 = (bf16[32,512]{1,0:T(8,128)(2,1)S(1)}, bf16[32,512]{1,0:T(8,128)(2,1)S(1)}, u32[]{:S(2)}, u32[]{:S(2)}) collective-permute-start(bf16[32,512]{1,0:T(8,128)(2,1)S(1)} %edges.1.ea_ref), channel_id=1, source_target_pairs={{0,1},{1,0},{2,3},{3,2},{4,5},{5,4},{6,7},{7,6},{8,9},{9,8},{10,11... | collective-permute-start | bytes 98312 | tf_op jit(solution)/shard_map/ppermute | solution.py:720
  31.7 6.5 %collective-permute-start.6 = (bf16[32,512]{1,0:T(8,128)(2,1)S(1)}, bf16[32,512]{1,0:T(8,128)(2,1)S(1)}, u32[]{:S(2)}, u32[]{:S(2)}) collective-permute-start(bf16[32,512]{1,0:T(8,128)(2,1)S(1)} %edges.1.ea_ref), channel_id=1, source_target_pairs={{0,2},{2,0},{1,3},{3,1},{4,6},{6,4},{5,7},{7,5},{8,10},{10,8},{9,1... | collective-permute-start | bytes 98312 | tf_op jit(solution)/shard_map/ppermute | solution.py:718
  32.9 5.3 %collective-permute-start.7 = (bf16[32,512]{1,0:T(8,128)(2,1)S(1)}, bf16[32,512]{1,0:T(8,128)(2,1)S(1)}, u32[]{:S(2)}, u32[]{:S(2)}) collective-permute-start(bf16[32,512]{1,0:T(8,128)(2,1)S(1)} %edges.1.ea_ref), channel_id=1, source_target_pairs={{0,3},{1,2},{2,1},{3,0},{4,7},{5,6},{6,5},{7,4},{8,11},{9,10},{10,... | collective-permute-start | bytes 98312 | tf_op jit(solution)/shard_map/ppermute | solution.py:719
  43.9 56.3 %copy-start = (bf16[4,4,4,128,128]{4,3,2,1,0:T(8,128)(2,1)S(1)}, bf16[4,4,4,128,128]{4,3,2,1,0:T(8,128)(2,1)}, u32[]{:S(2)}) copy-start(bf16[4,4,4,128,128]{4,3,2,1,0:T(8,128)(2,1)} %g_hbm.3) | copy-start | bytes 6291460
  52.6 31.2 %collective-permute-start.12 = (bf16[512,512]{1,0:T(8,128)(2,1)S(1)}, bf16[512,512]{1,0:T(8,128)(2,1)S(1)}, u32[]{:S(2)}, u32[]{:S(2)}) collective-permute-start(bf16[512,512]{1,0:T(8,128)(2,1)S(1)} %get-tuple-element.53.a_ref), channel_id=1, source_target_pairs={{0,2},{2,0},{1,3},{3,1},{4,6},{6,4},{5,7},{7,5},{8,10},{10,8},{9,1... | collective-permute-start | bytes 1572872 | tf_op jit(solution)/shard_map/ppermute | solution.py:711
  53.8 17.5 %all-to-all-start = ((bf16[8,16,768]{2,1,0:T(8,128)(2,1)}), bf16[8,16,768]{2,1,0:T(8,128)(2,1)S(1)}, u32[]{:S(2)}, u32[]{:S(2)}) async-start(bf16[8,16,768]{2,1,0:T(8,128)(2,1)} %get-tuple-element.39), calls=%async_computation | async-start | bytes 393216 | tf_op jit(solution)/shard_map/all_to_all | solution.py:742
  75.3 17.0 %all-to-all-start.1 = ((bf16[8,16,768]{2,1,0:T(8,128)(2,1)}), bf16[8,16,768]{2,1,0:T(8,128)(2,1)S(1)}, u32[]{:S(2)}, u32[]{:S(2)}) async-start(bf16[8,16,768]{2,1,0:T(8,128)(2,1)} %copy-done.11), calls=%async_computation.1 | async-start | bytes 393216 | tf_op jit(solution)/shard_map/all_to_all | solution.py:744
  83.9 41.0 %collective-permute-start.11 = (bf16[512,512]{1,0:T(8,128)(2,1)S(1)}, bf16[512,512]{1,0:T(8,128)(2,1)}, u32[]{:S(2)}, u32[]{:S(2)}) collective-permute-start(bf16[512,512]{1,0:T(8,128)(2,1)S(1)} %get-tuple-element.53.a_ref), channel_id=1, source_target_pairs={{0,1},{1,0},{2,3},{3,2},{4,5},{5,4},{6,7},{7,6},{8,9},{9,8},{10,11... | collective-permute-start | bytes 1572872 | tf_op jit(solution)/shard_map/ppermute | solution.py:712
  83.9 41.0 %collective-permute-start.13 = (bf16[512,512]{1,0:T(8,128)(2,1)S(1)}, bf16[512,512]{1,0:T(8,128)(2,1)}, u32[]{:S(2)}, u32[]{:S(2)}) collective-permute-start(bf16[512,512]{1,0:T(8,128)(2,1)S(1)} %collective-permute-done.12.c_ref), channel_id=1, source_target_pairs={{0,1},{1,0},{2,3},{3,2},{4,5},{5,4},{6,7},{7,6},{8,9},{9,8},{10,11... | collective-permute-start | bytes 1572872 | tf_op jit(solution)/shard_map/ppermute | solution.py:713
  98.0 2.3 %copy-start.14 = (f32[16,512]{1,0:T(8,128)}, f32[16,512]{1,0:T(8,128)S(1)}, u32[]{:S(2)}) copy-start(f32[16,512]{1,0:T(8,128)S(1)} %get-tuple-element.45.after_ref.error_ref) | copy-start | bytes 98308
  98.0 3.7 %collective-permute-start.10 = (bf16[64,512]{1,0:T(8,128)(2,1)S(1)}, bf16[64,512]{1,0:T(8,128)(2,1)S(1)}, u32[]{:S(2)}, u32[]{:S(2)}) collective-permute-start(bf16[64,512]{1,0:T(8,128)(2,1)S(1)} %get-tuple-element.44.a_ref), channel_id=1, source_target_pairs={{0,3},{1,2},{2,1},{3,0},{4,7},{5,6},{6,5},{7,4},{8,11},{9,10},{10,... | collective-permute-start | bytes 196616 | tf_op jit(solution)/shard_map/ppermute | solution.py:719
  98.0 3.7 %collective-permute-start.8 = (bf16[64,512]{1,0:T(8,128)(2,1)S(1)}, bf16[64,512]{1,0:T(8,128)(2,1)S(1)}, u32[]{:S(2)}, u32[]{:S(2)}) collective-permute-start(bf16[64,512]{1,0:T(8,128)(2,1)S(1)} %get-tuple-element.44.a_ref), channel_id=1, source_target_pairs={{0,1},{1,0},{2,3},{3,2},{4,5},{5,4},{6,7},{7,6},{8,9},{9,8},{10,11... | collective-permute-start | bytes 196616 | tf_op jit(solution)/shard_map/ppermute | solution.py:720
  98.1 5.1 %collective-permute-start.9 = (bf16[64,512]{1,0:T(8,128)(2,1)S(1)}, bf16[64,512]{1,0:T(8,128)(2,1)S(1)}, u32[]{:S(2)}, u32[]{:S(2)}) collective-permute-start(bf16[64,512]{1,0:T(8,128)(2,1)S(1)} %get-tuple-element.44.a_ref), channel_id=1, source_target_pairs={{0,2},{2,0},{1,3},{3,1},{4,6},{6,4},{5,7},{7,5},{8,10},{10,8},{9,1... | collective-permute-start | bytes 196616 | tf_op jit(solution)/shard_map/ppermute | solution.py:718
  100.2 3.0 %copy-start.15 = (f32[64,512]{1,0:T(8,128)S(1)}, f32[64,512]{1,0:T(8,128)}, u32[]{:S(2)}) copy-start(f32[64,512]{1,0:T(8,128)} %get-tuple-element.47.right_ref) | copy-start | bytes 393220
  100.2 3.0 %copy-start.20 = (f32[64,128]{1,0:T(8,128)S(1)}, f32[64,128]{1,0:T(8,128)}, u32[]{:S(2)}) copy-start(f32[64,128]{1,0:T(8,128)} %get-tuple-element.46.coef_ref) | copy-start | bytes 98308
  100.4 18.9 %copy-start.25 = (bf16[64,128]{1,0:T(8,128)(2,1)S(1)}, bf16[64,128]{1,0:T(8,128)(2,1)}, u32[]{:S(2)}) copy-start(bf16[64,128]{1,0:T(8,128)(2,1)} %copy-done.24) | copy-start | bytes 49156
  100.4 24.5 %copy-start.2 = (f32[512,128]{1,0:T(8,128)S(1)}, f32[512,128]{1,0:T(8,128)}, u32[]{:S(2)}) copy-start(f32[512,128]{1,0:T(8,128)} %get-tuple-element.35.coef_ref) | copy-start | bytes 786436
  105.2 15.0 %copy-start.16 = (f32[64,512]{1,0:T(8,128)}, f32[64,512]{1,0:T(8,128)S(1)}, u32[]{:S(2)}) copy-start(f32[64,512]{1,0:T(8,128)S(1)} %get-tuple-element.54.rows_ref) | copy-start | bytes 393220
  120.1 16.6 %all-to-all-start.3 = ((bf16[8,16,512]{2,1,0:T(8,128)(2,1)}), bf16[8,16,512]{2,1,0:T(8,128)(2,1)S(1)}, u32[]{:S(2)}, u32[]{:S(2)}) async-start(bf16[8,16,512]{2,1,0:T(8,128)(2,1)} %get-tuple-element.50), calls=%async_computation.3 | async-start | bytes 262144 | tf_op jit(solution)/shard_map/all_to_all | solution.py:753
  131.1 5.7 %copy-start.28 = (s32[16]{0:T(128)S(1)}, s32[16]{0:T(128)}, u32[]{:S(2)}) copy-start(s32[16]{0:T(128)} %index_ref.9) | copy-start | bytes 196
  131.1 5.7 %copy-start.31 = (bf16[32,128]{1,0:T(8,128)(2,1)S(1)}, bf16[32,128]{1,0:T(8,128)(2,1)}, u32[]{:S(2)}) copy-start(bf16[32,128]{1,0:T(8,128)(2,1)} %copy-done.30) | copy-start | bytes 24580
  (19 other events, 15.2 us)

commit v3 on v2

--- a/solution.py
+++ b/solution.py
@@ -25,25 +25,32 @@
     return jax.ShapeDtypeStruct(dims, dtype)
 
 
-def start_kernel(field_ref, middle_ref, top_ref, low_ref, last_ref, first_ref):
-    field = jnp.transpose(field_ref[...])
-    nodes = field.shape[0]
-    diffs = 2.0 * field - pltpu.roll(field, 1, 0) - pltpu.roll(field, nodes - 1, 0)
-    middle_ref[...] = diffs[EDGE : nodes - EDGE].astype(BF16)
-    top_ref[...] = field[: EDGE + 8]
-    low_ref[...] = field[nodes - EDGE - 8 :]
-    last_ref[...] = jnp.broadcast_to(field[nodes - 1 :], last_ref.shape)
-    first_ref[...] = jnp.broadcast_to(field[:1], first_ref.shape)
+def start_kernel(field_ref, middle_ref, top_ref, low_ref, last_ref, first_ref, rows_ref, sems):
+    modes, nodes = field_ref.shape
+    made = [
+        pltpu.make_async_copy(field_ref.at[pl.ds(j * LANES, LANES)], rows_ref.at[j], sems.at[j])
+        for j in range(modes // LANES)
+    ]
+    for copy in made:
+        copy.start()
+    for j, copy in enumerate(made):
+        copy.wait()
+        field = jnp.transpose(rows_ref[j])
+        lanes = slice(j * LANES, (j + 1) * LANES)
+        diffs = 2.0 * field - pltpu.roll(field, 1, 0) - pltpu.roll(field, nodes - 1, 0)
+        middle_ref[:, lanes] = diffs[EDGE : nodes - EDGE].astype(BF16)
+        top_ref[:, lanes] = field[: EDGE + 8]
+        low_ref[:, lanes] = field[nodes - EDGE - 8 :]
+        last_ref[:, lanes] = jnp.broadcast_to(field[nodes - 1 :], (8, LANES))
+        first_ref[:, lanes] = jnp.broadcast_to(field[:1], (8, LANES))
 
 
 def start(field):
     modes, nodes = field.shape
-    column = lambda rows: pl.BlockSpec((rows, LANES), lambda j: (0, j))
     return pl.pallas_call(
         start_kernel,
-        grid=(modes // LANES,),
-        in_specs=[pl.BlockSpec((LANES, nodes), lambda j: (j, 0))],
-        out_specs=[column(nodes - 2 * EDGE), column(EDGE + 8), column(EDGE + 8), column(8), column(8)],
+        in_specs=[pl.BlockSpec(memory_space=pltpu.HBM)],
+        out_specs=[VMEM] * 5,
         out_shape=[
             shape((nodes - 2 * EDGE, modes), BF16),
             shape((EDGE + 8, modes)),
@@ -51,6 +58,11 @@
             shape((8, modes)),
             shape((8, modes)),
         ],
+        scratch_shapes=[
+            pltpu.VMEM((modes // LANES, LANES, nodes), F32),
+            pltpu.SemaphoreType.DMA((modes // LANES,)),
+        ],
+        compiler_params=params(63600),
         name="start",
     )(field)
 
@@ -424,32 +436,20 @@
     return jnp.concatenate(two_terms(weights), axis=0).astype(BF16)
 
 
-def plane_kernel(p_ref, feeds_ref, out_ref, inside_ref, weights_ref, carry_ref):
+def plane_kernel(feeds_ref, out_ref, weights_ref):
     plane, coarse, width = feeds_ref.shape
     modes = width - 2 * LANES
-    p = p_ref[0]
     row, lane = lanes_and_rows(coarse)
     one = (row == lane).astype(F32)
-    none = jnp.zeros_like(one)
-    whole, before = one, none
-    wholes, befores = [], []
+    whole, wholes = one, []
     for q in range(plane - 1, -1, -1):
-        step = step_of(feeds_ref[q, :, modes : modes + LANES], coarse)
-        before = jnp.where(q == p - 1, one, before)
         wholes.append(whole)
-        befores.append(before)
-        whole = advance(whole, step, none)
-        before = advance(before, step, none)
-    carry_ref[...] = jnp.where(p == 0, one, before)
-    totals, excluding = side_by_side(wholes[::-1]), side_by_side(befores[::-1])
-    own = step_of(feeds_ref[p, :, modes : modes + LANES], coarse)
-    including = advance(own, excluding, (lane == p * coarse + row).astype(F32))
-    totals = terms_of(totals)
-    weights_ref[...] = jnp.concatenate([totals, terms_of(including)], axis=0)
+        whole = advance(whole, step_of(feeds_ref[q, :, modes : modes + LANES], coarse), jnp.zeros_like(one))
+    totals = terms_of(side_by_side(wholes[::-1]))
+    weights_ref[...] = totals
     feeds = feeds_ref[:, :, :modes].reshape(plane * coarse, modes)
-    sums = jnp.dot(jnp.concatenate([totals, terms_of(excluding)], axis=0), feeds, preferred_element_type=F32)
-    state = sums[:coarse] + sums[coarse : 2 * coarse]
-    inside_ref[...] = sums[2 * coarse : 3 * coarse] + sums[3 * coarse :]
+    sums = jnp.dot(totals, feeds, preferred_element_type=F32)
+    state = sums[:coarse] + sums[coarse:]
     matrix = jnp.where(lane < coarse, whole, 0.0)
     high, low = two_terms(matrix)
     first = feeds_ref[0, :, modes : modes + LANES].astype(F32)
@@ -467,21 +467,56 @@
         out_ref[z] = sent
 
 
-def plane_totals(p, feeds, planes):
+def plane_totals(feeds, planes):
     plane, coarse, width = feeds.shape
     return pl.pallas_call(
         plane_kernel,
-        in_specs=[SMEM, VMEM],
-        out_specs=[VMEM] * 4,
+        in_specs=[VMEM],
+        out_specs=[VMEM] * 2,
         out_shape=[
             shape((planes, coarse, width), BF16),
+            shape((2 * coarse, plane * coarse), BF16),
+        ],
+        compiler_params=params(52000),
+        name="plane_totals",
+    )(feeds)
+
+
+def inside_kernel(p_ref, feeds_ref, totals_ref, inside_ref, weights_ref, carry_ref):
+    plane, coarse, width = feeds_ref.shape
+    modes = width - 2 * LANES
+    p = p_ref[0]
+    row, lane = lanes_and_rows(coarse)
+    one = (row == lane).astype(F32)
+    before, befores = jnp.zeros_like(one), []
+    for q in range(plane - 1, -1, -1):
+        before = jnp.where(q == p - 1, one, before)
+        befores.append(before)
+        before = advance(before, step_of(feeds_ref[q, :, modes : modes + LANES], coarse), jnp.zeros_like(one))
+    carry_ref[...] = jnp.where(p == 0, one, before)
+    excluding = side_by_side(befores[::-1])
+    own = step_of(feeds_ref[p, :, modes : modes + LANES], coarse)
+    including = advance(own, excluding, (lane == p * coarse + row).astype(F32))
+    weights_ref[...] = jnp.concatenate([totals_ref[...], terms_of(including)], axis=0)
+    feeds = feeds_ref[:, :, :modes].reshape(plane * coarse, modes)
+    sums = jnp.dot(terms_of(excluding), feeds, preferred_element_type=F32)
+    inside_ref[...] = sums[:coarse] + sums[coarse:]
+
+
+def inside_plane(p, feeds, totals):
+    plane, coarse, width = feeds.shape
+    return pl.pallas_call(
+        inside_kernel,
+        in_specs=[SMEM, VMEM, VMEM],
+        out_specs=[VMEM] * 3,
+        out_shape=[
             shape((coarse, width - 2 * LANES)),
             shape((4 * coarse, plane * coarse), BF16),
             shape((coarse, LANES)),
         ],
         compiler_params=params(52000),
-        name="plane_totals",
-    )(p, feeds)
+        name="inside_plane",
+    )(p, feeds, totals)
 
 
 def second_plane_kernel(feeds_ref, weights_ref, out_ref, inside_ref):
@@ -740,7 +775,8 @@
     )
     parts = over_modes(diffs)
     feeds = lax.all_to_all(message, PLANE, 0, 0, tiled=True)
-    totals, inside, weights, carry = plane_totals(p, feeds, planes)
+    totals, weights = plane_totals(feeds, planes)
+    inside, weights, carry = inside_plane(p, feeds, weights)
     totals = lax.all_to_all(totals, "z", 0, 0, tiled=True)
     rows, error, plane_weights = correct(z, p, coarse_index, feeds, totals, inside, carry, near, nodes)
     rows = over_modes_directly(rows)

time: 141 us -> 137 us (0.972)
  blocking collectives: 14.1 us -> 31.7 us
  waiting for transfers between devices: 32.7 us -> 20.8 us
  starting transfers between devices: 40.2 us -> 31.1 us
    all_to_all x0 -> x1, blocking collectives: none -> 17.5 us  [shards(): feeds = lax.all_to_all(message, PLANE, 0, 0, tiled=True)]
    all_to_all x1 -> x0, starting transfers between devices: 9.14 us -> none  [shards(): feeds = lax.all_to_all(message, PLANE, 0, 0, tiled=True)]
    all_to_all x1 -> x0, waiting for transfers between devices: 8.37 us -> none  [shards(): feeds = lax.all_to_all(message, PLANE, 0, 0, tiled=True)]
    all_to_all x1, waiting for transfers between devices: 7.9 us -> 4.37 us  [shards(): totals = lax.all_to_all(totals, 'z', 0, 0, tiled=True)]
    pallas_call x2 -> x3, Pallas kernels: 5.15 us -> 4.44 us  [the longest x1 2.39 us: start(): pl.pallas_call(start_kernel, in_specs=[pl.BlockSpec(memory_space=pltpu.HB...]
    unnamed x68 -> x72, local copies, waits for them, and re-layouts: 15.2 us -> 15.9 us
  transfers between devices with their start and end apart: 17 -> 16, of which waited for: 6 -> 5; matrix products, arithmetic and copies ran while one was open for 0% -> 0% of each run, Pallas kernels for 16% -> 17%
where the time goes in v3:
time: 137 us; the launch traced here: 136 us
  Pallas kernels  35.5 us (26%)
  blocking collectives  31.7 us (23%)
  starting transfers between devices  31.1 us (23%)
  waiting for transfers between devices  20.8 us (15%)
  local copies, waits for them, and re-layouts  15.9 us (12%)
    all_to_all x1, blocking collectives, shards(): feeds = lax.all_to_all(message, PLANE, 0, 0, tiled=True)  17.5 us
    unnamed x72, local copies, waits for them, and re-layouts  15.9 us
    all_to_all x1, blocking collectives, shards(): later = lax.all_to_all(message, PLANE, 0, 0, tiled=True)  14.1 us
    ppermute x2, waiting for transfers between devices, over_modes(): across = lax.ppermute(own, 'yl', swap)  11.6 us
    all_to_all x1, starting transfers between devices, shards(): totals = lax.all_to_all(totals, 'z', 0, 0, tiled=True)  8.57 us
    pallas_call x1, Pallas kernels, first_update(): pl.pallas_call(first_kernel, in_specs=[SMEM] * 3 + [ANY] * 9 + [VMEM] + [...  7.42 us
    pallas_call x1, Pallas kernels, bulk(): pl.pallas_call(bulk_kernel, in_specs=[SMEM, SMEM] + [ANY] * 5 + [VMEM], o...  6.15 us
    pallas_call x1, Pallas kernels, last_local(): pl.pallas_call(last_local_kernel, grid=(modes // LANES,), in_specs=[SMEM,...  5.63 us
  transfers between devices with their start and end apart: 16, of which 5 were waited for; matrix products, arithmetic and copies ran while one was open for 0% of the time, Pallas kernels for 17%

profile of v3, /device:TPU:32, one launch (start us, length us, event | category | flops | bytes accessed | tf_op | source)
XLA Modules:
  0.0 136.0 jit_solution(13136446975260198521)
XLA Ops:
  0.7 2.4 %start.1 = (bf16[480,512]{1,0:T(8,128)(2,1)}, f32[24,512]{1,0:T(8,128)}, f32[24,512]{1,0:T(8,128)}, f32[8,512]{1,0:T(8,128)}, f32[8,512]{1,0:T(8,128)}) custom-call(f32[512,512]{1,0:T(8,128)} %field_ref.3), custom_call_target="tpu_custom_call" | custom-call | tf_op jit(solution)/shard_map/start/pallas_call | solution.py:50
  3.1 1.7 %collective-permute-start.1 = (bf16[480,512]{1,0:T(8,128)(2,1)}, bf16[480,512]{1,0:T(8,128)(2,1)S(1)}, u32[]{:S(2)}, u32[]{:S(2)}) collective-permute-start(bf16[480,512]{1,0:T(8,128)(2,1)} %get-tuple-element.31.a_ref), channel_id=1, source_target_pairs={{0,2},{2,0},{1,3},{3,1},{4,6},{6,4},{5,7},{7,5},{8,10},{10,8},{9,1... | collective-permute-start | bytes 1474568 | tf_op jit(solution)/shard_map/ppermute | solution.py:746
  4.8 11.6 %collective-permute-done.1.c_ref = bf16[480,512]{1,0:T(8,128)(2,1)S(1)} collective-permute-done((bf16[480,512]{1,0:T(8,128)(2,1)}, bf16[480,512]{1,0:T(8,128)(2,1)S(1)}, u32[]{:S(2)}, u32[]{:S(2)}) %collective-permute-start.1) | collective-permute-done | bytes 491552 | tf_op jit(solution)/shard_map/ppermute | solution.py:746
  16.3 5.1 %collective-permute-start.3 = (f32[8,512]{1,0:T(8,128)}, f32[8,512]{1,0:T(8,128)S(1)}, u32[]{:S(2)}, u32[]{:S(2)}) collective-permute-start(f32[8,512]{1,0:T(8,128)} %get-tuple-element.34), channel_id=1, source_target_pairs={{0,4},{4,8},{8,12},{12,16},{16,20},{20,24},{24,28},{28,32},{32,36}... | collective-permute-start | bytes 49160 | tf_op jit(solution)/shard_map/ppermute | solution.py:739
  21.4 5.3 %collective-permute-start.4 = (f32[8,512]{1,0:T(8,128)}, f32[8,512]{1,0:T(8,128)S(1)}, u32[]{:S(2)}, u32[]{:S(2)}) collective-permute-start(f32[8,512]{1,0:T(8,128)} %get-tuple-element.35), channel_id=1, source_target_pairs={{4,0},{8,4},{12,8},{16,12},{20,16},{24,20},{28,24},{32,28},{36,32}... | collective-permute-start | bytes 49160 | tf_op jit(solution)/shard_map/ppermute | solution.py:740
  26.7 2.1 %collective-permute-done.4.right_ref = f32[8,512]{1,0:T(8,128)S(1)} collective-permute-done((f32[8,512]{1,0:T(8,128)}, f32[8,512]{1,0:T(8,128)S(1)}, u32[]{:S(2)}, u32[]{:S(2)}) %collective-permute-start.4) | collective-permute-done | bytes 16416 | tf_op jit(solution)/shard_map/ppermute | solution.py:740
  30.5 1.2 collective-permute-start.6
  32.4 4.6 %prepare.1 = (f32[512,512]{1,0:T(8,128)}, bf16[512,512]{1,0:T(8,128)(2,1)}, f32[512,512]{1,0:T(8,128)}, f32[512,128]{1,0:T(8,128)}, f32[64,512]{1,0:T(8,128)}, /*index=5*/f32[64,128]{1,0:T(8,128)}) custom-call(s32[16]{0:T(128)} %index_ref.9, f32[512,512]{1,0:T(8,128)} %right_ref.1, bf16[512,512]{1,0:T(8,128)(2,1)} %inverse_ref.3, f32[512,512]{1,0:T(8,128)} %field_ref.3, ...), custom_call_target="tpu_custom_call" | custom-call | tf_op jit(solution)/shard_map/prepare/pallas_call | solution.py:119
  38.6 0.9 copy-done.1
  39.6 1.0 copy-done.6
  40.6 1.0 copy-done.8
  41.7 1.0 copy-done.10
  42.7 7.4 %first_update.1 = (bf16[8,16,768]{2,1,0:T(8,128)(2,1)S(1)}, f32[512,512]{1,0:T(8,128)}, bf16[512,512]{1,0:T(8,128)(2,1)S(1)}, f32[96,512]{1,0:T(8,128)S(1)}) custom-call(s32[1]{0:T(128)} %bitcast.me_ref, s32[4,4,16]{2,1,0:T(4,128)S(1)} %bitcast.4, s32[16]{0:T(128)S(1)} %copy-done.26, bf16[480,512]{1,0:T(8,128)(2,1)S(1)} %copy-done.4, ...), custom_call_target="tpu_custom_call" | custom-call | tf_op jit(solution)/shard_map/first_update/pallas_call | solution.py:379
  50.1 1.2 collective-permute-start.12
  51.3 17.5 %all_to_all.20.feeds_ref = bf16[8,16,768]{2,1,0:T(8,128)(2,1)S(1)} all-to-all(bf16[8,16,768]{2,1,0:T(8,128)(2,1)S(1)} %get-tuple-element.40), channel_id=1, replica_groups=mesh['z'=8,'x'=4,'yh'=2,'yl'=2,'core'=2] {'x','yh'}, dimensions={0} | all-to-all | bytes 393216 | tf_op jit(solution)/shard_map/all_to_all | solution.py:777
  68.8 1.0 plane_totals.1
  71.2 8.6 %all-to-all-start.1 = ((bf16[8,16,768]{2,1,0:T(8,128)(2,1)}), bf16[8,16,768]{2,1,0:T(8,128)(2,1)S(1)}, u32[]{:S(2)}, u32[]{:S(2)}) async-start(bf16[8,16,768]{2,1,0:T(8,128)(2,1)} %copy-done.11), calls=%async_computation.1 | async-start | bytes 393216 | tf_op jit(solution)/shard_map/all_to_all | solution.py:780
  80.9 1.0 inside_plane.1
  83.8 4.4 %all-to-all-done.1.totals_ref = bf16[8,16,768]{2,1,0:T(8,128)(2,1)S(1)} async-done(((bf16[8,16,768]{2,1,0:T(8,128)(2,1)}), bf16[8,16,768]{2,1,0:T(8,128)(2,1)S(1)}, u32[]{:S(2)}, u32[]{:S(2)}) %all-to-all-start.1) | async-done | bytes 196640 | tf_op jit(solution)/shard_map/all_to_all | solution.py:780
  88.1 0.9 copy-done.13
  91.2 2.1 %correct.1 = (bf16[64,512]{1,0:T(8,128)(2,1)S(1)}, f32[16,512]{1,0:T(8,128)S(1)}, bf16[32,128]{1,0:T(8,128)(2,1)S(1)}) custom-call(s32[1]{0:T(128)} %bitcast.2.z_ref, s32[1]{0:T(128)} %bitcast.3.p_ref, s32[16]{0:T(128)S(1)} %copy-done.27, bf16[8,16,768]{2,1,0:T(8,128)(2,1)S(1)} %all_to_all.20.feeds_ref, bf16[8,16,768]{2,1,0:T(8,128)(2,1)S(1)} %all-to-all-done.1.totals_ref, ...), custom_call_target="tpu_custom_call" | custom-call | tf_op jit(solution)/shard_map/correct/pallas_call | solution.py:604
  93.9 2.1 %collective-permute-start.9 = (bf16[64,512]{1,0:T(8,128)(2,1)S(1)}, bf16[64,512]{1,0:T(8,128)(2,1)S(1)}, u32[]{:S(2)}, u32[]{:S(2)}) collective-permute-start(bf16[64,512]{1,0:T(8,128)(2,1)S(1)} %get-tuple-element.46.a_ref), channel_id=1, source_target_pairs={{0,2},{2,0},{1,3},{3,1},{4,6},{6,4},{5,7},{7,5},{8,10},{10,8},{9,1... | collective-permute-start | bytes 196616 | tf_op jit(solution)/shard_map/ppermute | solution.py:753
  96.3 1.3 collective-permute-done.10.d_ref
  97.6 1.4 %collective-permute-done.9.c_ref = bf16[64,512]{1,0:T(8,128)(2,1)S(1)} collective-permute-done((bf16[64,512]{1,0:T(8,128)(2,1)S(1)}, bf16[64,512]{1,0:T(8,128)(2,1)S(1)}, u32[]{:S(2)}, u32[]{:S(2)}) %collective-permute-start.9) | collective-permute-done | bytes 65568 | tf_op jit(solution)/shard_map/ppermute | solution.py:753
  99.0 2.0 %redo.1 = (bf16[8,16,512]{2,1,0:T(8,128)(2,1)S(1)}, f32[64,512]{1,0:T(8,128)S(1)}) custom-call(s32[1]{0:T(128)} %bitcast.me_ref, s32[4,4,16]{2,1,0:T(4,128)S(1)} %bitcast.5, bf16[64,512]{1,0:T(8,128)(2,1)S(1)} %get-tuple-element.46.a_ref, bf16[64,512]{1,0:T(8,128)(2,1)S(1)} %collective-permute-done.8.b_ref, ...), custom_call_target="tpu_custom_call" | custom-call | tf_op jit(solution)/shard_map/redo/pallas_call | solution.py:639
  101.0 14.1 %all_to_all.21.feeds_ref = bf16[8,16,512]{2,1,0:T(8,128)(2,1)S(1)} all-to-all(bf16[8,16,512]{2,1,0:T(8,128)(2,1)S(1)} %get-tuple-element.50), channel_id=1, replica_groups=mesh['z'=8,'x'=4,'yh'=2,'yl'=2,'core'=2] {'x','yh'}, dimensions={0} | all-to-all | bytes 262144 | tf_op jit(solution)/shard_map/all_to_all | solution.py:786
  115.2 0.8 second_plane_totals.1
  116.0 4.7 %all-to-all-start.3 = ((bf16[8,16,512]{2,1,0:T(8,128)(2,1)}), bf16[8,16,512]{2,1,0:T(8,128)(2,1)S(1)}, u32[]{:S(2)}, u32[]{:S(2)}) async-start(bf16[8,16,512]{2,1,0:T(8,128)(2,1)} %get-tuple-element.52), calls=%async_computation.3 | async-start | bytes 262144 | tf_op jit(solution)/shard_map/all_to_all | solution.py:789
  120.8 6.1 %whole.1.op_ref = f32[512,512]{1,0:T(8,128)} custom-call(s32[1]{0:T(128)} %bitcast.me_ref, s32[4,4,16]{2,1,0:T(4,128)S(1)} %bitcast.6, bf16[512,512]{1,0:T(8,128)(2,1)S(1)} %get-tuple-element.55.a_ref, bf16[512,512]{1,0:T(8,128)(2,1)} %collective-permute-done.11.b_ref, bf16[512,512]{1,0:T(8,128)(2,1)S(1)} %collective-permute-done.12.c_ref, ...), custom_call_target="tpu_custom_call" | custom-call | tf_op jit(solution)/shard_map/whole/pallas_call | solution.py:240
  126.9 5.6 %last_local.1 = (f32[512,512]{1,0:T(8,128)}, f32[512,512]{1,0:T(8,128)}) custom-call(s32[16]{0:T(128)} %index_ref.9, f32[512,512]{1,0:T(8,128)} %whole.1.op_ref, f32[512,512]{1,0:T(8,128)} %get-tuple-element.37.right_ref, f32[64,512]{1,0:T(8,128)} %copy-done.16, bf16[512,512]{1,0:T(8,128)(2,1)} %get-tuple-element.38.sub_ref, ...), custom_call_target="tpu_custom_call" | custom-call | tf_op jit(solution)/shard_map/last_local/pallas_call | solution.py:671
  132.6 1.2 copy-done.3
  133.8 2.0 %last.1 = f32[512,512]{1,0:T(8,128)} custom-call(s32[16]{0:T(128)S(1)} %copy-done.28, bf16[8,16,512]{2,1,0:T(8,128)(2,1)S(1)} %all-to-all-done.3.totals_ref, f32[16,512]{1,0:T(8,128)S(1)} %get-tuple-element.53.inside_ref, bf16[32,128]{1,0:T(8,128)(2,1)S(1)} %copy-done.31, f32[512,512]{1,0:T(8,128)S(1)} %copy-done.3), custom_call_target="tpu_custom_call" | custom-call | tf_op jit(solution)/shard_map/last/pallas_call | solution.py:721
  (87 shorter events, 11.2 us)
Async XLA Ops:
  0.6 38.0 %copy-start.26 = (s32[16]{0:T(128)S(1)}, s32[16]{0:T(128)}, u32[]{:S(2)}) copy-start(s32[16]{0:T(128)} %index_ref.9) | copy-start | bytes 196
  0.6 38.0 %copy-start.17 = (s32[4,16,4]{1,2,0:T(4,128)S(1)}, s32[4,16,4]{1,2,0:T(4,128)}, u32[]{:S(2)}) copy-start(s32[4,16,4]{1,2,0:T(4,128)} %param.13) | copy-start | bytes 3076
  0.7 38.0 %copy-start.21 = (f32[16,16]{1,0:T(8,128)S(1)}, f32[16,16]{1,0:T(8,128)}, u32[]{:S(2)}) copy-start(f32[16,16]{1,0:T(8,128)} %inverse_ref.5) | copy-start | bytes 3076
  0.7 38.0 %copy-start.29 = (f32[16,16]{1,0:T(8,128)S(1)}, f32[16,16]{1,0:T(8,128)}, u32[]{:S(2)}) copy-start(f32[16,16]{1,0:T(8,128)} %coupling_ref.1) | copy-start | bytes 3076
  3.1 35.6 %copy-start.4 = (bf16[480,512]{1,0:T(8,128)(2,1)S(1)}, bf16[480,512]{1,0:T(8,128)(2,1)}, u32[]{:S(2)}) copy-start(bf16[480,512]{1,0:T(8,128)(2,1)} %get-tuple-element.31.a_ref) | copy-start | bytes 1474564
  3.1 13.3 %collective-permute-start.1 = (bf16[480,512]{1,0:T(8,128)(2,1)}, bf16[480,512]{1,0:T(8,128)(2,1)S(1)}, u32[]{:S(2)}, u32[]{:S(2)}) collective-permute-start(bf16[480,512]{1,0:T(8,128)(2,1)} %get-tuple-element.31.a_ref), channel_id=1, source_target_pairs={{0,2},{2,0},{1,3},{3,1},{4,6},{6,4},{5,7},{7,5},{8,10},{10,8},{9,1... | collective-permute-start | bytes 1474568 | tf_op jit(solution)/shard_map/ppermute | solution.py:746
  4.7 32.3 %collective-permute-start = (bf16[480,512]{1,0:T(8,128)(2,1)}, bf16[480,512]{1,0:T(8,128)(2,1)S(1)}, u32[]{:S(2)}, u32[]{:S(2)}) collective-permute-start(bf16[480,512]{1,0:T(8,128)(2,1)} %get-tuple-element.31.a_ref), channel_id=1, source_target_pairs={{0,1},{1,0},{2,3},{3,2},{4,5},{5,4},{6,7},{7,6},{8,9},{9,8},{10,11... | collective-permute-start | bytes 1474568 | tf_op jit(solution)/shard_map/ppermute | solution.py:747
  16.3 22.3 %copy-start.5 = (bf16[480,512]{1,0:T(8,128)(2,1)}, bf16[480,512]{1,0:T(8,128)(2,1)S(1)}, u32[]{:S(2)}) copy-start(bf16[480,512]{1,0:T(8,128)(2,1)S(1)} %collective-permute-done.1.c_ref) | copy-start | bytes 1474564
  16.3 21.5 %collective-permute-start.2 = (bf16[480,512]{1,0:T(8,128)(2,1)S(1)}, bf16[480,512]{1,0:T(8,128)(2,1)S(1)}, u32[]{:S(2)}, u32[]{:S(2)}) collective-permute-start(bf16[480,512]{1,0:T(8,128)(2,1)S(1)} %collective-permute-done.1.c_ref), channel_id=1, source_target_pairs={{0,1},{1,0},{2,3},{3,2},{4,5},{5,4},{6,7},{7,6},{8,9},{9,8},{10,11... | collective-permute-start | bytes 1474568 | tf_op jit(solution)/shard_map/ppermute | solution.py:748
  16.3 10.4 %collective-permute-start.3 = (f32[8,512]{1,0:T(8,128)}, f32[8,512]{1,0:T(8,128)S(1)}, u32[]{:S(2)}, u32[]{:S(2)}) collective-permute-start(f32[8,512]{1,0:T(8,128)} %get-tuple-element.34), channel_id=1, source_target_pairs={{0,4},{4,8},{8,12},{12,16},{16,20},{20,24},{24,28},{28,32},{32,36}... | collective-permute-start | bytes 49160 | tf_op jit(solution)/shard_map/ppermute | solution.py:739
  21.4 7.3 %collective-permute-start.4 = (f32[8,512]{1,0:T(8,128)}, f32[8,512]{1,0:T(8,128)S(1)}, u32[]{:S(2)}, u32[]{:S(2)}) collective-permute-start(f32[8,512]{1,0:T(8,128)} %get-tuple-element.35), channel_id=1, source_target_pairs={{4,0},{8,4},{12,8},{16,12},{20,16},{24,20},{28,24},{32,28},{36,32}... | collective-permute-start | bytes 49160 | tf_op jit(solution)/shard_map/ppermute | solution.py:740
  30.4 6.6 %collective-permute-start.5 = (bf16[32,512]{1,0:T(8,128)(2,1)S(1)}, bf16[32,512]{1,0:T(8,128)(2,1)S(1)}, u32[]{:S(2)}, u32[]{:S(2)}) collective-permute-start(bf16[32,512]{1,0:T(8,128)(2,1)S(1)} %edges.1.ea_ref), channel_id=1, source_target_pairs={{0,1},{1,0},{2,3},{3,2},{4,5},{5,4},{6,7},{7,6},{8,9},{9,8},{10,11... | collective-permute-start | bytes 98312 | tf_op jit(solution)/shard_map/ppermute | solution.py:755
  30.5 6.5 %collective-permute-start.6 = (bf16[32,512]{1,0:T(8,128)(2,1)S(1)}, bf16[32,512]{1,0:T(8,128)(2,1)S(1)}, u32[]{:S(2)}, u32[]{:S(2)}) collective-permute-start(bf16[32,512]{1,0:T(8,128)(2,1)S(1)} %edges.1.ea_ref), channel_id=1, source_target_pairs={{0,2},{2,0},{1,3},{3,1},{4,6},{6,4},{5,7},{7,5},{8,10},{10,8},{9,1... | collective-permute-start | bytes 98312 | tf_op jit(solution)/shard_map/ppermute | solution.py:753
  31.7 5.3 %collective-permute-start.7 = (bf16[32,512]{1,0:T(8,128)(2,1)S(1)}, bf16[32,512]{1,0:T(8,128)(2,1)S(1)}, u32[]{:S(2)}, u32[]{:S(2)}) collective-permute-start(bf16[32,512]{1,0:T(8,128)(2,1)S(1)} %edges.1.ea_ref), channel_id=1, source_target_pairs={{0,3},{1,2},{2,1},{3,0},{4,7},{5,6},{6,5},{7,4},{8,11},{9,10},{10,... | collective-permute-start | bytes 98312 | tf_op jit(solution)/shard_map/ppermute | solution.py:754
  42.7 53.4 %copy-start = (bf16[4,4,4,128,128]{4,3,2,1,0:T(8,128)(2,1)S(1)}, bf16[4,4,4,128,128]{4,3,2,1,0:T(8,128)(2,1)}, u32[]{:S(2)}) copy-start(bf16[4,4,4,128,128]{4,3,2,1,0:T(8,128)(2,1)} %g_hbm.3) | copy-start | bytes 6291460
  50.1 19.8 %copy-start.12 = (f32[96,512]{1,0:T(8,128)}, f32[96,512]{1,0:T(8,128)S(1)}, u32[]{:S(2)}) copy-start(f32[96,512]{1,0:T(8,128)S(1)} %get-tuple-element.45.around_ref) | copy-start | bytes 589828
  50.1 29.6 %collective-permute-start.12 = (bf16[512,512]{1,0:T(8,128)(2,1)S(1)}, bf16[512,512]{1,0:T(8,128)(2,1)S(1)}, u32[]{:S(2)}, u32[]{:S(2)}) collective-permute-start(bf16[512,512]{1,0:T(8,128)(2,1)S(1)} %get-tuple-element.55.a_ref), channel_id=1, source_target_pairs={{0,2},{2,0},{1,3},{3,1},{4,6},{6,4},{5,7},{7,5},{8,10},{10,8},{9,1... | collective-permute-start | bytes 1572872 | tf_op jit(solution)/shard_map/ppermute | solution.py:746
  71.2 17.0 %all-to-all-start.1 = ((bf16[8,16,768]{2,1,0:T(8,128)(2,1)}), bf16[8,16,768]{2,1,0:T(8,128)(2,1)S(1)}, u32[]{:S(2)}, u32[]{:S(2)}) async-start(bf16[8,16,768]{2,1,0:T(8,128)(2,1)} %copy-done.11), calls=%async_computation.1 | async-start | bytes 393216 | tf_op jit(solution)/shard_map/all_to_all | solution.py:780
  79.7 41.0 %collective-permute-start.11 = (bf16[512,512]{1,0:T(8,128)(2,1)S(1)}, bf16[512,512]{1,0:T(8,128)(2,1)}, u32[]{:S(2)}, u32[]{:S(2)}) collective-permute-start(bf16[512,512]{1,0:T(8,128)(2,1)S(1)} %get-tuple-element.55.a_ref), channel_id=1, source_target_pairs={{0,1},{1,0},{2,3},{3,2},{4,5},{5,4},{6,7},{7,6},{8,9},{9,8},{10,11... | collective-permute-start | bytes 1572872 | tf_op jit(solution)/shard_map/ppermute | solution.py:747
  79.7 41.0 %collective-permute-start.13 = (bf16[512,512]{1,0:T(8,128)(2,1)S(1)}, bf16[512,512]{1,0:T(8,128)(2,1)}, u32[]{:S(2)}, u32[]{:S(2)}) collective-permute-start(bf16[512,512]{1,0:T(8,128)(2,1)S(1)} %collective-permute-done.12.c_ref), channel_id=1, source_target_pairs={{0,1},{1,0},{2,3},{3,2},{4,5},{5,4},{6,7},{7,6},{8,9},{9,8},{10,11... | collective-permute-start | bytes 1572872 | tf_op jit(solution)/shard_map/ppermute | solution.py:748
  93.9 2.3 %copy-start.14 = (f32[16,512]{1,0:T(8,128)}, f32[16,512]{1,0:T(8,128)S(1)}, u32[]{:S(2)}) copy-start(f32[16,512]{1,0:T(8,128)S(1)} %get-tuple-element.47.after_ref.error_ref) | copy-start | bytes 98308
  93.9 3.7 %collective-permute-start.10 = (bf16[64,512]{1,0:T(8,128)(2,1)S(1)}, bf16[64,512]{1,0:T(8,128)(2,1)S(1)}, u32[]{:S(2)}, u32[]{:S(2)}) collective-permute-start(bf16[64,512]{1,0:T(8,128)(2,1)S(1)} %get-tuple-element.46.a_ref), channel_id=1, source_target_pairs={{0,3},{1,2},{2,1},{3,0},{4,7},{5,6},{6,5},{7,4},{8,11},{9,10},{10,... | collective-permute-start | bytes 196616 | tf_op jit(solution)/shard_map/ppermute | solution.py:754
  93.9 3.7 %collective-permute-start.8 = (bf16[64,512]{1,0:T(8,128)(2,1)S(1)}, bf16[64,512]{1,0:T(8,128)(2,1)S(1)}, u32[]{:S(2)}, u32[]{:S(2)}) collective-permute-start(bf16[64,512]{1,0:T(8,128)(2,1)S(1)} %get-tuple-element.46.a_ref), channel_id=1, source_target_pairs={{0,1},{1,0},{2,3},{3,2},{4,5},{5,4},{6,7},{7,6},{8,9},{9,8},{10,11... | collective-permute-start | bytes 196616 | tf_op jit(solution)/shard_map/ppermute | solution.py:755
  93.9 5.1 %collective-permute-start.9 = (bf16[64,512]{1,0:T(8,128)(2,1)S(1)}, bf16[64,512]{1,0:T(8,128)(2,1)S(1)}, u32[]{:S(2)}, u32[]{:S(2)}) collective-permute-start(bf16[64,512]{1,0:T(8,128)(2,1)S(1)} %get-tuple-element.46.a_ref), channel_id=1, source_target_pairs={{0,2},{2,0},{1,3},{3,1},{4,6},{6,4},{5,7},{7,5},{8,10},{10,8},{9,1... | collective-permute-start | bytes 196616 | tf_op jit(solution)/shard_map/ppermute | solution.py:753
  96.0 2.9 %copy-start.15 = (f32[64,512]{1,0:T(8,128)S(1)}, f32[64,512]{1,0:T(8,128)}, u32[]{:S(2)}) copy-start(f32[64,512]{1,0:T(8,128)} %get-tuple-element.49.right_ref) | copy-start | bytes 393220
  96.0 2.9 %copy-start.20 = (f32[64,128]{1,0:T(8,128)S(1)}, f32[64,128]{1,0:T(8,128)}, u32[]{:S(2)}) copy-start(f32[64,128]{1,0:T(8,128)} %get-tuple-element.48.coef_ref) | copy-start | bytes 98308
  96.2 18.9 %copy-start.25 = (bf16[64,128]{1,0:T(8,128)(2,1)S(1)}, bf16[64,128]{1,0:T(8,128)(2,1)}, u32[]{:S(2)}) copy-start(bf16[64,128]{1,0:T(8,128)(2,1)} %copy-done.24) | copy-start | bytes 49156
  96.3 24.5 %copy-start.2 = (f32[512,128]{1,0:T(8,128)S(1)}, f32[512,128]{1,0:T(8,128)}, u32[]{:S(2)}) copy-start(f32[512,128]{1,0:T(8,128)} %get-tuple-element.36.coef_ref) | copy-start | bytes 786436
  101.0 15.0 %copy-start.16 = (f32[64,512]{1,0:T(8,128)}, f32[64,512]{1,0:T(8,128)S(1)}, u32[]{:S(2)}) copy-start(f32[64,512]{1,0:T(8,128)S(1)} %get-tuple-element.56.rows_ref) | copy-start | bytes 393220
  116.0 16.6 %all-to-all-start.3 = ((bf16[8,16,512]{2,1,0:T(8,128)(2,1)}), bf16[8,16,512]{2,1,0:T(8,128)(2,1)S(1)}, u32[]{:S(2)}, u32[]{:S(2)}) async-start(bf16[8,16,512]{2,1,0:T(8,128)(2,1)} %get-tuple-element.52), calls=%async_computation.3 | async-start | bytes 262144 | tf_op jit(solution)/shard_map/all_to_all | solution.py:789
  126.9 5.7 %copy-start.28 = (s32[16]{0:T(128)S(1)}, s32[16]{0:T(128)}, u32[]{:S(2)}) copy-start(s32[16]{0:T(128)} %index_ref.9) | copy-start | bytes 196
  126.9 5.7 %copy-start.31 = (bf16[32,128]{1,0:T(8,128)(2,1)S(1)}, bf16[32,128]{1,0:T(8,128)(2,1)}, u32[]{:S(2)}) copy-start(bf16[32,128]{1,0:T(8,128)(2,1)} %copy-done.30) | copy-start | bytes 24580
  (20 other events, 15.8 us)

commit v4 on v3

--- a/solution.py
+++ b/solution.py
@@ -689,8 +689,13 @@
 
 def last_kernel(index_ref, totals_ref, inside_ref, weights_ref, base_ref, out_ref, base_vmem, out_vmem, sems):
     modes, nodes = base_ref.shape
-    load = pltpu.make_async_copy(base_ref, base_vmem, sems.at[0])
-    load.start()
+    rows_of = lambda n: pl.ds(n * LANES, LANES)
+    loads = [
+        pltpu.make_async_copy(base_ref.at[rows_of(n)], base_vmem.at[rows_of(n)], sems.at[n])
+        for n in range(modes // LANES)
+    ]
+    for load in loads:
+        load.start()
     planes, coarse, _ = totals_ref.shape
     totals = totals_ref[...].reshape(planes * coarse, modes)
     sums = jnp.dot(weights_ref[...], totals, preferred_element_type=F32)
@@ -706,12 +711,12 @@
         wanted = jnp.where(row == c, index_ref[c], wanted)
     onehot = (node == wanted).astype(F32)
     onehot = jnp.concatenate([onehot] * 3, axis=0).astype(BF16)
-    load.wait()
     made = []
     for n in range(modes // LANES):
         rows = slice(n * LANES, (n + 1) * LANES)
+        loads[n].wait()
         out_vmem[rows] = base_vmem[rows] + jnp.dot(terms[rows], onehot, preferred_element_type=F32)
-        made.append(pltpu.make_async_copy(out_vmem.at[rows], out_ref.at[rows], sems.at[1 + n]))
+        made.append(pltpu.make_async_copy(out_vmem.at[rows], out_ref.at[rows], sems.at[modes // LANES + n]))
         made[-1].start()
     finished(made)
 
@@ -726,8 +731,9 @@
         scratch_shapes=[
             pltpu.VMEM(base.shape, F32),
             pltpu.VMEM(base.shape, F32),
-            pltpu.SemaphoreType.DMA((1 + modes // LANES,)),
-        ],
+            pltpu.SemaphoreType.DMA((2 * modes // LANES,)),
+        ],
+        input_output_aliases={4: 0},
         compiler_params=params(52000),
         name="last",
     )(index, totals, inside, weights, base)

time: 137 us -> 137 us (level)
    unnamed x72 -> x70, local copies, waits for them, and re-layouts: 15.9 us -> 14.6 us
where the time goes in v4:
time: 137 us; the launch traced here: 136 us
  Pallas kernels  36.2 us (26%)
  blocking collectives  31.7 us (23%)
  starting transfers between devices  31.1 us (23%)
  waiting for transfers between devices  20.8 us (15%)
  local copies, waits for them, and re-layouts  14.6 us (11%)
    all_to_all x1, blocking collectives, shards(): feeds = lax.all_to_all(message, PLANE, 0, 0, tiled=True)  17.5 us
    unnamed x70, local copies, waits for them, and re-layouts  14.6 us
    all_to_all x1, blocking collectives, shards(): later = lax.all_to_all(message, PLANE, 0, 0, tiled=True)  14.1 us
    ppermute x2, waiting for transfers between devices, over_modes(): across = lax.ppermute(own, 'yl', swap)  11.6 us
    all_to_all x1, starting transfers between devices, shards(): totals = lax.all_to_all(totals, 'z', 0, 0, tiled=True)  8.57 us
    pallas_call x1, Pallas kernels, first_update(): pl.pallas_call(first_kernel, in_specs=[SMEM] * 3 + [ANY] * 9 + [VMEM] + [...  7.38 us
    pallas_call x1, Pallas kernels, bulk(): pl.pallas_call(bulk_kernel, in_specs=[SMEM, SMEM] + [ANY] * 5 + [VMEM], o...  6.14 us
    pallas_call x1, Pallas kernels, last_local(): pl.pallas_call(last_local_kernel, grid=(modes // LANES,), in_specs=[SMEM,...  5.63 us
  transfers between devices with their start and end apart: 16, of which 5 were waited for; matrix products, arithmetic and copies ran while one was open for 0% of the time, Pallas kernels for 17%

profile of v4, /device:TPU:32, one launch (start us, length us, event | category | flops | bytes accessed | tf_op | source)
XLA Modules:
  0.0 135.5 jit_solution(10525587336162490733)
XLA Ops:
  0.7 2.4 %start.1 = (bf16[480,512]{1,0:T(8,128)(2,1)}, f32[24,512]{1,0:T(8,128)}, f32[24,512]{1,0:T(8,128)}, f32[8,512]{1,0:T(8,128)}, f32[8,512]{1,0:T(8,128)}) custom-call(f32[512,512]{1,0:T(8,128)} %field_ref.3), custom_call_target="tpu_custom_call" | custom-call | tf_op jit(solution)/shard_map/start/pallas_call | solution.py:50
  3.1 1.7 %collective-permute-start.1 = (bf16[480,512]{1,0:T(8,128)(2,1)}, bf16[480,512]{1,0:T(8,128)(2,1)S(1)}, u32[]{:S(2)}, u32[]{:S(2)}) collective-permute-start(bf16[480,512]{1,0:T(8,128)(2,1)} %get-tuple-element.31.a_ref), channel_id=1, source_target_pairs={{0,2},{2,0},{1,3},{3,1},{4,6},{6,4},{5,7},{7,5},{8,10},{10,8},{9,1... | collective-permute-start | bytes 1474568 | tf_op jit(solution)/shard_map/ppermute | solution.py:752
  4.7 11.6 %collective-permute-done.1.c_ref = bf16[480,512]{1,0:T(8,128)(2,1)S(1)} collective-permute-done((bf16[480,512]{1,0:T(8,128)(2,1)}, bf16[480,512]{1,0:T(8,128)(2,1)S(1)}, u32[]{:S(2)}, u32[]{:S(2)}) %collective-permute-start.1) | collective-permute-done | bytes 491552 | tf_op jit(solution)/shard_map/ppermute | solution.py:752
  16.3 5.1 %collective-permute-start.3 = (f32[8,512]{1,0:T(8,128)}, f32[8,512]{1,0:T(8,128)S(1)}, u32[]{:S(2)}, u32[]{:S(2)}) collective-permute-start(f32[8,512]{1,0:T(8,128)} %get-tuple-element.34), channel_id=1, source_target_pairs={{0,4},{4,8},{8,12},{12,16},{16,20},{20,24},{24,28},{28,32},{32,36}... | collective-permute-start | bytes 49160 | tf_op jit(solution)/shard_map/ppermute | solution.py:745
  21.4 5.3 %collective-permute-start.4 = (f32[8,512]{1,0:T(8,128)}, f32[8,512]{1,0:T(8,128)S(1)}, u32[]{:S(2)}, u32[]{:S(2)}) collective-permute-start(f32[8,512]{1,0:T(8,128)} %get-tuple-element.35), channel_id=1, source_target_pairs={{4,0},{8,4},{12,8},{16,12},{20,16},{24,20},{28,24},{32,28},{36,32}... | collective-permute-start | bytes 49160 | tf_op jit(solution)/shard_map/ppermute | solution.py:746
  26.7 2.1 %collective-permute-done.4.right_ref = f32[8,512]{1,0:T(8,128)S(1)} collective-permute-done((f32[8,512]{1,0:T(8,128)}, f32[8,512]{1,0:T(8,128)S(1)}, u32[]{:S(2)}, u32[]{:S(2)}) %collective-permute-start.4) | collective-permute-done | bytes 16416 | tf_op jit(solution)/shard_map/ppermute | solution.py:746
  28.8 0.8 copy-done.17
  30.5 1.2 collective-permute-start.6
  32.3 4.6 %prepare.1 = (f32[512,512]{1,0:T(8,128)}, bf16[512,512]{1,0:T(8,128)(2,1)}, f32[512,512]{1,0:T(8,128)}, f32[512,128]{1,0:T(8,128)}, f32[64,512]{1,0:T(8,128)}, /*index=5*/f32[64,128]{1,0:T(8,128)}) custom-call(s32[16]{0:T(128)} %index_ref.9, f32[512,512]{1,0:T(8,128)} %right_ref.1, bf16[512,512]{1,0:T(8,128)(2,1)} %inverse_ref.3, f32[512,512]{1,0:T(8,128)} %field_ref.3, ...), custom_call_target="tpu_custom_call" | custom-call | tf_op jit(solution)/shard_map/prepare/pallas_call | solution.py:119
  38.6 0.9 copy-done.1
  39.5 1.0 copy-done.5
  40.6 1.0 copy-done.7
  41.6 1.0 copy-done.9
  42.6 7.4 %first_update.1 = (bf16[8,16,768]{2,1,0:T(8,128)(2,1)S(1)}, f32[512,512]{1,0:T(8,128)}, bf16[512,512]{1,0:T(8,128)(2,1)S(1)}, f32[96,512]{1,0:T(8,128)S(1)}) custom-call(s32[1]{0:T(128)} %bitcast.me_ref, s32[4,4,16]{2,1,0:T(4,128)S(1)} %bitcast.4, s32[16]{0:T(128)S(1)} %copy-done.25, bf16[480,512]{1,0:T(8,128)(2,1)S(1)} %copy-done.3, ...), custom_call_target="tpu_custom_call" | custom-call | tf_op jit(solution)/shard_map/first_update/pallas_call | solution.py:379
  50.0 1.2 collective-permute-start.12
  51.2 17.5 %all_to_all.20.feeds_ref = bf16[8,16,768]{2,1,0:T(8,128)(2,1)S(1)} all-to-all(bf16[8,16,768]{2,1,0:T(8,128)(2,1)S(1)} %get-tuple-element.40), channel_id=1, replica_groups=mesh['z'=8,'x'=4,'yh'=2,'yl'=2,'core'=2] {'x','yh'}, dimensions={0} | all-to-all | bytes 393216 | tf_op jit(solution)/shard_map/all_to_all | solution.py:783
  68.7 1.0 plane_totals.1
  71.0 8.6 %all-to-all-start.1 = ((bf16[8,16,768]{2,1,0:T(8,128)(2,1)}), bf16[8,16,768]{2,1,0:T(8,128)(2,1)S(1)}, u32[]{:S(2)}, u32[]{:S(2)}) async-start(bf16[8,16,768]{2,1,0:T(8,128)(2,1)} %copy-done.10), calls=%async_computation.1 | async-start | bytes 393216 | tf_op jit(solution)/shard_map/all_to_all | solution.py:786
  80.8 1.0 inside_plane.1
  83.7 4.4 %all-to-all-done.1.totals_ref = bf16[8,16,768]{2,1,0:T(8,128)(2,1)S(1)} async-done(((bf16[8,16,768]{2,1,0:T(8,128)(2,1)}), bf16[8,16,768]{2,1,0:T(8,128)(2,1)S(1)}, u32[]{:S(2)}, u32[]{:S(2)}) %all-to-all-start.1) | async-done | bytes 196640 | tf_op jit(solution)/shard_map/all_to_all | solution.py:786
  88.0 0.9 copy-done.12
  91.1 2.1 %correct.1 = (bf16[64,512]{1,0:T(8,128)(2,1)S(1)}, f32[16,512]{1,0:T(8,128)S(1)}, bf16[32,128]{1,0:T(8,128)(2,1)S(1)}) custom-call(s32[1]{0:T(128)} %bitcast.2.z_ref, s32[1]{0:T(128)} %bitcast.3.p_ref, s32[16]{0:T(128)S(1)} %copy-done.26, bf16[8,16,768]{2,1,0:T(8,128)(2,1)S(1)} %all_to_all.20.feeds_ref, bf16[8,16,768]{2,1,0:T(8,128)(2,1)S(1)} %all-to-all-done.1.totals_ref, ...), custom_call_target="tpu_custom_call" | custom-call | tf_op jit(solution)/shard_map/correct/pallas_call | solution.py:604
  93.8 2.1 %collective-permute-start.9 = (bf16[64,512]{1,0:T(8,128)(2,1)S(1)}, bf16[64,512]{1,0:T(8,128)(2,1)S(1)}, u32[]{:S(2)}, u32[]{:S(2)}) collective-permute-start(bf16[64,512]{1,0:T(8,128)(2,1)S(1)} %get-tuple-element.46.a_ref), channel_id=1, source_target_pairs={{0,2},{2,0},{1,3},{3,1},{4,6},{6,4},{5,7},{7,5},{8,10},{10,8},{9,1... | collective-permute-start | bytes 196616 | tf_op jit(solution)/shard_map/ppermute | solution.py:759
  96.2 1.3 collective-permute-done.10.d_ref
  97.5 1.4 %collective-permute-done.9.c_ref = bf16[64,512]{1,0:T(8,128)(2,1)S(1)} collective-permute-done((bf16[64,512]{1,0:T(8,128)(2,1)S(1)}, bf16[64,512]{1,0:T(8,128)(2,1)S(1)}, u32[]{:S(2)}, u32[]{:S(2)}) %collective-permute-start.9) | collective-permute-done | bytes 65568 | tf_op jit(solution)/shard_map/ppermute | solution.py:759
  98.9 2.0 %redo.1 = (bf16[8,16,512]{2,1,0:T(8,128)(2,1)S(1)}, f32[64,512]{1,0:T(8,128)S(1)}) custom-call(s32[1]{0:T(128)} %bitcast.me_ref, s32[4,4,16]{2,1,0:T(4,128)S(1)} %bitcast.5, bf16[64,512]{1,0:T(8,128)(2,1)S(1)} %get-tuple-element.46.a_ref, bf16[64,512]{1,0:T(8,128)(2,1)S(1)} %collective-permute-done.8.b_ref, ...), custom_call_target="tpu_custom_call" | custom-call | tf_op jit(solution)/shard_map/redo/pallas_call | solution.py:639
  100.9 14.1 %all_to_all.21.feeds_ref = bf16[8,16,512]{2,1,0:T(8,128)(2,1)S(1)} all-to-all(bf16[8,16,512]{2,1,0:T(8,128)(2,1)S(1)} %get-tuple-element.50), channel_id=1, replica_groups=mesh['z'=8,'x'=4,'yh'=2,'yl'=2,'core'=2] {'x','yh'}, dimensions={0} | all-to-all | bytes 262144 | tf_op jit(solution)/shard_map/all_to_all | solution.py:792
  115.1 0.8 second_plane_totals.1
  115.9 4.7 %all-to-all-start.3 = ((bf16[8,16,512]{2,1,0:T(8,128)(2,1)}), bf16[8,16,512]{2,1,0:T(8,128)(2,1)S(1)}, u32[]{:S(2)}, u32[]{:S(2)}) async-start(bf16[8,16,512]{2,1,0:T(8,128)(2,1)} %get-tuple-element.52), calls=%async_computation.3 | async-start | bytes 262144 | tf_op jit(solution)/shard_map/all_to_all | solution.py:795
  120.6 6.1 %whole.1.op_ref = f32[512,512]{1,0:T(8,128)} custom-call(s32[1]{0:T(128)} %bitcast.me_ref, s32[4,4,16]{2,1,0:T(4,128)S(1)} %bitcast.6, bf16[512,512]{1,0:T(8,128)(2,1)S(1)} %get-tuple-element.55.a_ref, bf16[512,512]{1,0:T(8,128)(2,1)} %collective-permute-done.11.b_ref, bf16[512,512]{1,0:T(8,128)(2,1)S(1)} %collective-permute-done.12.c_ref, ...), custom_call_target="tpu_custom_call" | custom-call | tf_op jit(solution)/shard_map/whole/pallas_call | solution.py:240
  126.8 5.6 %last_local.1 = (f32[512,512]{1,0:T(8,128)}, f32[512,512]{1,0:T(8,128)}) custom-call(s32[16]{0:T(128)} %index_ref.9, f32[512,512]{1,0:T(8,128)} %whole.1.op_ref, f32[512,512]{1,0:T(8,128)} %get-tuple-element.37.right_ref, f32[64,512]{1,0:T(8,128)} %copy-done.15, bf16[512,512]{1,0:T(8,128)(2,1)} %get-tuple-element.38.sub_ref, ...), custom_call_target="tpu_custom_call" | custom-call | tf_op jit(solution)/shard_map/last_local/pallas_call | solution.py:671
  132.5 2.9 %last.1 = f32[512,512]{1,0:T(8,128)} custom-call(s32[16]{0:T(128)S(1)} %copy-done.27, bf16[8,16,512]{2,1,0:T(8,128)(2,1)S(1)} %all-to-all-done.3.totals_ref, f32[16,512]{1,0:T(8,128)S(1)} %get-tuple-element.53.inside_ref, bf16[32,128]{1,0:T(8,128)(2,1)S(1)} %copy-done.30, f32[512,512]{1,0:T(8,128)} %get-tuple-element.58.base_ref), custom_call_target="tpu_custom_call", output_to_operand_aliasing={{}: (4, {})} | custom-call | tf_op jit(solution)/shard_map/last/pallas_call | solution.py:726
  (85 shorter events, 10.4 us)
Async XLA Ops:
  0.6 37.9 %copy-start.25 = (s32[16]{0:T(128)S(1)}, s32[16]{0:T(128)}, u32[]{:S(2)}) copy-start(s32[16]{0:T(128)} %index_ref.9) | copy-start | bytes 196
  0.6 37.9 %copy-start.16 = (s32[4,16,4]{1,2,0:T(4,128)S(1)}, s32[4,16,4]{1,2,0:T(4,128)}, u32[]{:S(2)}) copy-start(s32[4,16,4]{1,2,0:T(4,128)} %param.13) | copy-start | bytes 3076
  0.7 37.9 %copy-start.20 = (f32[16,16]{1,0:T(8,128)S(1)}, f32[16,16]{1,0:T(8,128)}, u32[]{:S(2)}) copy-start(f32[16,16]{1,0:T(8,128)} %inverse_ref.5) | copy-start | bytes 3076
  0.7 37.9 %copy-start.28 = (f32[16,16]{1,0:T(8,128)S(1)}, f32[16,16]{1,0:T(8,128)}, u32[]{:S(2)}) copy-start(f32[16,16]{1,0:T(8,128)} %coupling_ref.1) | copy-start | bytes 3076
  3.0 35.5 %copy-start.3 = (bf16[480,512]{1,0:T(8,128)(2,1)S(1)}, bf16[480,512]{1,0:T(8,128)(2,1)}, u32[]{:S(2)}) copy-start(bf16[480,512]{1,0:T(8,128)(2,1)} %get-tuple-element.31.a_ref) | copy-start | bytes 1474564
  3.1 13.3 %collective-permute-start.1 = (bf16[480,512]{1,0:T(8,128)(2,1)}, bf16[480,512]{1,0:T(8,128)(2,1)S(1)}, u32[]{:S(2)}, u32[]{:S(2)}) collective-permute-start(bf16[480,512]{1,0:T(8,128)(2,1)} %get-tuple-element.31.a_ref), channel_id=1, source_target_pairs={{0,2},{2,0},{1,3},{3,1},{4,6},{6,4},{5,7},{7,5},{8,10},{10,8},{9,1... | collective-permute-start | bytes 1474568 | tf_op jit(solution)/shard_map/ppermute | solution.py:752
  4.7 32.2 %collective-permute-start = (bf16[480,512]{1,0:T(8,128)(2,1)}, bf16[480,512]{1,0:T(8,128)(2,1)S(1)}, u32[]{:S(2)}, u32[]{:S(2)}) collective-permute-start(bf16[480,512]{1,0:T(8,128)(2,1)} %get-tuple-element.31.a_ref), channel_id=1, source_target_pairs={{0,1},{1,0},{2,3},{3,2},{4,5},{5,4},{6,7},{7,6},{8,9},{9,8},{10,11... | collective-permute-start | bytes 1474568 | tf_op jit(solution)/shard_map/ppermute | solution.py:753
  16.3 22.2 %copy-start.4 = (bf16[480,512]{1,0:T(8,128)(2,1)}, bf16[480,512]{1,0:T(8,128)(2,1)S(1)}, u32[]{:S(2)}) copy-start(bf16[480,512]{1,0:T(8,128)(2,1)S(1)} %collective-permute-done.1.c_ref) | copy-start | bytes 1474564
  16.3 21.4 %collective-permute-start.2 = (bf16[480,512]{1,0:T(8,128)(2,1)S(1)}, bf16[480,512]{1,0:T(8,128)(2,1)S(1)}, u32[]{:S(2)}, u32[]{:S(2)}) collective-permute-start(bf16[480,512]{1,0:T(8,128)(2,1)S(1)} %collective-permute-done.1.c_ref), channel_id=1, source_target_pairs={{0,1},{1,0},{2,3},{3,2},{4,5},{5,4},{6,7},{7,6},{8,9},{9,8},{10,11... | collective-permute-start | bytes 1474568 | tf_op jit(solution)/shard_map/ppermute | solution.py:754
  16.3 10.4 %collective-permute-start.3 = (f32[8,512]{1,0:T(8,128)}, f32[8,512]{1,0:T(8,128)S(1)}, u32[]{:S(2)}, u32[]{:S(2)}) collective-permute-start(f32[8,512]{1,0:T(8,128)} %get-tuple-element.34), channel_id=1, source_target_pairs={{0,4},{4,8},{8,12},{12,16},{16,20},{20,24},{24,28},{28,32},{32,36}... | collective-permute-start | bytes 49160 | tf_op jit(solution)/shard_map/ppermute | solution.py:745
  21.4 7.3 %collective-permute-start.4 = (f32[8,512]{1,0:T(8,128)}, f32[8,512]{1,0:T(8,128)S(1)}, u32[]{:S(2)}, u32[]{:S(2)}) collective-permute-start(f32[8,512]{1,0:T(8,128)} %get-tuple-element.35), channel_id=1, source_target_pairs={{4,0},{8,4},{12,8},{16,12},{20,16},{24,20},{28,24},{32,28},{36,32}... | collective-permute-start | bytes 49160 | tf_op jit(solution)/shard_map/ppermute | solution.py:746
  30.4 6.5 %collective-permute-start.5 = (bf16[32,512]{1,0:T(8,128)(2,1)S(1)}, bf16[32,512]{1,0:T(8,128)(2,1)S(1)}, u32[]{:S(2)}, u32[]{:S(2)}) collective-permute-start(bf16[32,512]{1,0:T(8,128)(2,1)S(1)} %edges.1.ea_ref), channel_id=1, source_target_pairs={{0,1},{1,0},{2,3},{3,2},{4,5},{5,4},{6,7},{7,6},{8,9},{9,8},{10,11... | collective-permute-start | bytes 98312 | tf_op jit(solution)/shard_map/ppermute | solution.py:761
  30.5 6.5 %collective-permute-start.6 = (bf16[32,512]{1,0:T(8,128)(2,1)S(1)}, bf16[32,512]{1,0:T(8,128)(2,1)S(1)}, u32[]{:S(2)}, u32[]{:S(2)}) collective-permute-start(bf16[32,512]{1,0:T(8,128)(2,1)S(1)} %edges.1.ea_ref), channel_id=1, source_target_pairs={{0,2},{2,0},{1,3},{3,1},{4,6},{6,4},{5,7},{7,5},{8,10},{10,8},{9,1... | collective-permute-start | bytes 98312 | tf_op jit(solution)/shard_map/ppermute | solution.py:759
  31.7 5.3 %collective-permute-start.7 = (bf16[32,512]{1,0:T(8,128)(2,1)S(1)}, bf16[32,512]{1,0:T(8,128)(2,1)S(1)}, u32[]{:S(2)}, u32[]{:S(2)}) collective-permute-start(bf16[32,512]{1,0:T(8,128)(2,1)S(1)} %edges.1.ea_ref), channel_id=1, source_target_pairs={{0,3},{1,2},{2,1},{3,0},{4,7},{5,6},{6,5},{7,4},{8,11},{9,10},{10,... | collective-permute-start | bytes 98312 | tf_op jit(solution)/shard_map/ppermute | solution.py:760
  42.6 53.3 %copy-start = (bf16[4,4,4,128,128]{4,3,2,1,0:T(8,128)(2,1)S(1)}, bf16[4,4,4,128,128]{4,3,2,1,0:T(8,128)(2,1)}, u32[]{:S(2)}) copy-start(bf16[4,4,4,128,128]{4,3,2,1,0:T(8,128)(2,1)} %g_hbm.3) | copy-start | bytes 6291460
  50.0 19.8 %copy-start.11 = (f32[96,512]{1,0:T(8,128)}, f32[96,512]{1,0:T(8,128)S(1)}, u32[]{:S(2)}) copy-start(f32[96,512]{1,0:T(8,128)S(1)} %get-tuple-element.45.around_ref) | copy-start | bytes 589828
  50.0 29.6 %collective-permute-start.12 = (bf16[512,512]{1,0:T(8,128)(2,1)S(1)}, bf16[512,512]{1,0:T(8,128)(2,1)S(1)}, u32[]{:S(2)}, u32[]{:S(2)}) collective-permute-start(bf16[512,512]{1,0:T(8,128)(2,1)S(1)} %get-tuple-element.55.a_ref), channel_id=1, source_target_pairs={{0,2},{2,0},{1,3},{3,1},{4,6},{6,4},{5,7},{7,5},{8,10},{10,8},{9,1... | collective-permute-start | bytes 1572872 | tf_op jit(solution)/shard_map/ppermute | solution.py:752
  71.0 17.0 %all-to-all-start.1 = ((bf16[8,16,768]{2,1,0:T(8,128)(2,1)}), bf16[8,16,768]{2,1,0:T(8,128)(2,1)S(1)}, u32[]{:S(2)}, u32[]{:S(2)}) async-start(bf16[8,16,768]{2,1,0:T(8,128)(2,1)} %copy-done.10), calls=%async_computation.1 | async-start | bytes 393216 | tf_op jit(solution)/shard_map/all_to_all | solution.py:786
  79.6 41.0 %collective-permute-start.11 = (bf16[512,512]{1,0:T(8,128)(2,1)S(1)}, bf16[512,512]{1,0:T(8,128)(2,1)}, u32[]{:S(2)}, u32[]{:S(2)}) collective-permute-start(bf16[512,512]{1,0:T(8,128)(2,1)S(1)} %get-tuple-element.55.a_ref), channel_id=1, source_target_pairs={{0,1},{1,0},{2,3},{3,2},{4,5},{5,4},{6,7},{7,6},{8,9},{9,8},{10,11... | collective-permute-start | bytes 1572872 | tf_op jit(solution)/shard_map/ppermute | solution.py:753
  79.6 41.0 %collective-permute-start.13 = (bf16[512,512]{1,0:T(8,128)(2,1)S(1)}, bf16[512,512]{1,0:T(8,128)(2,1)}, u32[]{:S(2)}, u32[]{:S(2)}) collective-permute-start(bf16[512,512]{1,0:T(8,128)(2,1)S(1)} %collective-permute-done.12.c_ref), channel_id=1, source_target_pairs={{0,1},{1,0},{2,3},{3,2},{4,5},{5,4},{6,7},{7,6},{8,9},{9,8},{10,11... | collective-permute-start | bytes 1572872 | tf_op jit(solution)/shard_map/ppermute | solution.py:754
  93.8 2.3 %copy-start.13 = (f32[16,512]{1,0:T(8,128)}, f32[16,512]{1,0:T(8,128)S(1)}, u32[]{:S(2)}) copy-start(f32[16,512]{1,0:T(8,128)S(1)} %get-tuple-element.47.after_ref.error_ref) | copy-start | bytes 98308
  93.8 3.7 %collective-permute-start.10 = (bf16[64,512]{1,0:T(8,128)(2,1)S(1)}, bf16[64,512]{1,0:T(8,128)(2,1)S(1)}, u32[]{:S(2)}, u32[]{:S(2)}) collective-permute-start(bf16[64,512]{1,0:T(8,128)(2,1)S(1)} %get-tuple-element.46.a_ref), channel_id=1, source_target_pairs={{0,3},{1,2},{2,1},{3,0},{4,7},{5,6},{6,5},{7,4},{8,11},{9,10},{10,... | collective-permute-start | bytes 196616 | tf_op jit(solution)/shard_map/ppermute | solution.py:760
  93.8 3.7 %collective-permute-start.8 = (bf16[64,512]{1,0:T(8,128)(2,1)S(1)}, bf16[64,512]{1,0:T(8,128)(2,1)S(1)}, u32[]{:S(2)}, u32[]{:S(2)}) collective-permute-start(bf16[64,512]{1,0:T(8,128)(2,1)S(1)} %get-tuple-element.46.a_ref), channel_id=1, source_target_pairs={{0,1},{1,0},{2,3},{3,2},{4,5},{5,4},{6,7},{7,6},{8,9},{9,8},{10,11... | collective-permute-start | bytes 196616 | tf_op jit(solution)/shard_map/ppermute | solution.py:761
  93.8 5.1 %collective-permute-start.9 = (bf16[64,512]{1,0:T(8,128)(2,1)S(1)}, bf16[64,512]{1,0:T(8,128)(2,1)S(1)}, u32[]{:S(2)}, u32[]{:S(2)}) collective-permute-start(bf16[64,512]{1,0:T(8,128)(2,1)S(1)} %get-tuple-element.46.a_ref), channel_id=1, source_target_pairs={{0,2},{2,0},{1,3},{3,1},{4,6},{6,4},{5,7},{7,5},{8,10},{10,8},{9,1... | collective-permute-start | bytes 196616 | tf_op jit(solution)/shard_map/ppermute | solution.py:759
  95.9 2.9 %copy-start.14 = (f32[64,512]{1,0:T(8,128)S(1)}, f32[64,512]{1,0:T(8,128)}, u32[]{:S(2)}) copy-start(f32[64,512]{1,0:T(8,128)} %get-tuple-element.49.right_ref) | copy-start | bytes 393220
  95.9 2.9 %copy-start.19 = (f32[64,128]{1,0:T(8,128)S(1)}, f32[64,128]{1,0:T(8,128)}, u32[]{:S(2)}) copy-start(f32[64,128]{1,0:T(8,128)} %get-tuple-element.48.coef_ref) | copy-start | bytes 98308
  96.1 18.9 %copy-start.24 = (bf16[64,128]{1,0:T(8,128)(2,1)S(1)}, bf16[64,128]{1,0:T(8,128)(2,1)}, u32[]{:S(2)}) copy-start(bf16[64,128]{1,0:T(8,128)(2,1)} %copy-done.23) | copy-start | bytes 49156
  96.1 24.5 %copy-start.2 = (f32[512,128]{1,0:T(8,128)S(1)}, f32[512,128]{1,0:T(8,128)}, u32[]{:S(2)}) copy-start(f32[512,128]{1,0:T(8,128)} %get-tuple-element.36.coef_ref) | copy-start | bytes 786436
  100.9 15.0 %copy-start.15 = (f32[64,512]{1,0:T(8,128)}, f32[64,512]{1,0:T(8,128)S(1)}, u32[]{:S(2)}) copy-start(f32[64,512]{1,0:T(8,128)S(1)} %get-tuple-element.56.rows_ref) | copy-start | bytes 393220
  115.9 16.6 %all-to-all-start.3 = ((bf16[8,16,512]{2,1,0:T(8,128)(2,1)}), bf16[8,16,512]{2,1,0:T(8,128)(2,1)S(1)}, u32[]{:S(2)}, u32[]{:S(2)}) async-start(bf16[8,16,512]{2,1,0:T(8,128)(2,1)} %get-tuple-element.52), calls=%async_computation.3 | async-start | bytes 262144 | tf_op jit(solution)/shard_map/all_to_all | solution.py:795
  126.8 5.7 %copy-start.27 = (s32[16]{0:T(128)S(1)}, s32[16]{0:T(128)}, u32[]{:S(2)}) copy-start(s32[16]{0:T(128)} %index_ref.9) | copy-start | bytes 196
  126.8 5.7 %copy-start.30 = (bf16[32,128]{1,0:T(8,128)(2,1)S(1)}, bf16[32,128]{1,0:T(8,128)(2,1)}, u32[]{:S(2)}) copy-start(bf16[32,128]{1,0:T(8,128)(2,1)} %copy-done.29) | copy-start | bytes 24580
  (19 other events, 14.6 us)
